TPU v7x, 32 devices: a whole 2x2x4 slice. The times are simulated.
32 devices in a mesh: modes: 4 (over y, core), gz: 8 (over z, x).
Axes of the slice: x: 2, y: 2, z: 4, core: 2. Of those that a mesh axis runs over, the one named last changes fastest.
Arguments:
- source_field: float32 [128, 2, 8, 2048], P('gz', None, None, 'modes'), may hold values from -0.075 to 0.075
- coupling_below: float32 [128], P('gz'), may hold values from 0.5 to 2
- coupling_above: float32 [128], P('gz'), may hold values from 0.5 to 2
- eigen_stream: float32 [8], replicated, may hold values from 0.000390625 to 0.015625
- eigen_span: float32 [2048], replicated, may hold values from 0.000390625 to 0.015625
Outputs:
- pressure: float32 [128, 2, 8, 2048], P('gz', None, 'modes')
All inputs are finite; a program needn't handle non-finite values.
Results may differ from a plain program's by a relative error of at most 0.0003.
Values sent between devices are 32-bit elements; how exact they have to be, the bound alone decides.
No kernel may reach another device: no remote copies, remote signals or barrier semaphores. Data moves between devices by JAX's collectives and lax.ppermute only.
A program may use at most 64 MiB of HBM per device.

v0:
```python
import functools

import jax
import jax.numpy as jnp
from jax import lax
from jax.experimental import pallas as pl
from jax.experimental.pallas import tpu as pltpu
from jax.sharding import PartitionSpec as P


LANES = 128
SUBLANES = 8


def sizes_of(source_field):
    rows, _, kx_total, ky_local = source_field.shape
    mode_count = lax.axis_size("modes")
    kx_count, tiles = kx_total // mode_count, ky_local // LANES
    return rows, kx_total, kx_count, tiles, mode_count, kx_count * tiles


def chunks_of(rows):
    size = rows // 4 if rows % 4 == 0 else rows
    return [(first, size) for first in range(0, rows, size)]


def reduce_kernel(sizes, below_ref, above_ref, stream_ref, span_ref, source_hbm, ports_ref, table_ref, spectral_ref, source_ref, sems):
    rows, kx_total, kx_count, tiles, mode_count, height = sizes
    me, partition = lax.axis_index("modes"), lax.axis_index("gz")
    copies = []
    for i, (first, size) in enumerate(chunks_of(rows)):
        copies.append(
            pltpu.make_async_copy(source_hbm.at[pl.ds(first, size)], source_ref.at[pl.ds(first, size)], sems.at[i])
        )
        copies[-1].start()
    lower = [below_ref[k] for k in range(rows)]
    upper = [above_ref[k] for k in range(rows)]
    lower[0] = jnp.where(partition == 0, 0.0, lower[0])
    upper[-1] = jnp.where(partition == lax.axis_size("gz") - 1, 0.0, upper[-1])
    lane = lax.broadcasted_iota(jnp.int32, (SUBLANES, LANES), 1)
    sub = lax.broadcasted_iota(jnp.int32, (SUBLANES, LANES), 0)
    table = jnp.zeros((SUBLANES, LANES), jnp.float32)
    for k in range(rows):
        table = jnp.where(lane == k, jnp.where(sub == 0, lower[k], upper[k]), table)
    table_ref[...] = table
    for d in range(mode_count):
        for t in range(tiles):
            spanwise = span_ref[pl.ds((me ^ d) * tiles + t, 1), :]
            for j in range(kx_count):
                at = d * height + t * kx_count + j
                spectral_ref[at : at + 1, :] = spanwise + stream_ref[me * kx_count + j]
    shape = (kx_total, LANES)
    kx_at = lax.broadcasted_iota(jnp.int32, shape, 0)
    streamwise = jnp.zeros(shape, jnp.float32)
    for i in range(kx_total):
        streamwise = jnp.where(kx_at == i, stream_ref[i], streamwise)
    each = range(tiles)
    spectral = [streamwise + span_ref[pl.ds(me * tiles + t, 1), :] for t in each]
    one, zero = jnp.ones(shape, jnp.float32), jnp.zeros(shape, jnp.float32)
    grown, passed = [one] * tiles, [one] * tiles
    partial = [[zero] * tiles, [zero] * tiles]
    first_value = [[zero] * tiles, [zero] * tiles]
    starts = {first: i for i, (first, _) in enumerate(chunks_of(rows))}
    for k in range(rows):
        if k in starts:
            copies[starts[k]].wait()
        for t in each:
            held = spectral[t] + lower[k] * grown[t]
            inverse = 1.0 / (upper[k] + held)
            grown[t] = held * inverse
            for c in range(2):
                source = source_ref[k, c, :, t * LANES : (t + 1) * LANES]
                partial[c][t] = (source + lower[k] * partial[c][t]) * inverse
                first_value[c][t] = first_value[c][t] + passed[t] * partial[c][t]
            passed[t] = passed[t] * (upper[k] * inverse)
    values = first_value + partial
    for dest in range(mode_count):
        to = dest ^ me
        for i in range(4):
            for t in each:
                at = i * height + t * kx_count
                ports_ref[to % 2, to // 2, at : at + kx_count, :] = values[i][t][dest * kx_count : (dest + 1) * kx_count]


def regroup_kernel(sizes, source_hbm, blocks_ref, source_ref, sems):
    rows, _, kx_count, tiles, mode_count, _ = sizes
    me = lax.axis_index("modes")
    copies = []
    for i, (first, size) in enumerate(chunks_of(rows)):
        copies.append(
            pltpu.make_async_copy(source_hbm.at[pl.ds(first, size)], source_ref.at[pl.ds(first, size)], sems.at[i])
        )
        copies[-1].start()
    for i, (first, size) in enumerate(chunks_of(rows)):
        copies[i].wait()
        for k in range(first, first + size):
            for c in range(2):
                for t in range(tiles):
                    at = t * kx_count
                    for dest in range(mode_count):
                        blocks_ref[dest ^ me, k, c, at : at + kx_count, :] = source_ref[
                            k, c, dest * kx_count : (dest + 1) * kx_count, t * LANES : (t + 1) * LANES
                        ]


def climb(spectral, num, den, near, far):
    product = near[0]
    for k in range(len(near)):
        num = spectral * den + near[k] * num
        before = den
        den = num + far[k] * den
        if k:
            product = product * near[k]
    return num, den, far[-1] * before, product


def couplings(table, line, rows):
    return [table[line : line + 1, k : k + 1] for k in range(rows)]


def merge_kernel(sizes, spectral_ref, table_ref, ports_ref, taken_ref, side_ref, *rest):
    rows, _, _, _, mode_count, height = sizes
    chips = mode_count // 2
    own_refs, pair_refs, message_ref = rest[: chips - 1], rest[chips - 1 : 2 * (chips - 1)], rest[-1]
    total = mode_count * height
    port = 4 * height
    upside = lax.axis_index("gz") % 2 == 1

    def gather(i, chunk):
        return jnp.concatenate([chunk(d, i * height) for d in range(mode_count)], axis=0)

    def own_chunk(d, at):
        if d >= 2:
            start = (d % 2) * port + at
            return own_refs[d // 2 - 1][start : start + height, :]
        return ports_ref[0, 0, at : at + height, :] if d == 0 else taken_ref[0, at : at + height, :]

    def pair_chunk(d, at):
        start = (d % 2) * port + at
        ref = side_ref if d < 2 else pair_refs[d // 2 - 1]
        return ref[start : start + height, :]

    own_table, pair_table = table_ref[...], side_ref[2 * port :, :]
    low_table = jnp.where(upside, pair_table, own_table)
    high_table = jnp.where(upside, own_table, pair_table)
    sub = lax.broadcasted_iota(jnp.int32, (SUBLANES, LANES), 0)
    message_ref[4 * total :, :] = jnp.where(sub < 2, low_table, pltpu.roll(high_table, 2, 0))
    spectral = spectral_ref[...]
    one = jnp.ones((total, LANES), jnp.float32)
    own = [gather(i, own_chunk) for i in range(4)]
    pair = [gather(i, pair_chunk) for i in range(4)]
    low = [jnp.where(upside, b, a) for a, b in zip(own, pair)]
    high = [jnp.where(upside, a, b) for a, b in zip(own, pair)]
    low_l, low_u = couplings(low_table, 0, rows), couplings(low_table, 1, rows)
    high_l, high_u = couplings(high_table, 0, rows), couplings(high_table, 1, rows)

    def store(i, value):
        message_ref[i * total : (i + 1) * total, :] = value

    num, den, tail, _ = climb(spectral, one, one, low_l, low_u)
    passed = tail / den
    _, den_all, _, product = climb(spectral, num, den, high_l, high_u)
    ratio = product * den / den_all
    for c in range(2):
        store(2 + c, high[2 + c] + ratio * (low[2 + c] + passed * high[c]))
    num, den, tail, _ = climb(spectral, one, one, high_u[::-1], high_l[::-1])
    passed = tail / den
    _, den_all, _, product = climb(spectral, num, den, low_u[::-1], low_l[::-1])
    ratio = product * den / den_all
    for c in range(2):
        store(c, low[c] + ratio * (high[c] + passed * low[2 + c]))


def final_kernel(sizes, pairs, spectral_ref, table_ref, side_ref, *rest):
    rows, _, _, _, mode_count, height = sizes
    chips = mode_count // 2
    total = mode_count * height
    port = 4 * height
    pair_refs, rest = rest[: chips - 1], rest[chips - 1 :]
    messages, rest = rest[: pairs - 1], rest[pairs - 1 :]
    sources, rest = rest[:mode_count], rest[mode_count:]
    out_hbm, out_ref, factor_ref, partial_ref, sems = rest
    me, partition = lax.axis_index("modes"), lax.axis_index("gz")
    upside, level = partition % 2 == 1, partition // 2
    spectral = spectral_ref[...]
    one = jnp.ones((total, LANES), jnp.float32)
    zero = jnp.zeros((total, LANES), jnp.float32)
    start = (one, zero, zero, zero)

    def enter(state, ports, entry, leave, near, far):
        grown, passed, *partial = state
        num, den, tail, product = climb(spectral, grown, one, near, far)
        inverse = 1.0 / den
        ratio = product * inverse
        new = [ports(leave + c) + ratio * (partial[c] + passed * ports(entry + c)) for c in range(2)]
        return (num * inverse, tail * inverse, *new)

    def up(state, ports, table, blocks):
        near = [v for b in blocks for v in couplings(table, 2 * b, rows)]
        far = [v for b in blocks for v in couplings(table, 2 * b + 1, rows)]
        return enter(state, ports, 0, 2, near, far)

    def down(state, ports, table, blocks):
        near = [v for b in blocks for v in couplings(table, 2 * b + 1, rows)]
        far = [v for b in blocks for v in couplings(table, 2 * b, rows)]
        return enter(state, ports, 2, 0, near[::-1], far[::-1])

    def of_message(d):
        ref = messages[d - 1]
        return (lambda i: ref[i * total : (i + 1) * total, :]), ref[4 * total :, :], (0, 1)

    def pair_chunk(d, at):
        at += (d % 2) * port
        ref = side_ref if d < 2 else pair_refs[d // 2 - 1]
        return ref[at : at + height, :]

    def of_pair():
        def ports(i):
            return jnp.concatenate([pair_chunk(d, i * height) for d in range(mode_count)], axis=0)

        return ports, side_ref[2 * port :, :], (0,)

    below, above = start, start
    for d in range(pairs - 1, 0, -1):
        below = lax.cond(level >= d, lambda s, d=d: up(s, *of_message(d)), lambda s: s, below)
    for d in range(1, pairs):
        above = lax.cond(level < d, lambda s, d=d: down(s, *of_message(d)), lambda s: s, above)
    below = lax.cond(upside, lambda s: up(s, *of_pair()), lambda s: s, below)
    above = lax.cond(upside, lambda s: s, lambda s: down(s, *of_pair()), above)

    table = table_ref[...]
    lower, upper = couplings(table, 0, rows), couplings(table, 1, rows)
    grown, _, *partial = below
    for k in range(rows):
        held = spectral + lower[k] * grown
        inverse = 1.0 / (upper[k] + held)
        factor = upper[k] * inverse
        grown = held * inverse
        factor_ref[k] = factor
        for c in range(2):
            source = jnp.concatenate([sources[d][k, c] for d in range(mode_count)], axis=0)
            partial[c] = (source + lower[k] * partial[c]) * inverse
            partial_ref[k, c] = partial[c]
    inverse = 1.0 / (grown + factor * above[0])
    value = [(partial[c] + factor * above[2 + c]) * inverse for c in range(2)]
    chunks = {first: (i, size) for i, (first, size) in enumerate(chunks_of(rows))}
    copies = []
    for k in range(rows - 1, -1, -1):
        for c in range(2):
            if k < rows - 1:
                value[c] = partial_ref[k, c] + factor_ref[k] * value[c]
            for d in range(mode_count):
                out_ref[k, c, me ^ d] = value[c][d * height : (d + 1) * height]
        if k in chunks:
            i, size = chunks[k]
            copies.append(pltpu.make_async_copy(out_ref.at[pl.ds(k, size)], out_hbm.at[pl.ds(k, size)], sems.at[i]))
            copies[-1].start()
    for copy in copies:
        copy.wait()


SMEM = pl.BlockSpec(memory_space=pltpu.SMEM)
VMEM = pl.BlockSpec(memory_space=pltpu.VMEM)
ANY = pl.BlockSpec(memory_space=pl.ANY)


def near(*arrays):
    return [pltpu.with_memory_space_constraint(a, pltpu.VMEM) for a in arrays]


def solve(source_field, coupling_below, coupling_above, eigen_stream, eigen_span):
    sizes = rows, kx_total, kx_count, tiles, mode_count, height = sizes_of(source_field)
    partitions = lax.axis_size("gz")
    chips, pairs = mode_count // 2, partitions // 2
    total = mode_count * height
    f32 = jnp.float32
    chunk_sems = pltpu.SemaphoreType.DMA((len(chunks_of(rows)),))

    def move(array, modes_by=0, pair=0, level=0):
        links = []
        for m in range(mode_count):
            for g in range(partitions):
                to = ((g // 2 + level) % pairs) * 2 + ((g % 2) ^ pair)
                links.append((m * partitions + g, (m ^ modes_by) * partitions + to))
        return lax.ppermute(array, ("modes", "gz"), links)

    ports, table, spectral = pl.pallas_call(
        functools.partial(reduce_kernel, sizes),
        out_shape=(
            pltpu.VMEM((2, chips, 4 * height, LANES), f32),
            pltpu.VMEM((SUBLANES, LANES), f32),
            pltpu.VMEM((total, LANES), f32),
        ),
        in_specs=[SMEM, SMEM, SMEM, VMEM, ANY],
        out_specs=(VMEM, VMEM, VMEM),
        scratch_shapes=[pltpu.VMEM(source_field.shape, f32), chunk_sems],
        name="reduce",
    )(coupling_below, coupling_above, eigen_stream, eigen_span.reshape(-1, LANES), source_field)
    blocks = pl.pallas_call(
        functools.partial(regroup_kernel, sizes),
        out_shape=pltpu.VMEM((mode_count, rows, 2, height, LANES), f32),
        in_specs=[ANY],
        out_specs=VMEM,
        scratch_shapes=[pltpu.VMEM(source_field.shape, f32), chunk_sems],
        name="regroup",
    )(source_field)

    taken = move(ports[1], modes_by=1)
    own_parts, pair_parts = [], []
    for d in range(1, chips):
        block = jnp.concatenate([ports[0, d], taken[d]], axis=0)
        pair_parts.append(move(block, modes_by=2 * d, pair=1))
        own_parts.append(move(block, modes_by=2 * d))
    side = move(jnp.concatenate([ports[0, 0], taken[0], table], axis=0), pair=1)
    message = pl.pallas_call(
        functools.partial(merge_kernel, sizes),
        out_shape=pltpu.VMEM((4 * total + SUBLANES, LANES), f32),
        in_specs=[VMEM] * (5 + 2 * (chips - 1)),
        out_specs=VMEM,
        name="merge",
    )(*near(spectral, table, ports, taken, side, *own_parts, *pair_parts))
    messages = [move(message, level=d) for d in range(1, pairs)]
    sources = [move(blocks[d], modes_by=d) if d else blocks[0] for d in range(mode_count)]
    out = pl.pallas_call(
        functools.partial(final_kernel, sizes, pairs),
        out_shape=jax.ShapeDtypeStruct((rows, 2, mode_count, height, LANES), f32),
        in_specs=[VMEM] * (3 + (chips - 1) + (pairs - 1) + mode_count),
        out_specs=ANY,
        scratch_shapes=[
            pltpu.VMEM((rows, 2, mode_count, height, LANES), f32),
            pltpu.VMEM((rows, total, LANES), f32),
            pltpu.VMEM((rows, 2, total, LANES), f32),
            chunk_sems,
        ],
        name="solve",
    )(*near(spectral, table, side, *pair_parts, *messages, *sources))
    out = out.reshape(rows, 2, mode_count * tiles, kx_count, LANES).transpose(0, 1, 3, 2, 4)
    return out.reshape(rows, 2, kx_count, -1)


def solution(mesh):
    in_specs = (P("gz", None, None, "modes"), P("gz"), P("gz"), P(), P())
    out_specs = P("gz", None, "modes", None)
    return jax.shard_map(solve, mesh=mesh, in_specs=in_specs, out_specs=out_specs, check_vma=False)
```

profile of v0, /device:TPU:0, one launch (start us, length us, event | category | flops | bytes accessed | tf_op | source)
XLA Modules:
  0.0 31.3 jit_solution(13173939875337102197)
XLA Ops:
  0.0 1.9 %reduce.1 = (f32[2,2,32,128]{3,2,1,0:T(8,128)S(1)}, f32[8,128]{1,0:T(8,128)S(1)}, f32[32,128]{1,0:T(8,128)S(1)}) custom-call(f32[16]{0:T(128)} %below_ref.1, f32[16]{0:T(128)} %above_ref.1, f32[8]{0:T(128)} %stream_ref.1, f32[16,128]{1,0:T(8,128)} %bitcast.24, f32[16,2,8,512]{3,2,1,0:T(8,128)} %source_hbm.3), custom_call_target="tpu_custom_call" | custom-call | tf_op jit(solution)/shard_map/reduce/pallas_call | solution.py:287
  1.9 0.6 %collective-permute-start = (f32[2,32,128]{2,1,0:T(8,128)S(1)}, f32[2,32,128]{2,1,0:T(8,128)S(1)}, u32[]{:S(2)}, u32[]{:S(2)}) collective-permute-start(f32[2,32,128]{2,1,0:T(8,128)S(1)} %slice_bitcast_fusion.4), channel_id=1, source_target_pairs={{0,8},{1,9},{2,10},{3,11},{4,12},{5,13},{6,14},{7,15},{8,0},{9,1},... | collective-permute-start | bytes 98312 | tf_op jit(solution)/shard_map/ppermute | solution.py:285
  2.5 1.2 %regroup.1 = f32[4,16,2,8,128]{4,3,2,1,0:T(8,128)S(1)} custom-call(f32[16,2,8,512]{3,2,1,0:T(8,128)} %source_hbm.3), custom_call_target="tpu_custom_call" | custom-call | tf_op jit(solution)/shard_map/regroup/pallas_call | solution.py:299
  3.7 2.7 %collective-permute-start.9 = (f32[16,2,8,128]{3,2,1,0:T(8,128)S(1)}, f32[16,2,8,128]{3,2,1,0:T(8,128)S(1)}, u32[]{:S(2)}, u32[]{:S(2)}) collective-permute-start(f32[16,2,8,128]{3,2,1,0:T(8,128)S(1)} %get-tuple-element.11), channel_id=1, source_target_pairs={{0,24},{1,25},{2,26},{3,27},{4,28},{5,29},{6,30},{7,31},{8,16},{9,... | collective-permute-start | bytes 393224 | tf_op jit(solution)/shard_map/ppermute | solution.py:285
  6.4 0.0 collective-permute-start.8
  6.4 0.2 collective-permute-start.7
  6.6 0.0 collective-permute-done.taken_ref
  6.6 1.9 %collective-permute-start.3 = (f32[64,128]{1,0:T(8,128)S(1)}, f32[64,128]{1,0:T(8,128)S(1)}, u32[]{:S(2)}, u32[]{:S(2)}) collective-permute-start(f32[64,128]{1,0:T(8,128)S(1)} %pad_maximum_fusion.1), channel_id=1, source_target_pairs={{0,16},{1,17},{2,18},{3,19},{4,20},{5,21},{6,22},{7,23},{8,24},{9,... | collective-permute-start | bytes 98312 | tf_op jit(solution)/shard_map/ppermute | solution.py:285
  8.6 1.5 %collective-permute-start.1 = (f32[72,128]{1,0:T(8,128)S(1)}, f32[72,128]{1,0:T(8,128)S(1)}, u32[]{:S(2)}, u32[]{:S(2)}) collective-permute-start(f32[72,128]{1,0:T(8,128)S(1)} %pad_maximum_fusion), channel_id=1, source_target_pairs={{0,1},{1,0},{2,3},{3,2},{4,5},{5,4},{6,7},{7,6},{8,9},{9,8},{10,11... | collective-permute-start | bytes 110600 | tf_op jit(solution)/shard_map/ppermute | solution.py:285
  10.0 3.9 %collective-permute-done.3.rest_0_ = f32[64,128]{1,0:T(8,128)S(1)} collective-permute-done((f32[64,128]{1,0:T(8,128)S(1)}, f32[64,128]{1,0:T(8,128)S(1)}, u32[]{:S(2)}, u32[]{:S(2)}) %collective-permute-start.3) | collective-permute-done | bytes 32800 | tf_op jit(solution)/shard_map/ppermute | solution.py:285
  14.0 2.6 %collective-permute-start.2 = (f32[64,128]{1,0:T(8,128)S(1)}, f32[64,128]{1,0:T(8,128)S(1)}, u32[]{:S(2)}, u32[]{:S(2)}) collective-permute-start(f32[64,128]{1,0:T(8,128)S(1)} %pad_maximum_fusion.1), channel_id=1, source_target_pairs={{0,17},{1,16},{2,19},{3,18},{4,21},{5,20},{6,23},{7,22},{8,25},{9,... | collective-permute-start | bytes 98312 | tf_op jit(solution)/shard_map/ppermute | solution.py:285
  16.6 2.2 %collective-permute-done.2.rest_1_.rest_0_ = f32[64,128]{1,0:T(8,128)S(1)} collective-permute-done((f32[64,128]{1,0:T(8,128)S(1)}, f32[64,128]{1,0:T(8,128)S(1)}, u32[]{:S(2)}, u32[]{:S(2)}) %collective-permute-start.2) | collective-permute-done | bytes 32800 | tf_op jit(solution)/shard_map/ppermute | solution.py:285
  18.8 0.0 collective-permute-done.1.side_ref
  18.8 0.3 %merge.1 = f32[136,128]{1,0:T(8,128)S(1)} custom-call(f32[32,128]{1,0:T(8,128)S(1)} %get-tuple-element.8.spectral_ref, f32[8,128]{1,0:T(8,128)S(1)} %get-tuple-element.9.table_ref, f32[2,2,32,128]{3,2,1,0:T(8,128)S(1)} %get-tuple-element.10.ports_ref, f32[2,32,128]{2,1,0:T(8,128)S(1)} %collective-permute-done.taken_ref, ...), custom_call_target="tpu_custom_call" | custom-call | tf_op jit(solution)/shard_map/merge/pallas_call | solution.py:315
  19.2 3.8 %collective-permute-start.6 = (f32[136,128]{1,0:T(8,128)S(1)}, f32[136,128]{1,0:T(8,128)S(1)}, u32[]{:S(2)}, u32[]{:S(2)}) collective-permute-start(f32[136,128]{1,0:T(8,128)S(1)} %merge.1), channel_id=1, source_target_pairs={{0,6},{1,7},{2,0},{3,1},{4,2},{5,3},{6,4},{7,5},{8,14},{9,15},{10,... | collective-permute-start | bytes 208904 | tf_op jit(solution)/shard_map/ppermute | solution.py:285
  22.9 0.0 collective-permute-start.5
  22.9 0.0 collective-permute-done.9.rest_7_
  22.9 1.0 %collective-permute-start.4 = (f32[136,128]{1,0:T(8,128)S(1)}, f32[136,128]{1,0:T(8,128)S(1)}, u32[]{:S(2)}, u32[]{:S(2)}) collective-permute-start(f32[136,128]{1,0:T(8,128)S(1)} %merge.1), channel_id=1, source_target_pairs={{0,2},{1,3},{2,4},{3,5},{4,6},{5,7},{6,0},{7,1},{8,10},{9,11},{10,... | collective-permute-start | bytes 208904 | tf_op jit(solution)/shard_map/ppermute | solution.py:285
  24.0 0.0 collective-permute-done.8.rest_6_
  24.0 0.0 collective-permute-done.7.rest_5_
  24.0 0.9 %collective-permute-done.6.rest_3_ = f32[136,128]{1,0:T(8,128)S(1)} collective-permute-done((f32[136,128]{1,0:T(8,128)S(1)}, f32[136,128]{1,0:T(8,128)S(1)}, u32[]{:S(2)}, u32[]{:S(2)}) %collective-permute-start.6) | collective-permute-done | bytes 69664 | tf_op jit(solution)/shard_map/ppermute | solution.py:285
  24.9 3.3 %collective-permute-done.5.rest_2_ = f32[136,128]{1,0:T(8,128)S(1)} collective-permute-done((f32[136,128]{1,0:T(8,128)S(1)}, f32[136,128]{1,0:T(8,128)S(1)}, u32[]{:S(2)}, u32[]{:S(2)}) %collective-permute-start.5) | collective-permute-done | bytes 69664 | tf_op jit(solution)/shard_map/ppermute | solution.py:285
  28.1 0.9 %collective-permute-done.4.rest_1_ = f32[136,128]{1,0:T(8,128)S(1)} collective-permute-done((f32[136,128]{1,0:T(8,128)S(1)}, f32[136,128]{1,0:T(8,128)S(1)}, u32[]{:S(2)}, u32[]{:S(2)}) %collective-permute-start.4) | collective-permute-done | bytes 69664 | tf_op jit(solution)/shard_map/ppermute | solution.py:285
  29.1 2.2 %solve.1 = f32[16,2,4,8,128]{4,3,2,1,0:T(8,128)} custom-call(f32[32,128]{1,0:T(8,128)S(1)} %get-tuple-element.8.spectral_ref, f32[8,128]{1,0:T(8,128)S(1)} %get-tuple-element.9.table_ref, f32[72,128]{1,0:T(8,128)S(1)} %collective-permute-done.1.side_ref, f32[64,128]{1,0:T(8,128)S(1)} %collective-permute-done.2.rest_1_.rest_0_, ...), custom_call_target="tpu_custom_call" | custom-call | tf_op jit(solution)/shard_map/solve/pallas_call | solution.py:324
  (6 shorter events, 0.1 us)
Async XLA Ops:
  1.9 4.7 %collective-permute-start = (f32[2,32,128]{2,1,0:T(8,128)S(1)}, f32[2,32,128]{2,1,0:T(8,128)S(1)}, u32[]{:S(2)}, u32[]{:S(2)}) collective-permute-start(f32[2,32,128]{2,1,0:T(8,128)S(1)} %slice_bitcast_fusion.4), channel_id=1, source_target_pairs={{0,8},{1,9},{2,10},{3,11},{4,12},{5,13},{6,14},{7,15},{8,0},{9,1},... | collective-permute-start | bytes 98312 | tf_op jit(solution)/shard_map/ppermute | solution.py:285
  3.7 19.2 %collective-permute-start.9 = (f32[16,2,8,128]{3,2,1,0:T(8,128)S(1)}, f32[16,2,8,128]{3,2,1,0:T(8,128)S(1)}, u32[]{:S(2)}, u32[]{:S(2)}) collective-permute-start(f32[16,2,8,128]{3,2,1,0:T(8,128)S(1)} %get-tuple-element.11), channel_id=1, source_target_pairs={{0,24},{1,25},{2,26},{3,27},{4,28},{5,29},{6,30},{7,31},{8,16},{9,... | collective-permute-start | bytes 393224 | tf_op jit(solution)/shard_map/ppermute | solution.py:285
  6.4 17.5 %collective-permute-start.8 = (f32[16,2,8,128]{3,2,1,0:T(8,128)S(1)}, f32[16,2,8,128]{3,2,1,0:T(8,128)S(1)}, u32[]{:S(2)}, u32[]{:S(2)}) collective-permute-start(f32[16,2,8,128]{3,2,1,0:T(8,128)S(1)} %get-tuple-element.12), channel_id=1, source_target_pairs={{0,16},{1,17},{2,18},{3,19},{4,20},{5,21},{6,22},{7,23},{8,24},{9,... | collective-permute-start | bytes 393224 | tf_op jit(solution)/shard_map/ppermute | solution.py:285
  6.4 17.5 %collective-permute-start.7 = (f32[16,2,8,128]{3,2,1,0:T(8,128)S(1)}, f32[16,2,8,128]{3,2,1,0:T(8,128)S(1)}, u32[]{:S(2)}, u32[]{:S(2)}) collective-permute-start(f32[16,2,8,128]{3,2,1,0:T(8,128)S(1)} %get-tuple-element.13), channel_id=1, source_target_pairs={{0,8},{1,9},{2,10},{3,11},{4,12},{5,13},{6,14},{7,15},{8,0},{9,1},... | collective-permute-start | bytes 393224 | tf_op jit(solution)/shard_map/ppermute | solution.py:285
  6.6 7.3 %collective-permute-start.3 = (f32[64,128]{1,0:T(8,128)S(1)}, f32[64,128]{1,0:T(8,128)S(1)}, u32[]{:S(2)}, u32[]{:S(2)}) collective-permute-start(f32[64,128]{1,0:T(8,128)S(1)} %pad_maximum_fusion.1), channel_id=1, source_target_pairs={{0,16},{1,17},{2,18},{3,19},{4,20},{5,21},{6,22},{7,23},{8,24},{9,... | collective-permute-start | bytes 98312 | tf_op jit(solution)/shard_map/ppermute | solution.py:285
  8.6 10.3 %collective-permute-start.1 = (f32[72,128]{1,0:T(8,128)S(1)}, f32[72,128]{1,0:T(8,128)S(1)}, u32[]{:S(2)}, u32[]{:S(2)}) collective-permute-start(f32[72,128]{1,0:T(8,128)S(1)} %pad_maximum_fusion), channel_id=1, source_target_pairs={{0,1},{1,0},{2,3},{3,2},{4,5},{5,4},{6,7},{7,6},{8,9},{9,8},{10,11... | collective-permute-start | bytes 110600 | tf_op jit(solution)/shard_map/ppermute | solution.py:285
  14.0 4.8 %collective-permute-start.2 = (f32[64,128]{1,0:T(8,128)S(1)}, f32[64,128]{1,0:T(8,128)S(1)}, u32[]{:S(2)}, u32[]{:S(2)}) collective-permute-start(f32[64,128]{1,0:T(8,128)S(1)} %pad_maximum_fusion.1), channel_id=1, source_target_pairs={{0,17},{1,16},{2,19},{3,18},{4,21},{5,20},{6,23},{7,22},{8,25},{9,... | collective-permute-start | bytes 98312 | tf_op jit(solution)/shard_map/ppermute | solution.py:285
  19.2 5.7 %collective-permute-start.6 = (f32[136,128]{1,0:T(8,128)S(1)}, f32[136,128]{1,0:T(8,128)S(1)}, u32[]{:S(2)}, u32[]{:S(2)}) collective-permute-start(f32[136,128]{1,0:T(8,128)S(1)} %merge.1), channel_id=1, source_target_pairs={{0,6},{1,7},{2,0},{3,1},{4,2},{5,3},{6,4},{7,5},{8,14},{9,15},{10,... | collective-permute-start | bytes 208904 | tf_op jit(solution)/shard_map/ppermute | solution.py:285
  22.9 5.2 %collective-permute-start.5 = (f32[136,128]{1,0:T(8,128)S(1)}, f32[136,128]{1,0:T(8,128)S(1)}, u32[]{:S(2)}, u32[]{:S(2)}) collective-permute-start(f32[136,128]{1,0:T(8,128)S(1)} %merge.1), channel_id=1, source_target_pairs={{0,4},{1,5},{2,6},{3,7},{4,0},{5,1},{6,2},{7,3},{8,12},{9,13},{10,... | collective-permute-start | bytes 208904 | tf_op jit(solution)/shard_map/ppermute | solution.py:285
  22.9 6.1 %collective-permute-start.4 = (f32[136,128]{1,0:T(8,128)S(1)}, f32[136,128]{1,0:T(8,128)S(1)}, u32[]{:S(2)}, u32[]{:S(2)}) collective-permute-start(f32[136,128]{1,0:T(8,128)S(1)} %merge.1), channel_id=1, source_target_pairs={{0,2},{1,3},{2,4},{3,5},{4,6},{5,7},{6,0},{7,1},{8,10},{9,11},{10,... | collective-permute-start | bytes 208904 | tf_op jit(solution)/shard_map/ppermute | solution.py:285
where the time goes:
time: 31.5 us; the launch traced here: 31.3 us
  starting transfers between devices  14.2 us (45%)
  waiting for transfers between devices  11.3 us (36%)
  Pallas kernels  5.65 us (18%)
    ppermute x10, starting transfers between devices, move(): return lax.ppermute(array, ('modes', 'gz'), links)  14.2 us
    ppermute x10, waiting for transfers between devices, move(): return lax.ppermute(array, ('modes', 'gz'), links)  11.3 us
    pallas_call x1, Pallas kernels, solve(): pl.pallas_call(functools.partial(final_kernel, sizes, pairs), out_shape=j...  2.2 us
    pallas_call x1, Pallas kernels, solve(): pl.pallas_call(functools.partial(reduce_kernel, sizes), out_shape=(pltpu....  1.89 us
    pallas_call x1, Pallas kernels, solve(): pl.pallas_call(functools.partial(regroup_kernel, sizes), out_shape=pltpu....  1.21 us
  transfers between devices with their start and end apart: 10, of which 5 were waited for; matrix products, arithmetic and copies ran while one was open for 0% of the time, Pallas kernels for 5%

commit v1 on v0

--- a/solution.py
+++ b/solution.py
@@ -24,15 +24,26 @@
     return [(first, size) for first in range(0, rows, size)]
 
 
-def reduce_kernel(sizes, below_ref, above_ref, stream_ref, span_ref, source_hbm, ports_ref, table_ref, spectral_ref, source_ref, sems):
+def fetch(pairs, sems):
+    copies = [pltpu.make_async_copy(source, to, sems.at[i]) for i, (source, to) in enumerate(pairs)]
+    for copy in copies:
+        copy.start()
+    return copies
+
+
+def reduce_kernel(
+    sizes, below_hbm, above_hbm, stream_hbm, span_hbm, source_hbm,
+    ports_ref, table_ref, spectral_ref, source_ref, below_ref, above_ref, stream_ref, span_ref, small_sems, sems,
+):
     rows, kx_total, kx_count, tiles, mode_count, height = sizes
     me, partition = lax.axis_index("modes"), lax.axis_index("gz")
-    copies = []
-    for i, (first, size) in enumerate(chunks_of(rows)):
-        copies.append(
-            pltpu.make_async_copy(source_hbm.at[pl.ds(first, size)], source_ref.at[pl.ds(first, size)], sems.at[i])
-        )
-        copies[-1].start()
+    small = fetch(
+        [(below_hbm, below_ref), (above_hbm, above_ref), (stream_hbm, stream_ref), (span_hbm, span_ref)], small_sems
+    )
+    parts = [pl.ds(first, size) for first, size in chunks_of(rows)]
+    copies = fetch([(source_hbm.at[p], source_ref.at[p]) for p in parts], sems)
+    for copy in small:
+        copy.wait()
     lower = [below_ref[k] for k in range(rows)]
     upper = [above_ref[k] for k in range(rows)]
     lower[0] = jnp.where(partition == 0, 0.0, lower[0])
@@ -82,25 +93,17 @@
                 ports_ref[to % 2, to // 2, at : at + kx_count, :] = values[i][t][dest * kx_count : (dest + 1) * kx_count]
 
 
-def regroup_kernel(sizes, source_hbm, blocks_ref, source_ref, sems):
+def regroup_kernel(sizes, source_ref, blocks_ref):
     rows, _, kx_count, tiles, mode_count, _ = sizes
     me = lax.axis_index("modes")
-    copies = []
-    for i, (first, size) in enumerate(chunks_of(rows)):
-        copies.append(
-            pltpu.make_async_copy(source_hbm.at[pl.ds(first, size)], source_ref.at[pl.ds(first, size)], sems.at[i])
-        )
-        copies[-1].start()
-    for i, (first, size) in enumerate(chunks_of(rows)):
-        copies[i].wait()
-        for k in range(first, first + size):
+    for dest in range(mode_count):
+        to = dest ^ me
+        lines = slice(dest * kx_count, (dest + 1) * kx_count)
+        for k in range(rows):
             for c in range(2):
                 for t in range(tiles):
                     at = t * kx_count
-                    for dest in range(mode_count):
-                        blocks_ref[dest ^ me, k, c, at : at + kx_count, :] = source_ref[
-                            k, c, dest * kx_count : (dest + 1) * kx_count, t * LANES : (t + 1) * LANES
-                        ]
+                    blocks_ref[to, k, c, at : at + kx_count, :] = source_ref[k, c, lines, t * LANES : (t + 1) * LANES]
 
 
 def climb(spectral, num, den, near, far):
@@ -171,17 +174,50 @@
         store(c, low[c] + ratio * (high[c] + passed * low[2 + c]))
 
 
-def final_kernel(sizes, pairs, spectral_ref, table_ref, side_ref, *rest):
+def prepare_kernel(sizes, spectral_ref, table_ref, *rest):
+    rows, _, _, _, mode_count, _ = sizes
+    sources, (part_ref, low_ref, high_ref) = rest[:mode_count], rest[mode_count:]
+    spectral, table = spectral_ref[...], table_ref[...]
+    lower, upper = couplings(table, 0, rows), couplings(table, 1, rows)
+    grown = jnp.ones(spectral.shape, jnp.float32)
+    carried = grown
+    partial = [jnp.zeros(spectral.shape, jnp.float32)] * 2
+    for k in range(rows):
+        held = spectral + lower[k] * grown
+        inverse = 1.0 / (upper[k] + held)
+        grown = held * inverse
+        scaled = lower[k] * inverse
+        carried = scaled * carried
+        low_ref[k] = carried
+        high_ref[k] = upper[k] * inverse
+        for c in range(2):
+            source = jnp.concatenate([sources[d][k, c] for d in range(mode_count)], axis=0)
+            partial[c] = source * inverse + scaled * partial[c]
+            part_ref[k, c] = partial[c]
+    low, high = low_ref[rows - 1], high_ref[rows - 1]
+    for k in range(rows - 2, -1, -1):
+        factor = high_ref[k]
+        low = low_ref[k] + factor * low
+        low_ref[k] = low
+        high = factor * high
+        high_ref[k] = high
+        for c in range(2):
+            partial[c] = part_ref[k, c] + factor * partial[c]
+            part_ref[k, c] = partial[c]
+
+
+def final_kernel(sizes, pairs, spectral_ref, table_ref, side_ref, part_ref, low_ref, high_ref, *rest):
     rows, _, _, _, mode_count, height = sizes
     chips = mode_count // 2
     total = mode_count * height
     port = 4 * height
     pair_refs, rest = rest[: chips - 1], rest[chips - 1 :]
     messages, rest = rest[: pairs - 1], rest[pairs - 1 :]
-    sources, rest = rest[:mode_count], rest[mode_count:]
-    out_hbm, out_ref, factor_ref, partial_ref, sems = rest
+    out_hbm, out_ref, level_ref, sems = rest
     me, partition = lax.axis_index("modes"), lax.axis_index("gz")
     upside, level = partition % 2 == 1, partition // 2
+    for d in range(1, pairs):
+        level_ref[level ^ d] = messages[d - 1][...]
     spectral = spectral_ref[...]
     one = jnp.ones((total, LANES), jnp.float32)
     zero = jnp.zeros((total, LANES), jnp.float32)
@@ -205,9 +241,8 @@
         far = [v for b in blocks for v in couplings(table, 2 * b, rows)]
         return enter(state, ports, 2, 0, near[::-1], far[::-1])
 
-    def of_message(d):
-        ref = messages[d - 1]
-        return (lambda i: ref[i * total : (i + 1) * total, :]), ref[4 * total :, :], (0, 1)
+    def of_level(at):
+        return (lambda i: level_ref[at, i * total : (i + 1) * total, :]), level_ref[at, 4 * total :, :], (0, 1)
 
     def pair_chunk(d, at):
         at += (d % 2) * port
@@ -220,46 +255,41 @@
 
         return ports, side_ref[2 * port :, :], (0,)
 
+    def of_own():
+        return (lambda i: part_ref[0 if i < 2 else rows - 1, i % 2]), table_ref[...], (0,)
+
     below, above = start, start
-    for d in range(pairs - 1, 0, -1):
-        below = lax.cond(level >= d, lambda s, d=d: up(s, *of_message(d)), lambda s: s, below)
-    for d in range(1, pairs):
-        above = lax.cond(level < d, lambda s, d=d: down(s, *of_message(d)), lambda s: s, above)
-    below = lax.cond(upside, lambda s: up(s, *of_pair()), lambda s: s, below)
-    above = lax.cond(upside, lambda s: s, lambda s: down(s, *of_pair()), above)
-
-    table = table_ref[...]
-    lower, upper = couplings(table, 0, rows), couplings(table, 1, rows)
-    grown, _, *partial = below
-    for k in range(rows):
-        held = spectral + lower[k] * grown
-        inverse = 1.0 / (upper[k] + held)
-        factor = upper[k] * inverse
-        grown = held * inverse
-        factor_ref[k] = factor
-        for c in range(2):
-            source = jnp.concatenate([sources[d][k, c] for d in range(mode_count)], axis=0)
-            partial[c] = (source + lower[k] * partial[c]) * inverse
-            partial_ref[k, c] = partial[c]
-    inverse = 1.0 / (grown + factor * above[0])
-    value = [(partial[c] + factor * above[2 + c]) * inverse for c in range(2)]
-    chunks = {first: (i, size) for i, (first, size) in enumerate(chunks_of(rows))}
+    for at in range(pairs - 1):
+        below = lax.cond(at < level, lambda s, at=at: up(s, *of_level(at)), lambda s: s, below)
+    for at in range(pairs - 1, 0, -1):
+        above = lax.cond(at > level, lambda s, at=at: down(s, *of_level(at)), lambda s: s, above)
+    below, above = lax.cond(
+        upside, lambda b, a: (up(b, *of_pair()), a), lambda b, a: (b, down(a, *of_pair())), below, above
+    )
+    leaving_up, leaving_down = up(below, *of_own()), down(above, *of_own())
+    inverse_up = 1.0 / (leaving_up[0] + leaving_up[1] * above[0])
+    inverse_down = 1.0 / (leaving_down[0] + leaving_down[1] * below[0])
+    under, over = [], []
+    for c in range(2, 4):
+        last = (leaving_up[c] + leaving_up[1] * above[c]) * inverse_up
+        over.append(above[c] + above[1] * last)
+        first = (leaving_down[c] + leaving_down[1] * below[c]) * inverse_down
+        under.append(below[c] + below[1] * first)
     copies = []
-    for k in range(rows - 1, -1, -1):
-        for c in range(2):
-            if k < rows - 1:
-                value[c] = partial_ref[k, c] + factor_ref[k] * value[c]
-            for d in range(mode_count):
-                out_ref[k, c, me ^ d] = value[c][d * height : (d + 1) * height]
-        if k in chunks:
-            i, size = chunks[k]
-            copies.append(pltpu.make_async_copy(out_ref.at[pl.ds(k, size)], out_hbm.at[pl.ds(k, size)], sems.at[i]))
-            copies[-1].start()
+    for i, (first, size) in enumerate(chunks_of(rows)):
+        for k in range(first, first + size):
+            low, high = low_ref[k], high_ref[k]
+            for c in range(2):
+                value = part_ref[k, c] + low * under[c] + high * over[c]
+                for d in range(mode_count):
+                    out_ref[k, c, me ^ d] = value[d * height : (d + 1) * height]
+        part = pl.ds(first, size)
+        copies.append(pltpu.make_async_copy(out_ref.at[part], out_hbm.at[part], sems.at[i]))
+        copies[-1].start()
     for copy in copies:
         copy.wait()
 
 
-SMEM = pl.BlockSpec(memory_space=pltpu.SMEM)
 VMEM = pl.BlockSpec(memory_space=pltpu.VMEM)
 ANY = pl.BlockSpec(memory_space=pl.ANY)
 
@@ -280,30 +310,38 @@
         links = []
         for m in range(mode_count):
             for g in range(partitions):
-                to = ((g // 2 + level) % pairs) * 2 + ((g % 2) ^ pair)
+                to = ((g // 2) ^ level) * 2 + ((g % 2) ^ pair)
                 links.append((m * partitions + g, (m ^ modes_by) * partitions + to))
         return lax.ppermute(array, ("modes", "gz"), links)
 
-    ports, table, spectral = pl.pallas_call(
+    span = eigen_span.reshape(-1, LANES)
+    ports, table, spectral, source = pl.pallas_call(
         functools.partial(reduce_kernel, sizes),
         out_shape=(
             pltpu.VMEM((2, chips, 4 * height, LANES), f32),
             pltpu.VMEM((SUBLANES, LANES), f32),
             pltpu.VMEM((total, LANES), f32),
+            pltpu.VMEM(source_field.shape, f32),
         ),
-        in_specs=[SMEM, SMEM, SMEM, VMEM, ANY],
-        out_specs=(VMEM, VMEM, VMEM),
-        scratch_shapes=[pltpu.VMEM(source_field.shape, f32), chunk_sems],
+        in_specs=[ANY] * 5,
+        out_specs=(VMEM,) * 4,
+        scratch_shapes=[
+            pltpu.SMEM(coupling_below.shape, f32),
+            pltpu.SMEM(coupling_above.shape, f32),
+            pltpu.SMEM(eigen_stream.shape, f32),
+            pltpu.VMEM(span.shape, f32),
+            pltpu.SemaphoreType.DMA((4,)),
+            chunk_sems,
+        ],
         name="reduce",
-    )(coupling_below, coupling_above, eigen_stream, eigen_span.reshape(-1, LANES), source_field)
+    )(coupling_below, coupling_above, eigen_stream, span, source_field)
     blocks = pl.pallas_call(
         functools.partial(regroup_kernel, sizes),
         out_shape=pltpu.VMEM((mode_count, rows, 2, height, LANES), f32),
-        in_specs=[ANY],
+        in_specs=[VMEM],
         out_specs=VMEM,
-        scratch_shapes=[pltpu.VMEM(source_field.shape, f32), chunk_sems],
         name="regroup",
-    )(source_field)
+    )(*near(source))
 
     taken = move(ports[1], modes_by=1)
     own_parts, pair_parts = [], []
@@ -312,6 +350,7 @@
         pair_parts.append(move(block, modes_by=2 * d, pair=1))
         own_parts.append(move(block, modes_by=2 * d))
     side = move(jnp.concatenate([ports[0, 0], taken[0], table], axis=0), pair=1)
+    sources = [move(blocks[d], modes_by=d) if d else blocks[0] for d in range(mode_count)]
     message = pl.pallas_call(
         functools.partial(merge_kernel, sizes),
         out_shape=pltpu.VMEM((4 * total + SUBLANES, LANES), f32),
@@ -320,20 +359,29 @@
         name="merge",
     )(*near(spectral, table, ports, taken, side, *own_parts, *pair_parts))
     messages = [move(message, level=d) for d in range(1, pairs)]
-    sources = [move(blocks[d], modes_by=d) if d else blocks[0] for d in range(mode_count)]
+    local = pl.pallas_call(
+        functools.partial(prepare_kernel, sizes),
+        out_shape=(
+            pltpu.VMEM((rows, 2, total, LANES), f32),
+            pltpu.VMEM((rows, total, LANES), f32),
+            pltpu.VMEM((rows, total, LANES), f32),
+        ),
+        in_specs=[VMEM] * (2 + mode_count),
+        out_specs=(VMEM,) * 3,
+        name="prepare",
+    )(*near(spectral, table, *sources))
     out = pl.pallas_call(
         functools.partial(final_kernel, sizes, pairs),
         out_shape=jax.ShapeDtypeStruct((rows, 2, mode_count, height, LANES), f32),
-        in_specs=[VMEM] * (3 + (chips - 1) + (pairs - 1) + mode_count),
+        in_specs=[VMEM] * (6 + (chips - 1) + (pairs - 1)),
         out_specs=ANY,
         scratch_shapes=[
             pltpu.VMEM((rows, 2, mode_count, height, LANES), f32),
-            pltpu.VMEM((rows, total, LANES), f32),
-            pltpu.VMEM((rows, 2, total, LANES), f32),
+            pltpu.VMEM((pairs, 4 * total + SUBLANES, LANES), f32),
             chunk_sems,
         ],
         name="solve",
-    )(*near(spectral, table, side, *pair_parts, *messages, *sources))
+    )(*near(spectral, table, side, *local, *pair_parts, *messages))
     out = out.reshape(rows, 2, mode_count * tiles, kx_count, LANES).transpose(0, 1, 3, 2, 4)
     return out.reshape(rows, 2, kx_count, -1)
 

time: 31.5 us -> 27.1 us (0.86)
  starting transfers between devices: 14.2 us -> 12.6 us
  waiting for transfers between devices: 11.3 us -> 9.85 us
  Pallas kernels: 5.65 us -> 4.31 us
    ppermute x10, starting transfers between devices: 14.2 us -> 12.6 us  [move(): return lax.ppermute(array, ('modes', 'gz'), links)]
    ppermute x10, waiting for transfers between devices: 11.3 us -> 9.85 us  [move(): return lax.ppermute(array, ('modes', 'gz'), links)]
    pallas_call x1, Pallas kernels: 1.21 us -> 0.18 us  [solve(): pl.pallas_call(functools.partial(regroup_kernel, sizes), out_shape=pltpu....]
    pallas_call x1, Pallas kernels: 1.89 us -> 1.24 us  [solve(): pl.pallas_call(functools.partial(reduce_kernel, sizes), out_shape=(pltpu....]
    pallas_call x0 -> x1, Pallas kernels: none -> 0.36 us  [solve(): pl.pallas_call(functools.partial(prepare_kernel, sizes), out_shape=(pltpu...]
  transfers between devices with their start and end apart: 10 -> 10, of which waited for: 5 -> 5; matrix products, arithmetic and copies ran while one was open for 0% -> 0% of each run, Pallas kernels for 5% -> 3%
where the time goes in v1:
time: 27.1 us; the launch traced here: 26.9 us
  starting transfers between devices  12.6 us (46%)
  waiting for transfers between devices  9.85 us (36%)
  Pallas kernels  4.31 us (16%)
    ppermute x10, starting transfers between devices, move(): return lax.ppermute(array, ('modes', 'gz'), links)  12.6 us
    ppermute x10, waiting for transfers between devices, move(): return lax.ppermute(array, ('modes', 'gz'), links)  9.85 us
    pallas_call x1, Pallas kernels, solve(): pl.pallas_call(functools.partial(final_kernel, sizes, pairs), out_shape=j...  2.19 us
    pallas_call x1, Pallas kernels, solve(): pl.pallas_call(functools.partial(reduce_kernel, sizes), out_shape=(pltpu....  1.24 us
  transfers between devices with their start and end apart: 10, of which 5 were waited for; matrix products, arithmetic and copies ran while one was open for 0% of the time, Pallas kernels for 3%

profile of v1, /device:TPU:0, one launch (start us, length us, event | category | flops | bytes accessed | tf_op | source)
XLA Modules:
  0.0 26.9 jit_solution(8353697113747115464)
XLA Ops:
  0.0 1.2 %reduce.1 = (f32[2,2,32,128]{3,2,1,0:T(8,128)S(1)}, f32[8,128]{1,0:T(8,128)S(1)}, f32[32,128]{1,0:T(8,128)S(1)}, f32[16,2,8,512]{3,2,1,0:T(8,128)S(1)}) custom-call(f32[16]{0:T(128)} %below_hbm.1, f32[16]{0:T(128)} %above_hbm.1, f32[8]{0:T(128)} %stream_hbm.1, f32[16,128]{1,0:T(8,128)} %bitcast.24, f32[16,2,8,512]{3,2,1,0:T(8,128)} %source_hbm.1), custom_call_target="tpu_custom_call" | custom-call | tf_op jit(solution)/shard_map/reduce/pallas_call | solution.py:318
  1.3 0.6 %collective-permute-start = (f32[2,32,128]{2,1,0:T(8,128)S(1)}, f32[2,32,128]{2,1,0:T(8,128)S(1)}, u32[]{:S(2)}, u32[]{:S(2)}) collective-permute-start(f32[2,32,128]{2,1,0:T(8,128)S(1)} %slice_bitcast_fusion.4), channel_id=1, source_target_pairs={{0,8},{1,9},{2,10},{3,11},{4,12},{5,13},{6,14},{7,15},{8,0},{9,1},... | collective-permute-start | bytes 98312 | tf_op jit(solution)/shard_map/ppermute | solution.py:315
  1.8 0.2 regroup.1
  2.0 0.1 collective-permute-start.2
  2.1 3.0 %collective-permute-start.3 = (f32[16,2,8,128]{3,2,1,0:T(8,128)S(1)}, f32[16,2,8,128]{3,2,1,0:T(8,128)S(1)}, u32[]{:S(2)}, u32[]{:S(2)}) collective-permute-start(f32[16,2,8,128]{3,2,1,0:T(8,128)S(1)} %get-tuple-element.20), channel_id=1, source_target_pairs={{0,16},{1,17},{2,18},{3,19},{4,20},{5,21},{6,22},{7,23},{8,24},{9,... | collective-permute-start | bytes 393224 | tf_op jit(solution)/shard_map/ppermute | solution.py:315
  5.1 0.0 collective-permute-start.4
  5.1 0.0 collective-permute-done.taken_ref
  5.2 2.4 %collective-permute-start.5 = (f32[64,128]{1,0:T(8,128)S(1)}, f32[64,128]{1,0:T(8,128)S(1)}, u32[]{:S(2)}, u32[]{:S(2)}) collective-permute-start(f32[64,128]{1,0:T(8,128)S(1)} %pad_maximum_fusion.1), channel_id=1, source_target_pairs={{0,17},{1,16},{2,19},{3,18},{4,21},{5,20},{6,23},{7,22},{8,25},{9,... | collective-permute-start | bytes 98312 | tf_op jit(solution)/shard_map/ppermute | solution.py:315
  7.6 0.5 %collective-permute-start.1 = (f32[72,128]{1,0:T(8,128)S(1)}, f32[72,128]{1,0:T(8,128)S(1)}, u32[]{:S(2)}, u32[]{:S(2)}) collective-permute-start(f32[72,128]{1,0:T(8,128)S(1)} %pad_maximum_fusion), channel_id=1, source_target_pairs={{0,1},{1,0},{2,3},{3,2},{4,5},{5,4},{6,7},{7,6},{8,9},{9,8},{10,11... | collective-permute-start | bytes 110600 | tf_op jit(solution)/shard_map/ppermute | solution.py:315
  8.1 1.9 %collective-permute-done.5.rest_1_.rest_0_ = f32[64,128]{1,0:T(8,128)S(1)} collective-permute-done((f32[64,128]{1,0:T(8,128)S(1)}, f32[64,128]{1,0:T(8,128)S(1)}, u32[]{:S(2)}, u32[]{:S(2)}) %collective-permute-start.5) | collective-permute-done | bytes 32800 | tf_op jit(solution)/shard_map/ppermute | solution.py:315
  10.0 1.6 %collective-permute-start.6 = (f32[64,128]{1,0:T(8,128)S(1)}, f32[64,128]{1,0:T(8,128)S(1)}, u32[]{:S(2)}, u32[]{:S(2)}) collective-permute-start(f32[64,128]{1,0:T(8,128)S(1)} %pad_maximum_fusion.1), channel_id=1, source_target_pairs={{0,16},{1,17},{2,18},{3,19},{4,20},{5,21},{6,22},{7,23},{8,24},{9,... | collective-permute-start | bytes 98312 | tf_op jit(solution)/shard_map/ppermute | solution.py:315
  11.7 2.3 %collective-permute-done.6.rest_0_ = f32[64,128]{1,0:T(8,128)S(1)} collective-permute-done((f32[64,128]{1,0:T(8,128)S(1)}, f32[64,128]{1,0:T(8,128)S(1)}, u32[]{:S(2)}, u32[]{:S(2)}) %collective-permute-start.6) | collective-permute-done | bytes 32800 | tf_op jit(solution)/shard_map/ppermute | solution.py:315
  14.0 0.0 collective-permute-done.1.side_ref
  14.0 0.3 %merge.1 = f32[136,128]{1,0:T(8,128)S(1)} custom-call(f32[32,128]{1,0:T(8,128)S(1)} %get-tuple-element.12.spectral_ref, f32[8,128]{1,0:T(8,128)S(1)} %get-tuple-element.13.table_ref, f32[2,2,32,128]{3,2,1,0:T(8,128)S(1)} %get-tuple-element.14.ports_ref, f32[2,32,128]{2,1,0:T(8,128)S(1)} %collective-permute-done.taken_ref, ...), custom_call_target="tpu_custom_call" | custom-call | tf_op jit(solution)/shard_map/merge/pallas_call | solution.py:354
  14.3 1.7 %collective-permute-start.7 = (f32[136,128]{1,0:T(8,128)S(1)}, f32[136,128]{1,0:T(8,128)S(1)}, u32[]{:S(2)}, u32[]{:S(2)}) collective-permute-start(f32[136,128]{1,0:T(8,128)S(1)} %merge.1), channel_id=1, source_target_pairs={{0,2},{1,3},{2,0},{3,1},{4,6},{5,7},{6,4},{7,5},{8,10},{9,11},{10,... | collective-permute-start | bytes 208904 | tf_op jit(solution)/shard_map/ppermute | solution.py:315
  16.0 2.6 %collective-permute-start.8 = (f32[136,128]{1,0:T(8,128)S(1)}, f32[136,128]{1,0:T(8,128)S(1)}, u32[]{:S(2)}, u32[]{:S(2)}) collective-permute-start(f32[136,128]{1,0:T(8,128)S(1)} %merge.1), channel_id=1, source_target_pairs={{0,4},{1,5},{2,6},{3,7},{4,0},{5,1},{6,2},{7,3},{8,12},{9,13},{10,... | collective-permute-start | bytes 208904 | tf_op jit(solution)/shard_map/ppermute | solution.py:315
  18.6 0.0 collective-permute-done.2.rest_1_
  18.6 0.1 collective-permute-start.9
  18.8 0.0 collective-permute-done.3.rest_2_
  18.8 0.0 collective-permute-done.4.rest_3_
  18.8 0.4 %prepare.1 = (f32[16,2,32,128]{3,2,1,0:T(8,128)S(1)}, f32[16,32,128]{2,1,0:T(8,128)S(1)}, f32[16,32,128]{2,1,0:T(8,128)S(1)}) custom-call(f32[32,128]{1,0:T(8,128)S(1)} %get-tuple-element.12.spectral_ref, f32[8,128]{1,0:T(8,128)S(1)} %get-tuple-element.13.table_ref, f32[16,2,8,128]{3,2,1,0:T(8,128)S(1)} %get-tuple-element.22.rest_0_, ...), custom_call_target="tpu_custom_call" | custom-call | tf_op jit(solution)/shard_map/prepare/pallas_call | solution.py:362
  19.1 0.2 collective-permute-done.7.rest_1_
  19.4 3.4 %collective-permute-done.8.rest_2_ = f32[136,128]{1,0:T(8,128)S(1)} collective-permute-done((f32[136,128]{1,0:T(8,128)S(1)}, f32[136,128]{1,0:T(8,128)S(1)}, u32[]{:S(2)}, u32[]{:S(2)}) %collective-permute-start.8) | collective-permute-done | bytes 69664 | tf_op jit(solution)/shard_map/ppermute | solution.py:315
  22.7 2.0 %collective-permute-done.9.rest_3_ = f32[136,128]{1,0:T(8,128)S(1)} collective-permute-done((f32[136,128]{1,0:T(8,128)S(1)}, f32[136,128]{1,0:T(8,128)S(1)}, u32[]{:S(2)}, u32[]{:S(2)}) %collective-permute-start.9) | collective-permute-done | bytes 69664 | tf_op jit(solution)/shard_map/ppermute | solution.py:315
  24.7 2.2 %solve.1 = f32[16,2,4,8,128]{4,3,2,1,0:T(8,128)} custom-call(f32[32,128]{1,0:T(8,128)S(1)} %get-tuple-element.12.spectral_ref, f32[8,128]{1,0:T(8,128)S(1)} %get-tuple-element.13.table_ref, f32[72,128]{1,0:T(8,128)S(1)} %collective-permute-done.1.side_ref, f32[16,2,32,128]{3,2,1,0:T(8,128)S(1)} %get-tuple-element.16.part_ref, ...), custom_call_target="tpu_custom_call" | custom-call | tf_op jit(solution)/shard_map/solve/pallas_call | solution.py:373
  (6 shorter events, 0.1 us)
Async XLA Ops:
  1.3 3.9 %collective-permute-start = (f32[2,32,128]{2,1,0:T(8,128)S(1)}, f32[2,32,128]{2,1,0:T(8,128)S(1)}, u32[]{:S(2)}, u32[]{:S(2)}) collective-permute-start(f32[2,32,128]{2,1,0:T(8,128)S(1)} %slice_bitcast_fusion.4), channel_id=1, source_target_pairs={{0,8},{1,9},{2,10},{3,11},{4,12},{5,13},{6,14},{7,15},{8,0},{9,1},... | collective-permute-start | bytes 98312 | tf_op jit(solution)/shard_map/ppermute | solution.py:315
  2.0 16.6 %collective-permute-start.2 = (f32[16,2,8,128]{3,2,1,0:T(8,128)S(1)}, f32[16,2,8,128]{3,2,1,0:T(8,128)S(1)}, u32[]{:S(2)}, u32[]{:S(2)}) collective-permute-start(f32[16,2,8,128]{3,2,1,0:T(8,128)S(1)} %get-tuple-element.21), channel_id=1, source_target_pairs={{0,8},{1,9},{2,10},{3,11},{4,12},{5,13},{6,14},{7,15},{8,0},{9,1},... | collective-permute-start | bytes 393224 | tf_op jit(solution)/shard_map/ppermute | solution.py:315
  2.1 16.6 %collective-permute-start.3 = (f32[16,2,8,128]{3,2,1,0:T(8,128)S(1)}, f32[16,2,8,128]{3,2,1,0:T(8,128)S(1)}, u32[]{:S(2)}, u32[]{:S(2)}) collective-permute-start(f32[16,2,8,128]{3,2,1,0:T(8,128)S(1)} %get-tuple-element.20), channel_id=1, source_target_pairs={{0,16},{1,17},{2,18},{3,19},{4,20},{5,21},{6,22},{7,23},{8,24},{9,... | collective-permute-start | bytes 393224 | tf_op jit(solution)/shard_map/ppermute | solution.py:315
  5.1 13.7 %collective-permute-start.4 = (f32[16,2,8,128]{3,2,1,0:T(8,128)S(1)}, f32[16,2,8,128]{3,2,1,0:T(8,128)S(1)}, u32[]{:S(2)}, u32[]{:S(2)}) collective-permute-start(f32[16,2,8,128]{3,2,1,0:T(8,128)S(1)} %get-tuple-element.19), channel_id=1, source_target_pairs={{0,24},{1,25},{2,26},{3,27},{4,28},{5,29},{6,30},{7,31},{8,16},{9,... | collective-permute-start | bytes 393224 | tf_op jit(solution)/shard_map/ppermute | solution.py:315
  5.2 4.9 %collective-permute-start.5 = (f32[64,128]{1,0:T(8,128)S(1)}, f32[64,128]{1,0:T(8,128)S(1)}, u32[]{:S(2)}, u32[]{:S(2)}) collective-permute-start(f32[64,128]{1,0:T(8,128)S(1)} %pad_maximum_fusion.1), channel_id=1, source_target_pairs={{0,17},{1,16},{2,19},{3,18},{4,21},{5,20},{6,23},{7,22},{8,25},{9,... | collective-permute-start | bytes 98312 | tf_op jit(solution)/shard_map/ppermute | solution.py:315
  7.6 6.4 %collective-permute-start.1 = (f32[72,128]{1,0:T(8,128)S(1)}, f32[72,128]{1,0:T(8,128)S(1)}, u32[]{:S(2)}, u32[]{:S(2)}) collective-permute-start(f32[72,128]{1,0:T(8,128)S(1)} %pad_maximum_fusion), channel_id=1, source_target_pairs={{0,1},{1,0},{2,3},{3,2},{4,5},{5,4},{6,7},{7,6},{8,9},{9,8},{10,11... | collective-permute-start | bytes 110600 | tf_op jit(solution)/shard_map/ppermute | solution.py:315
  10.0 3.9 %collective-permute-start.6 = (f32[64,128]{1,0:T(8,128)S(1)}, f32[64,128]{1,0:T(8,128)S(1)}, u32[]{:S(2)}, u32[]{:S(2)}) collective-permute-start(f32[64,128]{1,0:T(8,128)S(1)} %pad_maximum_fusion.1), channel_id=1, source_target_pairs={{0,16},{1,17},{2,18},{3,19},{4,20},{5,21},{6,22},{7,23},{8,24},{9,... | collective-permute-start | bytes 98312 | tf_op jit(solution)/shard_map/ppermute | solution.py:315
  14.3 5.0 %collective-permute-start.7 = (f32[136,128]{1,0:T(8,128)S(1)}, f32[136,128]{1,0:T(8,128)S(1)}, u32[]{:S(2)}, u32[]{:S(2)}) collective-permute-start(f32[136,128]{1,0:T(8,128)S(1)} %merge.1), channel_id=1, source_target_pairs={{0,2},{1,3},{2,0},{3,1},{4,6},{5,7},{6,4},{7,5},{8,10},{9,11},{10,... | collective-permute-start | bytes 208904 | tf_op jit(solution)/shard_map/ppermute | solution.py:315
  16.0 6.7 %collective-permute-start.8 = (f32[136,128]{1,0:T(8,128)S(1)}, f32[136,128]{1,0:T(8,128)S(1)}, u32[]{:S(2)}, u32[]{:S(2)}) collective-permute-start(f32[136,128]{1,0:T(8,128)S(1)} %merge.1), channel_id=1, source_target_pairs={{0,4},{1,5},{2,6},{3,7},{4,0},{5,1},{6,2},{7,3},{8,12},{9,13},{10,... | collective-permute-start | bytes 208904 | tf_op jit(solution)/shard_map/ppermute | solution.py:315
  18.6 6.1 %collective-permute-start.9 = (f32[136,128]{1,0:T(8,128)S(1)}, f32[136,128]{1,0:T(8,128)S(1)}, u32[]{:S(2)}, u32[]{:S(2)}) collective-permute-start(f32[136,128]{1,0:T(8,128)S(1)} %merge.1), channel_id=1, source_target_pairs={{0,6},{1,7},{2,4},{3,5},{4,2},{5,3},{6,0},{7,1},{8,14},{9,15},{10,... | collective-permute-start | bytes 208904 | tf_op jit(solution)/shard_map/ppermute | solution.py:315

commit v2 on v1

--- a/solution.py
+++ b/solution.py
@@ -52,7 +52,8 @@
     sub = lax.broadcasted_iota(jnp.int32, (SUBLANES, LANES), 0)
     table = jnp.zeros((SUBLANES, LANES), jnp.float32)
     for k in range(rows):
-        table = jnp.where(lane == k, jnp.where(sub == 0, lower[k], upper[k]), table)
+        table = jnp.where((lane == k) & (sub < 2), jnp.where(sub == 0, lower[k], upper[k]), table)
+        table = jnp.where((lane == rows - 1 - k) & (sub >= 2), jnp.where(sub == 2, upper[k], lower[k]), table)
     table_ref[...] = table
     for d in range(mode_count):
         for t in range(tiles):
@@ -106,19 +107,56 @@
                     blocks_ref[to, k, c, at : at + kx_count, :] = source_ref[k, c, lines, t * LANES : (t + 1) * LANES]
 
 
+def couplings(table, line, count):
+    return [table[line : line + 1, k : k + 1] for k in range(count)]
+
+
 def climb(spectral, num, den, near, far):
     product = near[0]
     for k in range(len(near)):
-        num = spectral * den + near[k] * num
+        step = near[k] * num
+        num = spectral * den + step
         before = den
-        den = num + far[k] * den
+        den = (spectral + far[k]) * den + step
         if k:
             product = product * near[k]
     return num, den, far[-1] * before, product
 
 
-def couplings(table, line, rows):
-    return [table[line : line + 1, k : k + 1] for k in range(rows)]
+def put_map(ref, lead, spectral, near, far):
+    total = spectral.shape[0]
+    num, den, tail = [near[0] + jnp.zeros_like(spectral), spectral], None, None
+    den = [num[0], spectral + far[0]]
+    tail = [jnp.zeros_like(spectral), far[0] + jnp.zeros_like(spectral)]
+    product = near[0]
+    for k in range(1, len(near)):
+        held = spectral + far[k]
+        if k == len(near) - 1:
+            tail = [far[k] * den[i] for i in range(2)]
+        step = [near[k] * num[i] for i in range(2)]
+        num = [spectral * den[i] + step[i] for i in range(2)]
+        den = [held * den[i] + step[i] for i in range(2)]
+        product = product * near[k]
+    for i, value in enumerate([*num, *den, *tail]):
+        ref[(*lead, slice(i * total, (i + 1) * total), slice(None))] = value
+    ref[(*lead, slice(6 * total, None), slice(None))] = jnp.broadcast_to(product, (SUBLANES, LANES))
+
+
+def apply_map(block, state, leave, entry):
+    grown, passed, *partial = state
+    inverse = 1.0 / (block(2) * grown + block(3))
+    ratio = block(6) * inverse
+    new = [leave[c] + ratio * (partial[c] + passed * entry[c]) for c in range(2)]
+    return ((block(0) * grown + block(1)) * inverse, (block(4) * grown + block(5)) * inverse, *new)
+
+
+def map_of(ref, lead, total):
+    def block(i):
+        if i == 6:
+            return ref[(*lead, slice(6 * total, 6 * total + 1), slice(None))]
+        return ref[(*lead, slice(i * total, (i + 1) * total), slice(None))]
+
+    return block
 
 
 def merge_kernel(sizes, spectral_ref, table_ref, ports_ref, taken_ref, side_ref, *rest):
@@ -147,36 +185,34 @@
     low_table = jnp.where(upside, pair_table, own_table)
     high_table = jnp.where(upside, own_table, pair_table)
     sub = lax.broadcasted_iota(jnp.int32, (SUBLANES, LANES), 0)
-    message_ref[4 * total :, :] = jnp.where(sub < 2, low_table, pltpu.roll(high_table, 2, 0))
+    lane = lax.broadcasted_iota(jnp.int32, (SUBLANES, LANES), 1)
+    ahead = jnp.where(sub < 2, low_table, high_table)
+    behind = jnp.where(sub < 2, high_table, low_table)
+    message_ref[4 * total :, :] = jnp.where(lane < rows, ahead, pltpu.roll(behind, rows, 1))
     spectral = spectral_ref[...]
     one = jnp.ones((total, LANES), jnp.float32)
     own = [gather(i, own_chunk) for i in range(4)]
     pair = [gather(i, pair_chunk) for i in range(4)]
     low = [jnp.where(upside, b, a) for a, b in zip(own, pair)]
     high = [jnp.where(upside, a, b) for a, b in zip(own, pair)]
-    low_l, low_u = couplings(low_table, 0, rows), couplings(low_table, 1, rows)
-    high_l, high_u = couplings(high_table, 0, rows), couplings(high_table, 1, rows)
 
     def store(i, value):
         message_ref[i * total : (i + 1) * total, :] = value
 
-    num, den, tail, _ = climb(spectral, one, one, low_l, low_u)
-    passed = tail / den
-    _, den_all, _, product = climb(spectral, num, den, high_l, high_u)
-    ratio = product * den / den_all
-    for c in range(2):
-        store(2 + c, high[2 + c] + ratio * (low[2 + c] + passed * high[c]))
-    num, den, tail, _ = climb(spectral, one, one, high_u[::-1], high_l[::-1])
-    passed = tail / den
-    _, den_all, _, product = climb(spectral, num, den, low_u[::-1], low_l[::-1])
-    ratio = product * den / den_all
-    for c in range(2):
-        store(c, low[c] + ratio * (high[c] + passed * low[2 + c]))
-
-
-def prepare_kernel(sizes, spectral_ref, table_ref, *rest):
-    rows, _, _, _, mode_count, _ = sizes
-    sources, (part_ref, low_ref, high_ref) = rest[:mode_count], rest[mode_count:]
+    for near_line, first, second, near_side, far_side in ((0, low_table, high_table, 0, 2), (2, high_table, low_table, 2, 0)):
+        lines = (near_line, near_line + 1)
+        num, den, tail, _ = climb(spectral, one, one, *(couplings(first, i, rows) for i in lines))
+        passed = tail / den
+        _, den_all, _, product = climb(spectral, num, den, *(couplings(second, i, rows) for i in lines))
+        ratio = product * den / den_all
+        before, after = (low, high) if near_line == 0 else (high, low)
+        for c in range(2):
+            store(far_side + c, after[far_side + c] + ratio * (before[far_side + c] + passed * after[near_side + c]))
+
+
+def prepare_kernel(sizes, spectral_ref, table_ref, side_ref, *rest):
+    rows, _, _, _, mode_count, height = sizes
+    sources, (part_ref, low_ref, high_ref, maps_ref) = rest[:mode_count], rest[mode_count:]
     spectral, table = spectral_ref[...], table_ref[...]
     lower, upper = couplings(table, 0, rows), couplings(table, 1, rows)
     grown = jnp.ones(spectral.shape, jnp.float32)
@@ -204,69 +240,82 @@
         for c in range(2):
             partial[c] = part_ref[k, c] + factor * partial[c]
             part_ref[k, c] = partial[c]
-
-
-def final_kernel(sizes, pairs, spectral_ref, table_ref, side_ref, part_ref, low_ref, high_ref, *rest):
+    pair_table = side_ref[2 * 4 * height :, :]
+    upside = lax.axis_index("gz") % 2 == 1
+    put_map(maps_ref, (0,), spectral, lower, upper)
+    put_map(maps_ref, (1,), spectral, couplings(table, 2, rows), couplings(table, 3, rows))
+    lines = jnp.where(upside, pair_table[0:2], pair_table[2:4])
+    put_map(maps_ref, (2,), spectral, couplings(lines, 0, rows), couplings(lines, 1, rows))
+
+
+def put_level(sizes, level, d, message_ref, spectral, ref, lead):
+    rows, total = sizes[0], spectral.shape[0]
+    table = message_ref[4 * total :, :]
+    lines = jnp.where((level ^ d) < level, table[0:2], table[2:4])
+    put_map(ref, lead, spectral, couplings(lines, 0, 2 * rows), couplings(lines, 1, 2 * rows))
+
+
+def level_kernel(sizes, levels, spectral_ref, *rest):
+    messages, maps_ref = rest[:-1], rest[-1]
+    level = lax.axis_index("gz") // 2
+    for i, d in enumerate(levels):
+        put_level(sizes, level, d, messages[i], spectral_ref[...], maps_ref, (d,))
+
+
+def final_kernel(sizes, pairs, late, spectral_ref, side_ref, part_ref, low_ref, high_ref, maps_ref, levels_ref, *rest):
     rows, _, _, _, mode_count, height = sizes
     chips = mode_count // 2
     total = mode_count * height
     port = 4 * height
     pair_refs, rest = rest[: chips - 1], rest[chips - 1 :]
     messages, rest = rest[: pairs - 1], rest[pairs - 1 :]
-    out_hbm, out_ref, level_ref, sems = rest
+    out_hbm, out_ref, late_ref, sems = rest
     me, partition = lax.axis_index("modes"), lax.axis_index("gz")
     upside, level = partition % 2 == 1, partition // 2
-    for d in range(1, pairs):
-        level_ref[level ^ d] = messages[d - 1][...]
-    spectral = spectral_ref[...]
+    put_level(sizes, level, late, messages[late - 1], spectral_ref[...], late_ref, ())
     one = jnp.ones((total, LANES), jnp.float32)
     zero = jnp.zeros((total, LANES), jnp.float32)
     start = (one, zero, zero, zero)
 
-    def enter(state, ports, entry, leave, near, far):
-        grown, passed, *partial = state
-        num, den, tail, product = climb(spectral, grown, one, near, far)
-        inverse = 1.0 / den
-        ratio = product * inverse
-        new = [ports(leave + c) + ratio * (partial[c] + passed * ports(entry + c)) for c in range(2)]
-        return (num * inverse, tail * inverse, *new)
-
-    def up(state, ports, table, blocks):
-        near = [v for b in blocks for v in couplings(table, 2 * b, rows)]
-        far = [v for b in blocks for v in couplings(table, 2 * b + 1, rows)]
-        return enter(state, ports, 0, 2, near, far)
-
-    def down(state, ports, table, blocks):
-        near = [v for b in blocks for v in couplings(table, 2 * b + 1, rows)]
-        far = [v for b in blocks for v in couplings(table, 2 * b, rows)]
-        return enter(state, ports, 2, 0, near[::-1], far[::-1])
-
-    def of_level(at):
-        return (lambda i: level_ref[at, i * total : (i + 1) * total, :]), level_ref[at, 4 * total :, :], (0, 1)
-
-    def pair_chunk(d, at):
-        at += (d % 2) * port
-        ref = side_ref if d < 2 else pair_refs[d // 2 - 1]
-        return ref[at : at + height, :]
-
-    def of_pair():
-        def ports(i):
-            return jnp.concatenate([pair_chunk(d, i * height) for d in range(mode_count)], axis=0)
-
-        return ports, side_ref[2 * port :, :], (0,)
-
-    def of_own():
-        return (lambda i: part_ref[0 if i < 2 else rows - 1, i % 2]), table_ref[...], (0,)
-
-    below, above = start, start
-    for at in range(pairs - 1):
-        below = lax.cond(at < level, lambda s, at=at: up(s, *of_level(at)), lambda s: s, below)
-    for at in range(pairs - 1, 0, -1):
-        above = lax.cond(at > level, lambda s, at=at: down(s, *of_level(at)), lambda s: s, above)
-    below, above = lax.cond(
-        upside, lambda b, a: (up(b, *of_pair()), a), lambda b, a: (b, down(a, *of_pair())), below, above
-    )
-    leaving_up, leaving_down = up(below, *of_own()), down(above, *of_own())
+    def cross(state, d, leave, entry):
+        ref = messages[d - 1]
+        ports = [ref[i * total : (i + 1) * total, :] for i in (leave, leave + 1, entry, entry + 1)]
+        block = map_of(late_ref, (), total) if d == late else map_of(levels_ref, (d,), total)
+        return apply_map(block, state, ports[:2], ports[2:])
+
+    def cross_levels(z, state, at):
+        leave, entry = (2, 0) if at < z else (0, 2)
+        return cross(state, z ^ at, leave, entry)
+
+    def at_level(z):
+        def states():
+            below, above = start, start
+            for at in range(z):
+                below = cross_levels(z, below, at)
+            for at in range(pairs - 1, z, -1):
+                above = cross_levels(z, above, at)
+            return below, above
+
+        return states
+
+    def pair_ports(i):
+        chunks = []
+        for d in range(mode_count):
+            at = i * height + (d % 2) * port
+            chunks.append((side_ref if d < 2 else pair_refs[d // 2 - 1])[at : at + height, :])
+        return jnp.concatenate(chunks, axis=0)
+
+    below, above = lax.switch(level, [at_level(z) for z in range(pairs)])
+    ports = [pair_ports(i) for i in range(4)]
+    near_state = [jnp.where(upside, b, a) for b, a in zip(below, above)]
+    leave = [jnp.where(upside, ports[2 + c], ports[c]) for c in range(2)]
+    entry = [jnp.where(upside, ports[c], ports[2 + c]) for c in range(2)]
+    crossed = apply_map(map_of(maps_ref, (2,), total), near_state, leave, entry)
+    below = [jnp.where(upside, new, old) for new, old in zip(crossed, below)]
+    above = [jnp.where(upside, old, new) for new, old in zip(crossed, above)]
+    own_first, own_last = [part_ref[0, c] for c in range(2)], [part_ref[rows - 1, c] for c in range(2)]
+    leaving_up = apply_map(map_of(maps_ref, (0,), total), below, own_last, own_first)
+    leaving_down = apply_map(map_of(maps_ref, (1,), total), above, own_first, own_last)
     inverse_up = 1.0 / (leaving_up[0] + leaving_up[1] * above[0])
     inverse_down = 1.0 / (leaving_down[0] + leaving_down[1] * below[0])
     under, over = [], []
@@ -290,6 +339,7 @@
         copy.wait()
 
 
+LIMIT = pltpu.CompilerParams(vmem_limit_bytes=16 << 20)
 VMEM = pl.BlockSpec(memory_space=pltpu.VMEM)
 ANY = pl.BlockSpec(memory_space=pl.ANY)
 
@@ -334,6 +384,7 @@
             chunk_sems,
         ],
         name="reduce",
+        compiler_params=LIMIT,
     )(coupling_below, coupling_above, eigen_stream, span, source_field)
     blocks = pl.pallas_call(
         functools.partial(regroup_kernel, sizes),
@@ -341,6 +392,7 @@
         in_specs=[VMEM],
         out_specs=VMEM,
         name="regroup",
+        compiler_params=LIMIT,
     )(*near(source))
 
     taken = move(ports[1], modes_by=1)
@@ -357,33 +409,52 @@
         in_specs=[VMEM] * (5 + 2 * (chips - 1)),
         out_specs=VMEM,
         name="merge",
+        compiler_params=LIMIT,
     )(*near(spectral, table, ports, taken, side, *own_parts, *pair_parts))
     messages = [move(message, level=d) for d in range(1, pairs)]
-    local = pl.pallas_call(
+    map_lines = 6 * total + SUBLANES
+    *local, maps = pl.pallas_call(
         functools.partial(prepare_kernel, sizes),
         out_shape=(
             pltpu.VMEM((rows, 2, total, LANES), f32),
             pltpu.VMEM((rows, total, LANES), f32),
             pltpu.VMEM((rows, total, LANES), f32),
+            pltpu.VMEM((3, map_lines, LANES), f32),
         ),
-        in_specs=[VMEM] * (2 + mode_count),
-        out_specs=(VMEM,) * 3,
+        in_specs=[VMEM] * (3 + mode_count),
+        out_specs=(VMEM,) * 4,
         name="prepare",
-    )(*near(spectral, table, *sources))
+        compiler_params=LIMIT,
+    )(*near(spectral, table, side, *sources))
+    late = late_level(pairs)
+    early = [d for d in range(1, pairs) if d != late]
+    level_maps = pl.pallas_call(
+        functools.partial(level_kernel, sizes, early),
+        out_shape=pltpu.VMEM((pairs, map_lines, LANES), f32),
+        in_specs=[VMEM] * (1 + len(early)),
+        out_specs=VMEM,
+        name="levels",
+        compiler_params=LIMIT,
+    )(*near(spectral, *(messages[d - 1] for d in early)))
     out = pl.pallas_call(
-        functools.partial(final_kernel, sizes, pairs),
+        functools.partial(final_kernel, sizes, pairs, late),
         out_shape=jax.ShapeDtypeStruct((rows, 2, mode_count, height, LANES), f32),
-        in_specs=[VMEM] * (6 + (chips - 1) + (pairs - 1)),
+        in_specs=[VMEM] * (7 + (chips - 1) + (pairs - 1)),
         out_specs=ANY,
         scratch_shapes=[
             pltpu.VMEM((rows, 2, mode_count, height, LANES), f32),
-            pltpu.VMEM((pairs, 4 * total + SUBLANES, LANES), f32),
+            pltpu.VMEM((map_lines, LANES), f32),
             chunk_sems,
         ],
         name="solve",
-    )(*near(spectral, table, side, *local, *pair_parts, *messages))
+        compiler_params=LIMIT,
+    )(*near(spectral, side, *local, maps, level_maps, *pair_parts, *messages))
     out = out.reshape(rows, 2, mode_count * tiles, kx_count, LANES).transpose(0, 1, 3, 2, 4)
     return out.reshape(rows, 2, kx_count, -1)
+
+
+def late_level(pairs):
+    return min(2, pairs - 1)
 
 
 def solution(mesh):

time: 27.1 us -> 31.6 us (1.17)
  local copies, waits for them, and re-layouts: 0.05 us -> 2.47 us
  waiting for transfers between devices: 9.85 us -> 11.1 us
  starting transfers between devices: 12.6 us -> 13.7 us
    unnamed x0 -> x10, local copies, waits for them, and re-layouts: none -> 2.42 us
    ppermute x10, waiting for transfers between devices: 9.85 us -> 11.1 us  [move(): return lax.ppermute(array, ('modes', 'gz'), links)]
    ppermute x10, starting transfers between devices: 12.6 us -> 13.7 us  [move(): return lax.ppermute(array, ('modes', 'gz'), links)]
    pallas_call x1 -> x2, Pallas kernels: 2.19 us -> 1.84 us  [the longest x1 1.32 us: solve(): pl.pallas_call(functools.partial(final_kernel, sizes, pairs, late), out_s...]
  transfers between devices with their start and end apart: 10 -> 10, of which waited for: 5 -> 5; matrix products, arithmetic and copies ran while one was open for 0% -> 0% of each run, Pallas kernels for 3% -> 5%
where the time goes in v2:
time: 31.6 us; the launch traced here: 31.4 us
  starting transfers between devices  13.7 us (43%)
  waiting for transfers between devices  11.1 us (35%)
  Pallas kernels  4 us (13%)
  local copies, waits for them, and re-layouts  2.47 us (8%)
    ppermute x10, starting transfers between devices, move(): return lax.ppermute(array, ('modes', 'gz'), links)  13.7 us
    ppermute x10, waiting for transfers between devices, move(): return lax.ppermute(array, ('modes', 'gz'), links)  11.1 us
    unnamed x10, local copies, waits for them, and re-layouts  2.42 us
    pallas_call x1, Pallas kernels, solve(): pl.pallas_call(functools.partial(final_kernel, sizes, pairs, late), out_s...  1.32 us
    pallas_call x1, Pallas kernels, solve(): pl.pallas_call(functools.partial(reduce_kernel, sizes), out_shape=(pltpu....  1 us
  transfers between devices with their start and end apart: 10, of which 5 were waited for; matrix products, arithmetic and copies ran while one was open for 0% of the time, Pallas kernels for 5%

profile of v2, /device:TPU:0, one launch (start us, length us, event | category | flops | bytes accessed | tf_op | source)
XLA Modules:
  0.0 31.4 jit_solution(794315103464201862)
XLA Ops:
  0.0 0.0 copy-start.2
  0.0 0.0 copy-start.3
  0.0 0.0 copy-start.4
  0.0 0.6 %copy-done.2 = f32[16]{0:T(128)S(1)} copy-done((f32[16]{0:T(128)S(1)}, f32[16]{0:T(128)}, u32[]{:S(2)}) %copy-start.2) | copy-done | bytes 88
  0.7 0.0 copy-done.3
  0.7 0.0 copy-done.4
  0.7 0.0 copy-start
  0.7 1.0 %copy-done = f32[16,2,8,512]{3,2,1,0:T(8,128)S(1)} copy-done((f32[16,2,8,512]{3,2,1,0:T(8,128)S(1)}, f32[16,2,8,512]{3,2,1,0:T(8,128)}, u32[]{:S(2)}) %copy-start) | copy-done | bytes 524312
  1.7 0.0 copy-start.1
  1.7 0.7 %copy-done.1 = f32[2048]{0:T(1024)S(1)} copy-done((f32[2048]{0:T(1024)S(1)}, f32[2048]{0:T(1024)}, u32[]{:S(2)}) %copy-start.1) | copy-done | bytes 8216
  2.4 1.0 %reduce.1 = (f32[2,2,32,128]{3,2,1,0:T(8,128)S(1)}, f32[8,128]{1,0:T(8,128)S(1)}, f32[32,128]{1,0:T(8,128)S(1)}, f32[16,2,8,512]{3,2,1,0:T(8,128)S(1)}) custom-call(f32[16]{0:T(128)S(1)} %copy-done.2, f32[16]{0:T(128)S(1)} %copy-done.3, f32[8]{0:T(128)S(1)} %copy-done.4, f32[16,128]{1,0:T(8,128)S(1)} %bitcast.24, f32[16,2,8,512]{3,2,1,0:T(8,128)S(1)} %copy-done), custom_call_target="tpu_custom_call" | custom-call | tf_op jit(solution)/shard_map/reduce/pallas_call | solution.py:368
  3.5 0.6 %collective-permute-start = (f32[2,32,128]{2,1,0:T(8,128)S(1)}, f32[2,32,128]{2,1,0:T(8,128)S(1)}, u32[]{:S(2)}, u32[]{:S(2)}) collective-permute-start(f32[2,32,128]{2,1,0:T(8,128)S(1)} %slice_bitcast_fusion.4), channel_id=1, source_target_pairs={{0,8},{1,9},{2,10},{3,11},{4,12},{5,13},{6,14},{7,15},{8,0},{9,1},... | collective-permute-start | bytes 98312 | tf_op jit(solution)/shard_map/ppermute | solution.py:365
  4.0 0.2 regroup.1
  4.2 0.1 collective-permute-start.2
  4.3 3.0 %collective-permute-start.3 = (f32[16,2,8,128]{3,2,1,0:T(8,128)S(1)}, f32[16,2,8,128]{3,2,1,0:T(8,128)S(1)}, u32[]{:S(2)}, u32[]{:S(2)}) collective-permute-start(f32[16,2,8,128]{3,2,1,0:T(8,128)S(1)} %get-tuple-element.22), channel_id=1, source_target_pairs={{0,16},{1,17},{2,18},{3,19},{4,20},{5,21},{6,22},{7,23},{8,24},{9,... | collective-permute-start | bytes 393224 | tf_op jit(solution)/shard_map/ppermute | solution.py:365
  7.3 0.0 collective-permute-start.4
  7.3 0.0 collective-permute-done.taken_ref
  7.4 1.5 %collective-permute-start.5 = (f32[64,128]{1,0:T(8,128)S(1)}, f32[64,128]{1,0:T(8,128)S(1)}, u32[]{:S(2)}, u32[]{:S(2)}) collective-permute-start(f32[64,128]{1,0:T(8,128)S(1)} %pad_maximum_fusion.1), channel_id=1, source_target_pairs={{0,16},{1,17},{2,18},{3,19},{4,20},{5,21},{6,22},{7,23},{8,24},{9,... | collective-permute-start | bytes 98312 | tf_op jit(solution)/shard_map/ppermute | solution.py:365
  8.8 1.5 %collective-permute-start.1 = (f32[72,128]{1,0:T(8,128)S(1)}, f32[72,128]{1,0:T(8,128)S(1)}, u32[]{:S(2)}, u32[]{:S(2)}) collective-permute-start(f32[72,128]{1,0:T(8,128)S(1)} %pad_maximum_fusion), channel_id=1, source_target_pairs={{0,1},{1,0},{2,3},{3,2},{4,5},{5,4},{6,7},{7,6},{8,9},{9,8},{10,11... | collective-permute-start | bytes 110600 | tf_op jit(solution)/shard_map/ppermute | solution.py:365
  10.3 4.2 %collective-permute-done.5.rest_0_ = f32[64,128]{1,0:T(8,128)S(1)} collective-permute-done((f32[64,128]{1,0:T(8,128)S(1)}, f32[64,128]{1,0:T(8,128)S(1)}, u32[]{:S(2)}, u32[]{:S(2)}) %collective-permute-start.5) | collective-permute-done | bytes 32800 | tf_op jit(solution)/shard_map/ppermute | solution.py:365
  14.6 2.7 %collective-permute-start.6 = (f32[64,128]{1,0:T(8,128)S(1)}, f32[64,128]{1,0:T(8,128)S(1)}, u32[]{:S(2)}, u32[]{:S(2)}) collective-permute-start(f32[64,128]{1,0:T(8,128)S(1)} %pad_maximum_fusion.1), channel_id=1, source_target_pairs={{0,17},{1,16},{2,19},{3,18},{4,21},{5,20},{6,23},{7,22},{8,25},{9,... | collective-permute-start | bytes 98312 | tf_op jit(solution)/shard_map/ppermute | solution.py:365
  17.2 2.1 %collective-permute-done.6.rest_1_.rest_0_ = f32[64,128]{1,0:T(8,128)S(1)} collective-permute-done((f32[64,128]{1,0:T(8,128)S(1)}, f32[64,128]{1,0:T(8,128)S(1)}, u32[]{:S(2)}, u32[]{:S(2)}) %collective-permute-start.6) | collective-permute-done | bytes 32800 | tf_op jit(solution)/shard_map/ppermute | solution.py:365
  19.4 0.0 collective-permute-done.1.side_ref
  19.4 0.4 %merge.1 = f32[136,128]{1,0:T(8,128)S(1)} custom-call(f32[32,128]{1,0:T(8,128)S(1)} %get-tuple-element.13.spectral_ref, f32[8,128]{1,0:T(8,128)S(1)} %get-tuple-element.15.table_ref, f32[2,2,32,128]{3,2,1,0:T(8,128)S(1)} %get-tuple-element.14.ports_ref, f32[2,32,128]{2,1,0:T(8,128)S(1)} %collective-permute-done.taken_ref, ...), custom_call_target="tpu_custom_call" | custom-call | tf_op jit(solution)/shard_map/merge/pallas_call | solution.py:406
  19.8 1.9 %collective-permute-start.7 = (f32[136,128]{1,0:T(8,128)S(1)}, f32[136,128]{1,0:T(8,128)S(1)}, u32[]{:S(2)}, u32[]{:S(2)}) collective-permute-start(f32[136,128]{1,0:T(8,128)S(1)} %merge.1), channel_id=1, source_target_pairs={{0,2},{1,3},{2,0},{3,1},{4,6},{5,7},{6,4},{7,5},{8,10},{9,11},{10,... | collective-permute-start | bytes 208904 | tf_op jit(solution)/shard_map/ppermute | solution.py:365
  21.6 2.5 %collective-permute-start.8 = (f32[136,128]{1,0:T(8,128)S(1)}, f32[136,128]{1,0:T(8,128)S(1)}, u32[]{:S(2)}, u32[]{:S(2)}) collective-permute-start(f32[136,128]{1,0:T(8,128)S(1)} %merge.1), channel_id=1, source_target_pairs={{0,6},{1,7},{2,4},{3,5},{4,2},{5,3},{6,0},{7,1},{8,14},{9,15},{10,... | collective-permute-start | bytes 208904 | tf_op jit(solution)/shard_map/ppermute | solution.py:365
  24.1 0.0 collective-permute-done.2.rest_1_
  24.1 0.1 collective-permute-start.9
  24.2 0.0 collective-permute-done.3.rest_2_
  24.2 0.0 collective-permute-done.4.rest_3_
  24.2 0.6 %prepare.1 = (f32[16,2,32,128]{3,2,1,0:T(8,128)S(1)}, f32[16,32,128]{2,1,0:T(8,128)S(1)}, f32[16,32,128]{2,1,0:T(8,128)S(1)}, f32[3,200,128]{2,1,0:T(8,128)S(1)}) custom-call(f32[32,128]{1,0:T(8,128)S(1)} %get-tuple-element.13.spectral_ref, f32[8,128]{1,0:T(8,128)S(1)} %get-tuple-element.15.table_ref, f32[72,128]{1,0:T(8,128)S(1)} %collective-permute-done.1.side_ref, ...), custom_call_target="tpu_custom_call" | custom-call | tf_op jit(solution)/shard_map/prepare/pallas_call | solution.py:416
  24.8 0.1 collective-permute-done.7.rest_0_.rest_1_
  24.9 2.9 %collective-permute-done.8.rest_1_.rest_3_ = f32[136,128]{1,0:T(8,128)S(1)} collective-permute-done((f32[136,128]{1,0:T(8,128)S(1)}, f32[136,128]{1,0:T(8,128)S(1)}, u32[]{:S(2)}, u32[]{:S(2)}) %collective-permute-start.8) | collective-permute-done | bytes 69664 | tf_op jit(solution)/shard_map/ppermute | solution.py:365
  27.8 0.5 %levels.1.levels_ref = f32[4,200,128]{2,1,0:T(8,128)S(1)} custom-call(f32[32,128]{1,0:T(8,128)S(1)} %get-tuple-element.13.spectral_ref, f32[136,128]{1,0:T(8,128)S(1)} %collective-permute-done.7.rest_0_.rest_1_, f32[136,128]{1,0:T(8,128)S(1)} %collective-permute-done.8.rest_1_.rest_3_), custom_call_target="tpu_custom_call" | custom-call | tf_op jit(solution)/shard_map/levels/pallas_call | solution.py:431
  28.3 1.7 %collective-permute-done.9.rest_2_ = f32[136,128]{1,0:T(8,128)S(1)} collective-permute-done((f32[136,128]{1,0:T(8,128)S(1)}, f32[136,128]{1,0:T(8,128)S(1)}, u32[]{:S(2)}, u32[]{:S(2)}) %collective-permute-start.9) | collective-permute-done | bytes 69664 | tf_op jit(solution)/shard_map/ppermute | solution.py:365
  30.1 1.3 %solve.1 = f32[16,2,4,8,128]{4,3,2,1,0:T(8,128)} custom-call(f32[32,128]{1,0:T(8,128)S(1)} %get-tuple-element.13.spectral_ref, f32[72,128]{1,0:T(8,128)S(1)} %collective-permute-done.1.side_ref, f32[16,2,32,128]{3,2,1,0:T(8,128)S(1)} %get-tuple-element.17.part_ref, f32[16,32,128]{2,1,0:T(8,128)S(1)} %get-tuple-element.18.low_ref, ...), custom_call_target="tpu_custom_call" | custom-call | tf_op jit(solution)/shard_map/solve/pallas_call | solution.py:439
  (6 shorter events, 0.1 us)
Async XLA Ops:
  0.0 0.7 %copy-start.2 = (f32[16]{0:T(128)S(1)}, f32[16]{0:T(128)}, u32[]{:S(2)}) copy-start(f32[16]{0:T(128)} %below_hbm.1) | copy-start | bytes 196
  0.0 0.7 %copy-start.3 = (f32[16]{0:T(128)S(1)}, f32[16]{0:T(128)}, u32[]{:S(2)}) copy-start(f32[16]{0:T(128)} %above_hbm.1) | copy-start | bytes 196
  0.0 0.7 %copy-start.4 = (f32[8]{0:T(128)S(1)}, f32[8]{0:T(128)}, u32[]{:S(2)}) copy-start(f32[8]{0:T(128)} %stream_hbm.1) | copy-start | bytes 100
  0.7 1.0 %copy-start = (f32[16,2,8,512]{3,2,1,0:T(8,128)S(1)}, f32[16,2,8,512]{3,2,1,0:T(8,128)}, u32[]{:S(2)}) copy-start(f32[16,2,8,512]{3,2,1,0:T(8,128)} %source_hbm.1) | copy-start | bytes 1572868
  1.7 0.7 %copy-start.1 = (f32[2048]{0:T(1024)S(1)}, f32[2048]{0:T(1024)}, u32[]{:S(2)}) copy-start(f32[2048]{0:T(1024)} %param.9) | copy-start | bytes 24580
  3.5 3.9 %collective-permute-start = (f32[2,32,128]{2,1,0:T(8,128)S(1)}, f32[2,32,128]{2,1,0:T(8,128)S(1)}, u32[]{:S(2)}, u32[]{:S(2)}) collective-permute-start(f32[2,32,128]{2,1,0:T(8,128)S(1)} %slice_bitcast_fusion.4), channel_id=1, source_target_pairs={{0,8},{1,9},{2,10},{3,11},{4,12},{5,13},{6,14},{7,15},{8,0},{9,1},... | collective-permute-start | bytes 98312 | tf_op jit(solution)/shard_map/ppermute | solution.py:365
  4.2 19.9 %collective-permute-start.2 = (f32[16,2,8,128]{3,2,1,0:T(8,128)S(1)}, f32[16,2,8,128]{3,2,1,0:T(8,128)S(1)}, u32[]{:S(2)}, u32[]{:S(2)}) collective-permute-start(f32[16,2,8,128]{3,2,1,0:T(8,128)S(1)} %get-tuple-element.23), channel_id=1, source_target_pairs={{0,8},{1,9},{2,10},{3,11},{4,12},{5,13},{6,14},{7,15},{8,0},{9,1},... | collective-permute-start | bytes 393224 | tf_op jit(solution)/shard_map/ppermute | solution.py:365
  4.3 19.9 %collective-permute-start.3 = (f32[16,2,8,128]{3,2,1,0:T(8,128)S(1)}, f32[16,2,8,128]{3,2,1,0:T(8,128)S(1)}, u32[]{:S(2)}, u32[]{:S(2)}) collective-permute-start(f32[16,2,8,128]{3,2,1,0:T(8,128)S(1)} %get-tuple-element.22), channel_id=1, source_target_pairs={{0,16},{1,17},{2,18},{3,19},{4,20},{5,21},{6,22},{7,23},{8,24},{9,... | collective-permute-start | bytes 393224 | tf_op jit(solution)/shard_map/ppermute | solution.py:365
  7.3 16.9 %collective-permute-start.4 = (f32[16,2,8,128]{3,2,1,0:T(8,128)S(1)}, f32[16,2,8,128]{3,2,1,0:T(8,128)S(1)}, u32[]{:S(2)}, u32[]{:S(2)}) collective-permute-start(f32[16,2,8,128]{3,2,1,0:T(8,128)S(1)} %get-tuple-element.21), channel_id=1, source_target_pairs={{0,24},{1,25},{2,26},{3,27},{4,28},{5,29},{6,30},{7,31},{8,16},{9,... | collective-permute-start | bytes 393224 | tf_op jit(solution)/shard_map/ppermute | solution.py:365
  7.4 7.2 %collective-permute-start.5 = (f32[64,128]{1,0:T(8,128)S(1)}, f32[64,128]{1,0:T(8,128)S(1)}, u32[]{:S(2)}, u32[]{:S(2)}) collective-permute-start(f32[64,128]{1,0:T(8,128)S(1)} %pad_maximum_fusion.1), channel_id=1, source_target_pairs={{0,16},{1,17},{2,18},{3,19},{4,20},{5,21},{6,22},{7,23},{8,24},{9,... | collective-permute-start | bytes 98312 | tf_op jit(solution)/shard_map/ppermute | solution.py:365
  8.8 10.5 %collective-permute-start.1 = (f32[72,128]{1,0:T(8,128)S(1)}, f32[72,128]{1,0:T(8,128)S(1)}, u32[]{:S(2)}, u32[]{:S(2)}) collective-permute-start(f32[72,128]{1,0:T(8,128)S(1)} %pad_maximum_fusion), channel_id=1, source_target_pairs={{0,1},{1,0},{2,3},{3,2},{4,5},{5,4},{6,7},{7,6},{8,9},{9,8},{10,11... | collective-permute-start | bytes 110600 | tf_op jit(solution)/shard_map/ppermute | solution.py:365
  14.6 4.8 %collective-permute-start.6 = (f32[64,128]{1,0:T(8,128)S(1)}, f32[64,128]{1,0:T(8,128)S(1)}, u32[]{:S(2)}, u32[]{:S(2)}) collective-permute-start(f32[64,128]{1,0:T(8,128)S(1)} %pad_maximum_fusion.1), channel_id=1, source_target_pairs={{0,17},{1,16},{2,19},{3,18},{4,21},{5,20},{6,23},{7,22},{8,25},{9,... | collective-permute-start | bytes 98312 | tf_op jit(solution)/shard_map/ppermute | solution.py:365
  19.8 5.1 %collective-permute-start.7 = (f32[136,128]{1,0:T(8,128)S(1)}, f32[136,128]{1,0:T(8,128)S(1)}, u32[]{:S(2)}, u32[]{:S(2)}) collective-permute-start(f32[136,128]{1,0:T(8,128)S(1)} %merge.1), channel_id=1, source_target_pairs={{0,2},{1,3},{2,0},{3,1},{4,6},{5,7},{6,4},{7,5},{8,10},{9,11},{10,... | collective-permute-start | bytes 208904 | tf_op jit(solution)/shard_map/ppermute | solution.py:365
  21.6 6.2 %collective-permute-start.8 = (f32[136,128]{1,0:T(8,128)S(1)}, f32[136,128]{1,0:T(8,128)S(1)}, u32[]{:S(2)}, u32[]{:S(2)}) collective-permute-start(f32[136,128]{1,0:T(8,128)S(1)} %merge.1), channel_id=1, source_target_pairs={{0,6},{1,7},{2,4},{3,5},{4,2},{5,3},{6,0},{7,1},{8,14},{9,15},{10,... | collective-permute-start | bytes 208904 | tf_op jit(solution)/shard_map/ppermute | solution.py:365
  24.1 6.0 %collective-permute-start.9 = (f32[136,128]{1,0:T(8,128)S(1)}, f32[136,128]{1,0:T(8,128)S(1)}, u32[]{:S(2)}, u32[]{:S(2)}) collective-permute-start(f32[136,128]{1,0:T(8,128)S(1)} %merge.1), channel_id=1, source_target_pairs={{0,4},{1,5},{2,6},{3,7},{4,0},{5,1},{6,2},{7,3},{8,12},{9,13},{10,... | collective-permute-start | bytes 208904 | tf_op jit(solution)/shard_map/ppermute | solution.py:365

commit v3 on v2

--- a/solution.py
+++ b/solution.py
@@ -272,7 +272,8 @@
     out_hbm, out_ref, late_ref, sems = rest
     me, partition = lax.axis_index("modes"), lax.axis_index("gz")
     upside, level = partition % 2 == 1, partition // 2
-    put_level(sizes, level, late, messages[late - 1], spectral_ref[...], late_ref, ())
+    for i, d in enumerate(late):
+        put_level(sizes, level, d, messages[d - 1], spectral_ref[...], late_ref, (i,))
     one = jnp.ones((total, LANES), jnp.float32)
     zero = jnp.zeros((total, LANES), jnp.float32)
     start = (one, zero, zero, zero)
@@ -280,7 +281,7 @@
     def cross(state, d, leave, entry):
         ref = messages[d - 1]
         ports = [ref[i * total : (i + 1) * total, :] for i in (leave, leave + 1, entry, entry + 1)]
-        block = map_of(late_ref, (), total) if d == late else map_of(levels_ref, (d,), total)
+        block = map_of(late_ref, (late.index(d),), total) if d in late else map_of(levels_ref, (d,), total)
         return apply_map(block, state, ports[:2], ports[2:])
 
     def cross_levels(z, state, at):
@@ -384,7 +385,6 @@
             chunk_sems,
         ],
         name="reduce",
-        compiler_params=LIMIT,
     )(coupling_below, coupling_above, eigen_stream, span, source_field)
     blocks = pl.pallas_call(
         functools.partial(regroup_kernel, sizes),
@@ -392,7 +392,6 @@
         in_specs=[VMEM],
         out_specs=VMEM,
         name="regroup",
-        compiler_params=LIMIT,
     )(*near(source))
 
     taken = move(ports[1], modes_by=1)
@@ -409,7 +408,6 @@
         in_specs=[VMEM] * (5 + 2 * (chips - 1)),
         out_specs=VMEM,
         name="merge",
-        compiler_params=LIMIT,
     )(*near(spectral, table, ports, taken, side, *own_parts, *pair_parts))
     messages = [move(message, level=d) for d in range(1, pairs)]
     map_lines = 6 * total + SUBLANES
@@ -424,10 +422,9 @@
         in_specs=[VMEM] * (3 + mode_count),
         out_specs=(VMEM,) * 4,
         name="prepare",
-        compiler_params=LIMIT,
     )(*near(spectral, table, side, *sources))
-    late = late_level(pairs)
-    early = [d for d in range(1, pairs) if d != late]
+    late = late_levels(pairs)
+    early = [d for d in range(1, pairs) if d not in late]
     level_maps = pl.pallas_call(
         functools.partial(level_kernel, sizes, early),
         out_shape=pltpu.VMEM((pairs, map_lines, LANES), f32),
@@ -443,7 +440,7 @@
         out_specs=ANY,
         scratch_shapes=[
             pltpu.VMEM((rows, 2, mode_count, height, LANES), f32),
-            pltpu.VMEM((map_lines, LANES), f32),
+            pltpu.VMEM((len(late), map_lines, LANES), f32),
             chunk_sems,
         ],
         name="solve",
@@ -453,8 +450,8 @@
     return out.reshape(rows, 2, kx_count, -1)
 
 
-def late_level(pairs):
-    return min(2, pairs - 1)
+def late_levels(pairs):
+    return [d for d in (1, 2) if d < pairs]
 
 
 def solution(mesh):

time: 31.6 us -> 28.4 us (0.90)
  local copies, waits for them, and re-layouts: 2.47 us -> 0.05 us
  waiting for transfers between devices: 11.1 us -> 10.1 us
    unnamed x10 -> x0, local copies, waits for them, and re-layouts: 2.42 us -> none
    ppermute x10, waiting for transfers between devices: 11.1 us -> 10.1 us  [move(): return lax.ppermute(array, ('modes', 'gz'), links)]
  transfers between devices with their start and end apart: 10 -> 10, of which waited for: 5 -> 4; matrix products, arithmetic and copies ran while one was open for 0% -> 0% of each run, Pallas kernels for 5% -> 5%
where the time goes in v3:
time: 28.4 us; the launch traced here: 28.3 us
  starting transfers between devices  13.8 us (49%)
  waiting for transfers between devices  10.1 us (36%)
  Pallas kernels  4.24 us (15%)
    ppermute x10, starting transfers between devices, move(): return lax.ppermute(array, ('modes', 'gz'), links)  13.8 us
    ppermute x10, waiting for transfers between devices, move(): return lax.ppermute(array, ('modes', 'gz'), links)  10.1 us
    pallas_call x1, Pallas kernels, solve(): pl.pallas_call(functools.partial(final_kernel, sizes, pairs, late), out_s...  1.54 us
    pallas_call x1, Pallas kernels, solve(): pl.pallas_call(functools.partial(reduce_kernel, sizes), out_shape=(pltpu....  1.24 us
    pallas_call x1, Pallas kernels, solve(): pl.pallas_call(functools.partial(prepare_kernel, sizes), out_shape=(pltpu...  0.59 us
  transfers between devices with their start and end apart: 10, of which 4 were waited for; matrix products, arithmetic and copies ran while one was open for 0% of the time, Pallas kernels for 5%

profile of v3, /device:TPU:0, one launch (start us, length us, event | category | flops | bytes accessed | tf_op | source)
XLA Modules:
  0.0 28.3 jit_solution(18321615534847902252)
XLA Ops:
  0.0 1.2 %reduce.1 = (f32[2,2,32,128]{3,2,1,0:T(8,128)S(1)}, f32[8,128]{1,0:T(8,128)S(1)}, f32[32,128]{1,0:T(8,128)S(1)}, f32[16,2,8,512]{3,2,1,0:T(8,128)S(1)}) custom-call(f32[16]{0:T(128)} %below_hbm.1, f32[16]{0:T(128)} %above_hbm.1, f32[8]{0:T(128)} %stream_hbm.1, f32[16,128]{1,0:T(8,128)} %bitcast.24, f32[16,2,8,512]{3,2,1,0:T(8,128)} %source_hbm.1), custom_call_target="tpu_custom_call" | custom-call | tf_op jit(solution)/shard_map/reduce/pallas_call | solution.py:369
  1.3 0.6 %collective-permute-start = (f32[2,32,128]{2,1,0:T(8,128)S(1)}, f32[2,32,128]{2,1,0:T(8,128)S(1)}, u32[]{:S(2)}, u32[]{:S(2)}) collective-permute-start(f32[2,32,128]{2,1,0:T(8,128)S(1)} %slice_bitcast_fusion.4), channel_id=1, source_target_pairs={{0,8},{1,9},{2,10},{3,11},{4,12},{5,13},{6,14},{7,15},{8,0},{9,1},... | collective-permute-start | bytes 98312 | tf_op jit(solution)/shard_map/ppermute | solution.py:366
  1.8 0.2 regroup.1
  2.0 0.1 collective-permute-start.2
  2.1 3.0 %collective-permute-start.3 = (f32[16,2,8,128]{3,2,1,0:T(8,128)S(1)}, f32[16,2,8,128]{3,2,1,0:T(8,128)S(1)}, u32[]{:S(2)}, u32[]{:S(2)}) collective-permute-start(f32[16,2,8,128]{3,2,1,0:T(8,128)S(1)} %get-tuple-element.22), channel_id=1, source_target_pairs={{0,16},{1,17},{2,18},{3,19},{4,20},{5,21},{6,22},{7,23},{8,24},{9,... | collective-permute-start | bytes 393224 | tf_op jit(solution)/shard_map/ppermute | solution.py:366
  5.1 0.0 collective-permute-start.4
  5.1 0.0 collective-permute-done.taken_ref
  5.2 1.5 %collective-permute-start.5 = (f32[64,128]{1,0:T(8,128)S(1)}, f32[64,128]{1,0:T(8,128)S(1)}, u32[]{:S(2)}, u32[]{:S(2)}) collective-permute-start(f32[64,128]{1,0:T(8,128)S(1)} %pad_maximum_fusion.1), channel_id=1, source_target_pairs={{0,16},{1,17},{2,18},{3,19},{4,20},{5,21},{6,22},{7,23},{8,24},{9,... | collective-permute-start | bytes 98312 | tf_op jit(solution)/shard_map/ppermute | solution.py:366
  6.7 1.5 %collective-permute-start.1 = (f32[72,128]{1,0:T(8,128)S(1)}, f32[72,128]{1,0:T(8,128)S(1)}, u32[]{:S(2)}, u32[]{:S(2)}) collective-permute-start(f32[72,128]{1,0:T(8,128)S(1)} %pad_maximum_fusion), channel_id=1, source_target_pairs={{0,1},{1,0},{2,3},{3,2},{4,5},{5,4},{6,7},{7,6},{8,9},{9,8},{10,11... | collective-permute-start | bytes 110600 | tf_op jit(solution)/shard_map/ppermute | solution.py:366
  8.1 4.2 %collective-permute-done.5.rest_0_ = f32[64,128]{1,0:T(8,128)S(1)} collective-permute-done((f32[64,128]{1,0:T(8,128)S(1)}, f32[64,128]{1,0:T(8,128)S(1)}, u32[]{:S(2)}, u32[]{:S(2)}) %collective-permute-start.5) | collective-permute-done | bytes 32800 | tf_op jit(solution)/shard_map/ppermute | solution.py:366
  12.4 2.7 %collective-permute-start.6 = (f32[64,128]{1,0:T(8,128)S(1)}, f32[64,128]{1,0:T(8,128)S(1)}, u32[]{:S(2)}, u32[]{:S(2)}) collective-permute-start(f32[64,128]{1,0:T(8,128)S(1)} %pad_maximum_fusion.1), channel_id=1, source_target_pairs={{0,17},{1,16},{2,19},{3,18},{4,21},{5,20},{6,23},{7,22},{8,25},{9,... | collective-permute-start | bytes 98312 | tf_op jit(solution)/shard_map/ppermute | solution.py:366
  15.0 2.1 %collective-permute-done.6.rest_1_.rest_0_ = f32[64,128]{1,0:T(8,128)S(1)} collective-permute-done((f32[64,128]{1,0:T(8,128)S(1)}, f32[64,128]{1,0:T(8,128)S(1)}, u32[]{:S(2)}, u32[]{:S(2)}) %collective-permute-start.6) | collective-permute-done | bytes 32800 | tf_op jit(solution)/shard_map/ppermute | solution.py:366
  17.2 0.0 collective-permute-done.1.side_ref
  17.2 0.4 %merge.1 = f32[136,128]{1,0:T(8,128)S(1)} custom-call(f32[32,128]{1,0:T(8,128)S(1)} %get-tuple-element.13.spectral_ref, f32[8,128]{1,0:T(8,128)S(1)} %get-tuple-element.15.table_ref, f32[2,2,32,128]{3,2,1,0:T(8,128)S(1)} %get-tuple-element.14.ports_ref, f32[2,32,128]{2,1,0:T(8,128)S(1)} %collective-permute-done.taken_ref, ...), custom_call_target="tpu_custom_call" | custom-call | tf_op jit(solution)/shard_map/merge/pallas_call | solution.py:405
  17.6 3.9 %collective-permute-start.7 = (f32[136,128]{1,0:T(8,128)S(1)}, f32[136,128]{1,0:T(8,128)S(1)}, u32[]{:S(2)}, u32[]{:S(2)}) collective-permute-start(f32[136,128]{1,0:T(8,128)S(1)} %merge.1), channel_id=1, source_target_pairs={{0,6},{1,7},{2,4},{3,5},{4,2},{5,3},{6,0},{7,1},{8,14},{9,15},{10,... | collective-permute-start | bytes 208904 | tf_op jit(solution)/shard_map/ppermute | solution.py:366
  21.5 0.0 collective-permute-start.8
  21.5 0.0 collective-permute-done.2.rest_1_
  21.5 0.6 %collective-permute-start.9 = (f32[136,128]{1,0:T(8,128)S(1)}, f32[136,128]{1,0:T(8,128)S(1)}, u32[]{:S(2)}, u32[]{:S(2)}) collective-permute-start(f32[136,128]{1,0:T(8,128)S(1)} %merge.1), channel_id=1, source_target_pairs={{0,4},{1,5},{2,6},{3,7},{4,0},{5,1},{6,2},{7,3},{8,12},{9,13},{10,... | collective-permute-start | bytes 208904 | tf_op jit(solution)/shard_map/ppermute | solution.py:366
  22.1 0.0 collective-permute-done.3.rest_2_
  22.1 0.0 collective-permute-done.4.rest_3_
  22.1 0.6 %prepare.1 = (f32[16,2,32,128]{3,2,1,0:T(8,128)S(1)}, f32[16,32,128]{2,1,0:T(8,128)S(1)}, f32[16,32,128]{2,1,0:T(8,128)S(1)}, f32[3,200,128]{2,1,0:T(8,128)S(1)}) custom-call(f32[32,128]{1,0:T(8,128)S(1)} %get-tuple-element.13.spectral_ref, f32[8,128]{1,0:T(8,128)S(1)} %get-tuple-element.15.table_ref, f32[72,128]{1,0:T(8,128)S(1)} %collective-permute-done.1.side_ref, ...), custom_call_target="tpu_custom_call" | custom-call | tf_op jit(solution)/shard_map/prepare/pallas_call | solution.py:414
  22.7 1.2 %collective-permute-done.7.rest_0_.rest_3_ = f32[136,128]{1,0:T(8,128)S(1)} collective-permute-done((f32[136,128]{1,0:T(8,128)S(1)}, f32[136,128]{1,0:T(8,128)S(1)}, u32[]{:S(2)}, u32[]{:S(2)}) %collective-permute-start.7) | collective-permute-done | bytes 69664 | tf_op jit(solution)/shard_map/ppermute | solution.py:366
  24.0 0.3 %levels.1.levels_ref = f32[4,200,128]{2,1,0:T(8,128)S(1)} custom-call(f32[32,128]{1,0:T(8,128)S(1)} %get-tuple-element.13.spectral_ref, f32[136,128]{1,0:T(8,128)S(1)} %collective-permute-done.7.rest_0_.rest_3_), custom_call_target="tpu_custom_call" | custom-call | tf_op jit(solution)/shard_map/levels/pallas_call | solution.py:428
  24.3 2.4 %collective-permute-done.8.rest_1_ = f32[136,128]{1,0:T(8,128)S(1)} collective-permute-done((f32[136,128]{1,0:T(8,128)S(1)}, f32[136,128]{1,0:T(8,128)S(1)}, u32[]{:S(2)}, u32[]{:S(2)}) %collective-permute-start.8) | collective-permute-done | bytes 69664 | tf_op jit(solution)/shard_map/ppermute | solution.py:366
  26.7 0.0 collective-permute-done.9.rest_2_
  26.7 1.5 %solve.1 = f32[16,2,4,8,128]{4,3,2,1,0:T(8,128)} custom-call(f32[32,128]{1,0:T(8,128)S(1)} %get-tuple-element.13.spectral_ref, f32[72,128]{1,0:T(8,128)S(1)} %collective-permute-done.1.side_ref, f32[16,2,32,128]{3,2,1,0:T(8,128)S(1)} %get-tuple-element.17.part_ref, f32[16,32,128]{2,1,0:T(8,128)S(1)} %get-tuple-element.18.low_ref, ...), custom_call_target="tpu_custom_call" | custom-call | tf_op jit(solution)/shard_map/solve/pallas_call | solution.py:436
  (6 shorter events, 0.1 us)
Async XLA Ops:
  1.3 3.9 %collective-permute-start = (f32[2,32,128]{2,1,0:T(8,128)S(1)}, f32[2,32,128]{2,1,0:T(8,128)S(1)}, u32[]{:S(2)}, u32[]{:S(2)}) collective-permute-start(f32[2,32,128]{2,1,0:T(8,128)S(1)} %slice_bitcast_fusion.4), channel_id=1, source_target_pairs={{0,8},{1,9},{2,10},{3,11},{4,12},{5,13},{6,14},{7,15},{8,0},{9,1},... | collective-permute-start | bytes 98312 | tf_op jit(solution)/shard_map/ppermute | solution.py:366
  2.0 19.4 %collective-permute-start.2 = (f32[16,2,8,128]{3,2,1,0:T(8,128)S(1)}, f32[16,2,8,128]{3,2,1,0:T(8,128)S(1)}, u32[]{:S(2)}, u32[]{:S(2)}) collective-permute-start(f32[16,2,8,128]{3,2,1,0:T(8,128)S(1)} %get-tuple-element.23), channel_id=1, source_target_pairs={{0,8},{1,9},{2,10},{3,11},{4,12},{5,13},{6,14},{7,15},{8,0},{9,1},... | collective-permute-start | bytes 393224 | tf_op jit(solution)/shard_map/ppermute | solution.py:366
  2.1 20.0 %collective-permute-start.3 = (f32[16,2,8,128]{3,2,1,0:T(8,128)S(1)}, f32[16,2,8,128]{3,2,1,0:T(8,128)S(1)}, u32[]{:S(2)}, u32[]{:S(2)}) collective-permute-start(f32[16,2,8,128]{3,2,1,0:T(8,128)S(1)} %get-tuple-element.22), channel_id=1, source_target_pairs={{0,16},{1,17},{2,18},{3,19},{4,20},{5,21},{6,22},{7,23},{8,24},{9,... | collective-permute-start | bytes 393224 | tf_op jit(solution)/shard_map/ppermute | solution.py:366
  5.1 17.0 %collective-permute-start.4 = (f32[16,2,8,128]{3,2,1,0:T(8,128)S(1)}, f32[16,2,8,128]{3,2,1,0:T(8,128)S(1)}, u32[]{:S(2)}, u32[]{:S(2)}) collective-permute-start(f32[16,2,8,128]{3,2,1,0:T(8,128)S(1)} %get-tuple-element.21), channel_id=1, source_target_pairs={{0,24},{1,25},{2,26},{3,27},{4,28},{5,29},{6,30},{7,31},{8,16},{9,... | collective-permute-start | bytes 393224 | tf_op jit(solution)/shard_map/ppermute | solution.py:366
  5.2 7.2 %collective-permute-start.5 = (f32[64,128]{1,0:T(8,128)S(1)}, f32[64,128]{1,0:T(8,128)S(1)}, u32[]{:S(2)}, u32[]{:S(2)}) collective-permute-start(f32[64,128]{1,0:T(8,128)S(1)} %pad_maximum_fusion.1), channel_id=1, source_target_pairs={{0,16},{1,17},{2,18},{3,19},{4,20},{5,21},{6,22},{7,23},{8,24},{9,... | collective-permute-start | bytes 98312 | tf_op jit(solution)/shard_map/ppermute | solution.py:366
  6.7 10.5 %collective-permute-start.1 = (f32[72,128]{1,0:T(8,128)S(1)}, f32[72,128]{1,0:T(8,128)S(1)}, u32[]{:S(2)}, u32[]{:S(2)}) collective-permute-start(f32[72,128]{1,0:T(8,128)S(1)} %pad_maximum_fusion), channel_id=1, source_target_pairs={{0,1},{1,0},{2,3},{3,2},{4,5},{5,4},{6,7},{7,6},{8,9},{9,8},{10,11... | collective-permute-start | bytes 110600 | tf_op jit(solution)/shard_map/ppermute | solution.py:366
  12.4 4.8 %collective-permute-start.6 = (f32[64,128]{1,0:T(8,128)S(1)}, f32[64,128]{1,0:T(8,128)S(1)}, u32[]{:S(2)}, u32[]{:S(2)}) collective-permute-start(f32[64,128]{1,0:T(8,128)S(1)} %pad_maximum_fusion.1), channel_id=1, source_target_pairs={{0,17},{1,16},{2,19},{3,18},{4,21},{5,20},{6,23},{7,22},{8,25},{9,... | collective-permute-start | bytes 98312 | tf_op jit(solution)/shard_map/ppermute | solution.py:366
  17.6 6.4 %collective-permute-start.7 = (f32[136,128]{1,0:T(8,128)S(1)}, f32[136,128]{1,0:T(8,128)S(1)}, u32[]{:S(2)}, u32[]{:S(2)}) collective-permute-start(f32[136,128]{1,0:T(8,128)S(1)} %merge.1), channel_id=1, source_target_pairs={{0,6},{1,7},{2,4},{3,5},{4,2},{5,3},{6,0},{7,1},{8,14},{9,15},{10,... | collective-permute-start | bytes 208904 | tf_op jit(solution)/shard_map/ppermute | solution.py:366
  21.5 5.2 %collective-permute-start.8 = (f32[136,128]{1,0:T(8,128)S(1)}, f32[136,128]{1,0:T(8,128)S(1)}, u32[]{:S(2)}, u32[]{:S(2)}) collective-permute-start(f32[136,128]{1,0:T(8,128)S(1)} %merge.1), channel_id=1, source_target_pairs={{0,2},{1,3},{2,0},{3,1},{4,6},{5,7},{6,4},{7,5},{8,10},{9,11},{10,... | collective-permute-start | bytes 208904 | tf_op jit(solution)/shard_map/ppermute | solution.py:366
  21.5 5.2 %collective-permute-start.9 = (f32[136,128]{1,0:T(8,128)S(1)}, f32[136,128]{1,0:T(8,128)S(1)}, u32[]{:S(2)}, u32[]{:S(2)}) collective-permute-start(f32[136,128]{1,0:T(8,128)S(1)} %merge.1), channel_id=1, source_target_pairs={{0,4},{1,5},{2,6},{3,7},{4,0},{5,1},{6,2},{7,3},{8,12},{9,13},{10,... | collective-permute-start | bytes 208904 | tf_op jit(solution)/shard_map/ppermute | solution.py:366

commit v4 on v2

--- a/solution.py
+++ b/solution.py
@@ -19,8 +19,8 @@
     return rows, kx_total, kx_count, tiles, mode_count, kx_count * tiles
 
 
-def chunks_of(rows):
-    size = rows // 4 if rows % 4 == 0 else rows
+def chunks_of(rows, count=4):
+    size = rows // count if rows % count == 0 else rows
     return [(first, size) for first in range(0, rows, size)]
 
 
@@ -123,11 +123,15 @@
     return num, den, far[-1] * before, product
 
 
+MAP_PARTS = 7
+
+
 def put_map(ref, lead, spectral, near, far):
     total = spectral.shape[0]
-    num, den, tail = [near[0] + jnp.zeros_like(spectral), spectral], None, None
+    zero = jnp.zeros_like(spectral)
+    num = [near[0] + zero, spectral]
     den = [num[0], spectral + far[0]]
-    tail = [jnp.zeros_like(spectral), far[0] + jnp.zeros_like(spectral)]
+    tail = [zero, far[0] + zero]
     product = near[0]
     for k in range(1, len(near)):
         held = spectral + far[k]
@@ -137,26 +141,20 @@
         num = [spectral * den[i] + step[i] for i in range(2)]
         den = [held * den[i] + step[i] for i in range(2)]
         product = product * near[k]
-    for i, value in enumerate([*num, *den, *tail]):
-        ref[(*lead, slice(i * total, (i + 1) * total), slice(None))] = value
-    ref[(*lead, slice(6 * total, None), slice(None))] = jnp.broadcast_to(product, (SUBLANES, LANES))
+    scale = 1.0 / (den[0] + den[1])
+    for i, value in enumerate([*num, *den, *tail, product]):
+        ref[(*lead, slice(i * total, (i + 1) * total), slice(None))] = value * scale
 
 
 def apply_map(block, state, leave, entry):
-    grown, passed, *partial = state
-    inverse = 1.0 / (block(2) * grown + block(3))
-    ratio = block(6) * inverse
-    new = [leave[c] + ratio * (partial[c] + passed * entry[c]) for c in range(2)]
-    return ((block(0) * grown + block(1)) * inverse, (block(4) * grown + block(5)) * inverse, *new)
+    num, den, tail, *partial = state
+    new_den = block(2) * num + block(3) * den
+    new = [leave[c] * new_den + block(6) * (partial[c] + tail * entry[c]) for c in range(2)]
+    return (block(0) * num + block(1) * den, new_den, block(4) * num + block(5) * den, *new)
 
 
 def map_of(ref, lead, total):
-    def block(i):
-        if i == 6:
-            return ref[(*lead, slice(6 * total, 6 * total + 1), slice(None))]
-        return ref[(*lead, slice(i * total, (i + 1) * total), slice(None))]
-
-    return block
+    return lambda i: ref[(*lead, slice(i * total, (i + 1) * total), slice(None))]
 
 
 def merge_kernel(sizes, spectral_ref, table_ref, ports_ref, taken_ref, side_ref, *rest):
@@ -255,33 +253,30 @@
     put_map(ref, lead, spectral, couplings(lines, 0, 2 * rows), couplings(lines, 1, 2 * rows))
 
 
-def level_kernel(sizes, levels, spectral_ref, *rest):
-    messages, maps_ref = rest[:-1], rest[-1]
-    level = lax.axis_index("gz") // 2
-    for i, d in enumerate(levels):
-        put_level(sizes, level, d, messages[i], spectral_ref[...], maps_ref, (d,))
-
-
-def final_kernel(sizes, pairs, late, spectral_ref, side_ref, part_ref, low_ref, high_ref, maps_ref, levels_ref, *rest):
+def level_kernel(sizes, d, spectral_ref, message_ref, map_ref):
+    put_level(sizes, lax.axis_index("gz") // 2, d, message_ref, spectral_ref[...], map_ref, ())
+
+
+def final_kernel(sizes, pairs, late, spectral_ref, side_ref, part_ref, low_ref, high_ref, maps_ref, *rest):
     rows, _, _, _, mode_count, height = sizes
     chips = mode_count // 2
     total = mode_count * height
     port = 4 * height
     pair_refs, rest = rest[: chips - 1], rest[chips - 1 :]
     messages, rest = rest[: pairs - 1], rest[pairs - 1 :]
-    out_hbm, out_ref, late_ref, sems = rest
+    level_maps, (out_hbm, out_ref, late_ref, sems) = list(rest[: pairs - 2]), rest[pairs - 2 :]
+    level_maps.insert(late - 1, late_ref)
     me, partition = lax.axis_index("modes"), lax.axis_index("gz")
     upside, level = partition % 2 == 1, partition // 2
     put_level(sizes, level, late, messages[late - 1], spectral_ref[...], late_ref, ())
     one = jnp.ones((total, LANES), jnp.float32)
     zero = jnp.zeros((total, LANES), jnp.float32)
-    start = (one, zero, zero, zero)
+    start = (one, one, zero, zero, zero)
 
     def cross(state, d, leave, entry):
         ref = messages[d - 1]
         ports = [ref[i * total : (i + 1) * total, :] for i in (leave, leave + 1, entry, entry + 1)]
-        block = map_of(late_ref, (), total) if d == late else map_of(levels_ref, (d,), total)
-        return apply_map(block, state, ports[:2], ports[2:])
+        return apply_map(map_of(level_maps[d - 1], (), total), state, ports[:2], ports[2:])
 
     def cross_levels(z, state, at):
         leave, entry = (2, 0) if at < z else (0, 2)
@@ -316,14 +311,15 @@
     own_first, own_last = [part_ref[0, c] for c in range(2)], [part_ref[rows - 1, c] for c in range(2)]
     leaving_up = apply_map(map_of(maps_ref, (0,), total), below, own_last, own_first)
     leaving_down = apply_map(map_of(maps_ref, (1,), total), above, own_first, own_last)
-    inverse_up = 1.0 / (leaving_up[0] + leaving_up[1] * above[0])
-    inverse_down = 1.0 / (leaving_down[0] + leaving_down[1] * below[0])
+    inverse_up = 1.0 / (leaving_up[0] * above[1] + leaving_up[2] * above[0])
+    inverse_down = 1.0 / (leaving_down[0] * below[1] + leaving_down[2] * below[0])
+    inverse_below, inverse_above = 1.0 / below[1], 1.0 / above[1]
     under, over = [], []
-    for c in range(2, 4):
-        last = (leaving_up[c] + leaving_up[1] * above[c]) * inverse_up
-        over.append(above[c] + above[1] * last)
-        first = (leaving_down[c] + leaving_down[1] * below[c]) * inverse_down
-        under.append(below[c] + below[1] * first)
+    for c in range(3, 5):
+        last = (leaving_up[c] * above[1] + leaving_up[2] * above[c]) * inverse_up
+        over.append((above[c] + above[2] * last) * inverse_above)
+        first = (leaving_down[c] * below[1] + leaving_down[2] * below[c]) * inverse_down
+        under.append((below[c] + below[2] * first) * inverse_below)
     copies = []
     for i, (first, size) in enumerate(chunks_of(rows)):
         for k in range(first, first + size):
@@ -384,7 +380,6 @@
             chunk_sems,
         ],
         name="reduce",
-        compiler_params=LIMIT,
     )(coupling_below, coupling_above, eigen_stream, span, source_field)
     blocks = pl.pallas_call(
         functools.partial(regroup_kernel, sizes),
@@ -392,7 +387,6 @@
         in_specs=[VMEM],
         out_specs=VMEM,
         name="regroup",
-        compiler_params=LIMIT,
     )(*near(source))
 
     taken = move(ports[1], modes_by=1)
@@ -409,10 +403,9 @@
         in_specs=[VMEM] * (5 + 2 * (chips - 1)),
         out_specs=VMEM,
         name="merge",
-        compiler_params=LIMIT,
     )(*near(spectral, table, ports, taken, side, *own_parts, *pair_parts))
     messages = [move(message, level=d) for d in range(1, pairs)]
-    map_lines = 6 * total + SUBLANES
+    map_lines = MAP_PARTS * total
     *local, maps = pl.pallas_call(
         functools.partial(prepare_kernel, sizes),
         out_shape=(
@@ -424,22 +417,24 @@
         in_specs=[VMEM] * (3 + mode_count),
         out_specs=(VMEM,) * 4,
         name="prepare",
-        compiler_params=LIMIT,
     )(*near(spectral, table, side, *sources))
     late = late_level(pairs)
-    early = [d for d in range(1, pairs) if d != late]
-    level_maps = pl.pallas_call(
-        functools.partial(level_kernel, sizes, early),
-        out_shape=pltpu.VMEM((pairs, map_lines, LANES), f32),
-        in_specs=[VMEM] * (1 + len(early)),
-        out_specs=VMEM,
-        name="levels",
-        compiler_params=LIMIT,
-    )(*near(spectral, *(messages[d - 1] for d in early)))
+    level_maps = []
+    for d in range(1, pairs):
+        if d != late:
+            level_maps.append(
+                pl.pallas_call(
+                    functools.partial(level_kernel, sizes, d),
+                    out_shape=pltpu.VMEM((map_lines, LANES), f32),
+                    in_specs=[VMEM] * 2,
+                    out_specs=VMEM,
+                    name="levels",
+                )(*near(spectral, messages[d - 1]))
+            )
     out = pl.pallas_call(
         functools.partial(final_kernel, sizes, pairs, late),
         out_shape=jax.ShapeDtypeStruct((rows, 2, mode_count, height, LANES), f32),
-        in_specs=[VMEM] * (7 + (chips - 1) + (pairs - 1)),
+        in_specs=[VMEM] * (6 + (chips - 1) + (pairs - 1) + len(level_maps)),
         out_specs=ANY,
         scratch_shapes=[
             pltpu.VMEM((rows, 2, mode_count, height, LANES), f32),
@@ -448,7 +443,7 @@
         ],
         name="solve",
         compiler_params=LIMIT,
-    )(*near(spectral, side, *local, maps, level_maps, *pair_parts, *messages))
+    )(*near(spectral, side, *local, maps, *pair_parts, *messages, *level_maps))
     out = out.reshape(rows, 2, mode_count * tiles, kx_count, LANES).transpose(0, 1, 3, 2, 4)
     return out.reshape(rows, 2, kx_count, -1)
 

time: 31.6 us -> 26.1 us (0.83)
  local copies, waits for them, and re-layouts: 2.47 us -> 0.05 us
  waiting for transfers between devices: 11.1 us -> 8.93 us
  starting transfers between devices: 13.7 us -> 12.5 us
  Pallas kernels: 4 us -> 4.4 us
    unnamed x10 -> x0, local copies, waits for them, and re-layouts: 2.42 us -> none
    ppermute x10, waiting for transfers between devices: 11.1 us -> 8.93 us  [move(): return lax.ppermute(array, ('modes', 'gz'), links)]
    ppermute x10, starting transfers between devices: 13.7 us -> 12.5 us  [move(): return lax.ppermute(array, ('modes', 'gz'), links)]
    pallas_call x1 -> x2, Pallas kernels: 0.52 us -> 0.66 us  [solve(): pl.pallas_call(functools.partial(level_kernel, sizes, d), out_shape=pltpu...]
  transfers between devices with their start and end apart: 10 -> 10, of which waited for: 5 -> 4; matrix products, arithmetic and copies ran while one was open for 0% -> 0% of each run, Pallas kernels for 5% -> 7%
where the time goes in v4:
time: 26.1 us; the launch traced here: 26 us
  starting transfers between devices  12.5 us (48%)
  waiting for transfers between devices  8.93 us (34%)
  Pallas kernels  4.4 us (17%)
    ppermute x10, starting transfers between devices, move(): return lax.ppermute(array, ('modes', 'gz'), links)  12.5 us
    ppermute x10, waiting for transfers between devices, move(): return lax.ppermute(array, ('modes', 'gz'), links)  8.93 us
    pallas_call x1, Pallas kernels, solve(): pl.pallas_call(functools.partial(final_kernel, sizes, pairs, late), out_s...  1.31 us
    pallas_call x1, Pallas kernels, solve(): pl.pallas_call(functools.partial(reduce_kernel, sizes), out_shape=(pltpu....  1.24 us
    pallas_call x2, Pallas kernels, solve(): pl.pallas_call(functools.partial(level_kernel, sizes, d), out_shape=pltpu...  0.66 us
    pallas_call x1, Pallas kernels, solve(): pl.pallas_call(functools.partial(prepare_kernel, sizes), out_shape=(pltpu...  0.63 us
  transfers between devices with their start and end apart: 10, of which 4 were waited for; matrix products, arithmetic and copies ran while one was open for 0% of the time, Pallas kernels for 7%

profile of v4, /device:TPU:0, one launch (start us, length us, event | category | flops | bytes accessed | tf_op | source)
XLA Modules:
  0.0 26.0 jit_solution(12280802986819718594)
XLA Ops:
  0.0 1.2 %reduce.1 = (f32[2,2,32,128]{3,2,1,0:T(8,128)S(1)}, f32[8,128]{1,0:T(8,128)S(1)}, f32[32,128]{1,0:T(8,128)S(1)}, f32[16,2,8,512]{3,2,1,0:T(8,128)S(1)}) custom-call(f32[16]{0:T(128)} %below_hbm.1, f32[16]{0:T(128)} %above_hbm.1, f32[8]{0:T(128)} %stream_hbm.1, f32[16,128]{1,0:T(8,128)} %bitcast.24, f32[16,2,8,512]{3,2,1,0:T(8,128)} %source_hbm.1), custom_call_target="tpu_custom_call" | custom-call | tf_op jit(solution)/shard_map/reduce/pallas_call | solution.py:364
  1.3 0.6 %collective-permute-start = (f32[2,32,128]{2,1,0:T(8,128)S(1)}, f32[2,32,128]{2,1,0:T(8,128)S(1)}, u32[]{:S(2)}, u32[]{:S(2)}) collective-permute-start(f32[2,32,128]{2,1,0:T(8,128)S(1)} %slice_bitcast_fusion.4), channel_id=1, source_target_pairs={{0,8},{1,9},{2,10},{3,11},{4,12},{5,13},{6,14},{7,15},{8,0},{9,1},... | collective-permute-start | bytes 98312 | tf_op jit(solution)/shard_map/ppermute | solution.py:361
  1.8 0.2 regroup.1
  2.0 0.1 collective-permute-start.2
  2.1 3.0 %collective-permute-start.3 = (f32[16,2,8,128]{3,2,1,0:T(8,128)S(1)}, f32[16,2,8,128]{3,2,1,0:T(8,128)S(1)}, u32[]{:S(2)}, u32[]{:S(2)}) collective-permute-start(f32[16,2,8,128]{3,2,1,0:T(8,128)S(1)} %get-tuple-element.22), channel_id=1, source_target_pairs={{0,16},{1,17},{2,18},{3,19},{4,20},{5,21},{6,22},{7,23},{8,24},{9,... | collective-permute-start | bytes 393224 | tf_op jit(solution)/shard_map/ppermute | solution.py:361
  5.1 0.0 collective-permute-start.4
  5.1 0.0 collective-permute-done.taken_ref
  5.2 2.4 %collective-permute-start.5 = (f32[64,128]{1,0:T(8,128)S(1)}, f32[64,128]{1,0:T(8,128)S(1)}, u32[]{:S(2)}, u32[]{:S(2)}) collective-permute-start(f32[64,128]{1,0:T(8,128)S(1)} %pad_maximum_fusion.1), channel_id=1, source_target_pairs={{0,17},{1,16},{2,19},{3,18},{4,21},{5,20},{6,23},{7,22},{8,25},{9,... | collective-permute-start | bytes 98312 | tf_op jit(solution)/shard_map/ppermute | solution.py:361
  7.6 0.5 %collective-permute-start.1 = (f32[72,128]{1,0:T(8,128)S(1)}, f32[72,128]{1,0:T(8,128)S(1)}, u32[]{:S(2)}, u32[]{:S(2)}) collective-permute-start(f32[72,128]{1,0:T(8,128)S(1)} %pad_maximum_fusion), channel_id=1, source_target_pairs={{0,1},{1,0},{2,3},{3,2},{4,5},{5,4},{6,7},{7,6},{8,9},{9,8},{10,11... | collective-permute-start | bytes 110600 | tf_op jit(solution)/shard_map/ppermute | solution.py:361
  8.1 1.9 %collective-permute-done.5.rest_1_.rest_0_ = f32[64,128]{1,0:T(8,128)S(1)} collective-permute-done((f32[64,128]{1,0:T(8,128)S(1)}, f32[64,128]{1,0:T(8,128)S(1)}, u32[]{:S(2)}, u32[]{:S(2)}) %collective-permute-start.5) | collective-permute-done | bytes 32800 | tf_op jit(solution)/shard_map/ppermute | solution.py:361
  10.0 1.6 %collective-permute-start.6 = (f32[64,128]{1,0:T(8,128)S(1)}, f32[64,128]{1,0:T(8,128)S(1)}, u32[]{:S(2)}, u32[]{:S(2)}) collective-permute-start(f32[64,128]{1,0:T(8,128)S(1)} %pad_maximum_fusion.1), channel_id=1, source_target_pairs={{0,16},{1,17},{2,18},{3,19},{4,20},{5,21},{6,22},{7,23},{8,24},{9,... | collective-permute-start | bytes 98312 | tf_op jit(solution)/shard_map/ppermute | solution.py:361
  11.7 2.3 %collective-permute-done.6.rest_0_ = f32[64,128]{1,0:T(8,128)S(1)} collective-permute-done((f32[64,128]{1,0:T(8,128)S(1)}, f32[64,128]{1,0:T(8,128)S(1)}, u32[]{:S(2)}, u32[]{:S(2)}) %collective-permute-start.6) | collective-permute-done | bytes 32800 | tf_op jit(solution)/shard_map/ppermute | solution.py:361
  14.0 0.0 collective-permute-done.1.side_ref
  14.0 0.4 %merge.1 = f32[136,128]{1,0:T(8,128)S(1)} custom-call(f32[32,128]{1,0:T(8,128)S(1)} %get-tuple-element.13.spectral_ref, f32[8,128]{1,0:T(8,128)S(1)} %get-tuple-element.15.table_ref, f32[2,2,32,128]{3,2,1,0:T(8,128)S(1)} %get-tuple-element.14.ports_ref, f32[2,32,128]{2,1,0:T(8,128)S(1)} %collective-permute-done.taken_ref, ...), custom_call_target="tpu_custom_call" | custom-call | tf_op jit(solution)/shard_map/merge/pallas_call | solution.py:400
  14.3 1.7 %collective-permute-start.7 = (f32[136,128]{1,0:T(8,128)S(1)}, f32[136,128]{1,0:T(8,128)S(1)}, u32[]{:S(2)}, u32[]{:S(2)}) collective-permute-start(f32[136,128]{1,0:T(8,128)S(1)} %merge.1), channel_id=1, source_target_pairs={{0,2},{1,3},{2,0},{3,1},{4,6},{5,7},{6,4},{7,5},{8,10},{9,11},{10,... | collective-permute-start | bytes 208904 | tf_op jit(solution)/shard_map/ppermute | solution.py:361
  16.1 2.5 %collective-permute-start.9 = (f32[136,128]{1,0:T(8,128)S(1)}, f32[136,128]{1,0:T(8,128)S(1)}, u32[]{:S(2)}, u32[]{:S(2)}) collective-permute-start(f32[136,128]{1,0:T(8,128)S(1)} %merge.1), channel_id=1, source_target_pairs={{0,6},{1,7},{2,4},{3,5},{4,2},{5,3},{6,0},{7,1},{8,14},{9,15},{10,... | collective-permute-start | bytes 208904 | tf_op jit(solution)/shard_map/ppermute | solution.py:361
  18.6 0.0 collective-permute-done.2.rest_1_
  18.6 0.1 collective-permute-start.8
  18.7 0.0 collective-permute-done.3.rest_2_
  18.7 0.0 collective-permute-done.4.rest_3_
  18.7 0.6 %prepare.1 = (f32[16,2,32,128]{3,2,1,0:T(8,128)S(1)}, f32[16,32,128]{2,1,0:T(8,128)S(1)}, f32[16,32,128]{2,1,0:T(8,128)S(1)}, f32[3,224,128]{2,1,0:T(8,128)S(1)}) custom-call(f32[32,128]{1,0:T(8,128)S(1)} %get-tuple-element.13.spectral_ref, f32[8,128]{1,0:T(8,128)S(1)} %get-tuple-element.15.table_ref, f32[72,128]{1,0:T(8,128)S(1)} %collective-permute-done.1.side_ref, ...), custom_call_target="tpu_custom_call" | custom-call | tf_op jit(solution)/shard_map/prepare/pallas_call | solution.py:409
  19.3 0.0 collective-permute-done.7.message_ref.rest_1_
  19.3 0.3 %levels.2.rest_4_ = f32[224,128]{1,0:T(8,128)S(1)} custom-call(f32[32,128]{1,0:T(8,128)S(1)} %get-tuple-element.13.spectral_ref, f32[136,128]{1,0:T(8,128)S(1)} %collective-permute-done.7.message_ref.rest_1_), custom_call_target="tpu_custom_call" | custom-call | tf_op jit(solution)/shard_map/levels/pallas_call | solution.py:426
  19.7 2.8 %collective-permute-done.9.message_ref.rest_3_ = f32[136,128]{1,0:T(8,128)S(1)} collective-permute-done((f32[136,128]{1,0:T(8,128)S(1)}, f32[136,128]{1,0:T(8,128)S(1)}, u32[]{:S(2)}, u32[]{:S(2)}) %collective-permute-start.9) | collective-permute-done | bytes 69664 | tf_op jit(solution)/shard_map/ppermute | solution.py:361
  22.4 0.3 %levels.3.rest_5_ = f32[224,128]{1,0:T(8,128)S(1)} custom-call(f32[32,128]{1,0:T(8,128)S(1)} %get-tuple-element.13.spectral_ref, f32[136,128]{1,0:T(8,128)S(1)} %collective-permute-done.9.message_ref.rest_3_), custom_call_target="tpu_custom_call" | custom-call | tf_op jit(solution)/shard_map/levels/pallas_call | solution.py:426
  22.8 1.9 %collective-permute-done.8.rest_2_ = f32[136,128]{1,0:T(8,128)S(1)} collective-permute-done((f32[136,128]{1,0:T(8,128)S(1)}, f32[136,128]{1,0:T(8,128)S(1)}, u32[]{:S(2)}, u32[]{:S(2)}) %collective-permute-start.8) | collective-permute-done | bytes 69664 | tf_op jit(solution)/shard_map/ppermute | solution.py:361
  24.7 1.3 %solve.1 = f32[16,2,4,8,128]{4,3,2,1,0:T(8,128)} custom-call(f32[32,128]{1,0:T(8,128)S(1)} %get-tuple-element.13.spectral_ref, f32[72,128]{1,0:T(8,128)S(1)} %collective-permute-done.1.side_ref, f32[16,2,32,128]{3,2,1,0:T(8,128)S(1)} %get-tuple-element.17.part_ref, f32[16,32,128]{2,1,0:T(8,128)S(1)} %get-tuple-element.18.low_ref, ...), custom_call_target="tpu_custom_call" | custom-call | tf_op jit(solution)/shard_map/solve/pallas_call | solution.py:434
  (6 shorter events, 0.1 us)
Async XLA Ops:
  1.3 3.9 %collective-permute-start = (f32[2,32,128]{2,1,0:T(8,128)S(1)}, f32[2,32,128]{2,1,0:T(8,128)S(1)}, u32[]{:S(2)}, u32[]{:S(2)}) collective-permute-start(f32[2,32,128]{2,1,0:T(8,128)S(1)} %slice_bitcast_fusion.4), channel_id=1, source_target_pairs={{0,8},{1,9},{2,10},{3,11},{4,12},{5,13},{6,14},{7,15},{8,0},{9,1},... | collective-permute-start | bytes 98312 | tf_op jit(solution)/shard_map/ppermute | solution.py:361
  2.0 16.5 %collective-permute-start.2 = (f32[16,2,8,128]{3,2,1,0:T(8,128)S(1)}, f32[16,2,8,128]{3,2,1,0:T(8,128)S(1)}, u32[]{:S(2)}, u32[]{:S(2)}) collective-permute-start(f32[16,2,8,128]{3,2,1,0:T(8,128)S(1)} %get-tuple-element.23), channel_id=1, source_target_pairs={{0,8},{1,9},{2,10},{3,11},{4,12},{5,13},{6,14},{7,15},{8,0},{9,1},... | collective-permute-start | bytes 393224 | tf_op jit(solution)/shard_map/ppermute | solution.py:361
  2.1 16.5 %collective-permute-start.3 = (f32[16,2,8,128]{3,2,1,0:T(8,128)S(1)}, f32[16,2,8,128]{3,2,1,0:T(8,128)S(1)}, u32[]{:S(2)}, u32[]{:S(2)}) collective-permute-start(f32[16,2,8,128]{3,2,1,0:T(8,128)S(1)} %get-tuple-element.22), channel_id=1, source_target_pairs={{0,16},{1,17},{2,18},{3,19},{4,20},{5,21},{6,22},{7,23},{8,24},{9,... | collective-permute-start | bytes 393224 | tf_op jit(solution)/shard_map/ppermute | solution.py:361
  5.1 13.6 %collective-permute-start.4 = (f32[16,2,8,128]{3,2,1,0:T(8,128)S(1)}, f32[16,2,8,128]{3,2,1,0:T(8,128)S(1)}, u32[]{:S(2)}, u32[]{:S(2)}) collective-permute-start(f32[16,2,8,128]{3,2,1,0:T(8,128)S(1)} %get-tuple-element.21), channel_id=1, source_target_pairs={{0,24},{1,25},{2,26},{3,27},{4,28},{5,29},{6,30},{7,31},{8,16},{9,... | collective-permute-start | bytes 393224 | tf_op jit(solution)/shard_map/ppermute | solution.py:361
  5.2 4.9 %collective-permute-start.5 = (f32[64,128]{1,0:T(8,128)S(1)}, f32[64,128]{1,0:T(8,128)S(1)}, u32[]{:S(2)}, u32[]{:S(2)}) collective-permute-start(f32[64,128]{1,0:T(8,128)S(1)} %pad_maximum_fusion.1), channel_id=1, source_target_pairs={{0,17},{1,16},{2,19},{3,18},{4,21},{5,20},{6,23},{7,22},{8,25},{9,... | collective-permute-start | bytes 98312 | tf_op jit(solution)/shard_map/ppermute | solution.py:361
  7.6 6.4 %collective-permute-start.1 = (f32[72,128]{1,0:T(8,128)S(1)}, f32[72,128]{1,0:T(8,128)S(1)}, u32[]{:S(2)}, u32[]{:S(2)}) collective-permute-start(f32[72,128]{1,0:T(8,128)S(1)} %pad_maximum_fusion), channel_id=1, source_target_pairs={{0,1},{1,0},{2,3},{3,2},{4,5},{5,4},{6,7},{7,6},{8,9},{9,8},{10,11... | collective-permute-start | bytes 110600 | tf_op jit(solution)/shard_map/ppermute | solution.py:361
  10.0 3.9 %collective-permute-start.6 = (f32[64,128]{1,0:T(8,128)S(1)}, f32[64,128]{1,0:T(8,128)S(1)}, u32[]{:S(2)}, u32[]{:S(2)}) collective-permute-start(f32[64,128]{1,0:T(8,128)S(1)} %pad_maximum_fusion.1), channel_id=1, source_target_pairs={{0,16},{1,17},{2,18},{3,19},{4,20},{5,21},{6,22},{7,23},{8,24},{9,... | collective-permute-start | bytes 98312 | tf_op jit(solution)/shard_map/ppermute | solution.py:361
  14.3 5.0 %collective-permute-start.7 = (f32[136,128]{1,0:T(8,128)S(1)}, f32[136,128]{1,0:T(8,128)S(1)}, u32[]{:S(2)}, u32[]{:S(2)}) collective-permute-start(f32[136,128]{1,0:T(8,128)S(1)} %merge.1), channel_id=1, source_target_pairs={{0,2},{1,3},{2,0},{3,1},{4,6},{5,7},{6,4},{7,5},{8,10},{9,11},{10,... | collective-permute-start | bytes 208904 | tf_op jit(solution)/shard_map/ppermute | solution.py:361
  16.1 6.4 %collective-permute-start.9 = (f32[136,128]{1,0:T(8,128)S(1)}, f32[136,128]{1,0:T(8,128)S(1)}, u32[]{:S(2)}, u32[]{:S(2)}) collective-permute-start(f32[136,128]{1,0:T(8,128)S(1)} %merge.1), channel_id=1, source_target_pairs={{0,6},{1,7},{2,4},{3,5},{4,2},{5,3},{6,0},{7,1},{8,14},{9,15},{10,... | collective-permute-start | bytes 208904 | tf_op jit(solution)/shard_map/ppermute | solution.py:361
  18.6 6.1 %collective-permute-start.8 = (f32[136,128]{1,0:T(8,128)S(1)}, f32[136,128]{1,0:T(8,128)S(1)}, u32[]{:S(2)}, u32[]{:S(2)}) collective-permute-start(f32[136,128]{1,0:T(8,128)S(1)} %merge.1), channel_id=1, source_target_pairs={{0,4},{1,5},{2,6},{3,7},{4,0},{5,1},{6,2},{7,3},{8,12},{9,13},{10,... | collective-permute-start | bytes 208904 | tf_op jit(solution)/shard_map/ppermute | solution.py:361

commit v5 on v4

--- a/solution.py
+++ b/solution.py
@@ -57,10 +57,11 @@
     table_ref[...] = table
     for d in range(mode_count):
         for t in range(tiles):
-            spanwise = span_ref[pl.ds((me ^ d) * tiles + t, 1), :]
-            for j in range(kx_count):
-                at = d * height + t * kx_count + j
-                spectral_ref[at : at + 1, :] = spanwise + stream_ref[me * kx_count + j]
+            for owner in range(2):
+                spanwise = span_ref[pl.ds((me ^ owner ^ d) * tiles + t, 1), :]
+                for j in range(kx_count):
+                    at = d * height + t * kx_count + j
+                    spectral_ref[owner, at : at + 1, :] = spanwise + stream_ref[(me ^ owner) * kx_count + j]
     shape = (kx_total, LANES)
     kx_at = lax.broadcasted_iota(jnp.int32, shape, 0)
     streamwise = jnp.zeros(shape, jnp.float32)
@@ -116,48 +117,51 @@
     for k in range(len(near)):
         step = near[k] * num
         num = spectral * den + step
-        before = den
         den = (spectral + far[k]) * den + step
         if k:
             product = product * near[k]
-    return num, den, far[-1] * before, product
-
-
-MAP_PARTS = 7
+    return num, den, product
+
+
+MAP_PARTS = 5
 
 
 def put_map(ref, lead, spectral, near, far):
     total = spectral.shape[0]
-    zero = jnp.zeros_like(spectral)
-    num = [near[0] + zero, spectral]
+    num = [near[0] + jnp.zeros_like(spectral), spectral]
     den = [num[0], spectral + far[0]]
-    tail = [zero, far[0] + zero]
     product = near[0]
     for k in range(1, len(near)):
         held = spectral + far[k]
-        if k == len(near) - 1:
-            tail = [far[k] * den[i] for i in range(2)]
         step = [near[k] * num[i] for i in range(2)]
         num = [spectral * den[i] + step[i] for i in range(2)]
         den = [held * den[i] + step[i] for i in range(2)]
         product = product * near[k]
     scale = 1.0 / (den[0] + den[1])
-    for i, value in enumerate([*num, *den, *tail, product]):
+    for i, value in enumerate([*num, *den, product]):
         ref[(*lead, slice(i * total, (i + 1) * total), slice(None))] = value * scale
 
 
+def leave_with(state, new_den, product, leave, entry):
+    num, den, *partial = state
+    return [leave[c] * new_den + product * (partial[c] + (den - num) * entry[c]) for c in range(2)]
+
+
 def apply_map(block, state, leave, entry):
-    num, den, tail, *partial = state
+    num, den = state[:2]
     new_den = block(2) * num + block(3) * den
-    new = [leave[c] * new_den + block(6) * (partial[c] + tail * entry[c]) for c in range(2)]
-    return (block(0) * num + block(1) * den, new_den, block(4) * num + block(5) * den, *new)
+    return (block(0) * num + block(1) * den, new_den, *leave_with(state, new_den, block(4), leave, entry))
+
+
+def choose(condition, first, second):
+    return [jnp.where(condition, a, b) for a, b in zip(first, second)]
 
 
 def map_of(ref, lead, total):
     return lambda i: ref[(*lead, slice(i * total, (i + 1) * total), slice(None))]
 
 
-def merge_kernel(sizes, spectral_ref, table_ref, ports_ref, taken_ref, side_ref, *rest):
+def merge_kernel(sizes, spectral_ref, table_ref, own_ref, side_ref, *rest):
     rows, _, _, _, mode_count, height = sizes
     chips = mode_count // 2
     own_refs, pair_refs, message_ref = rest[: chips - 1], rest[chips - 1 : 2 * (chips - 1)], rest[-1]
@@ -169,10 +173,8 @@
         return jnp.concatenate([chunk(d, i * height) for d in range(mode_count)], axis=0)
 
     def own_chunk(d, at):
-        if d >= 2:
-            start = (d % 2) * port + at
-            return own_refs[d // 2 - 1][start : start + height, :]
-        return ports_ref[0, 0, at : at + height, :] if d == 0 else taken_ref[0, at : at + height, :]
+        start = (d % 2) * port + at
+        return (own_ref if d < 2 else own_refs[d // 2 - 1])[start : start + height, :]
 
     def pair_chunk(d, at):
         start = (d % 2) * port + at
@@ -199,9 +201,9 @@
 
     for near_line, first, second, near_side, far_side in ((0, low_table, high_table, 0, 2), (2, high_table, low_table, 2, 0)):
         lines = (near_line, near_line + 1)
-        num, den, tail, _ = climb(spectral, one, one, *(couplings(first, i, rows) for i in lines))
-        passed = tail / den
-        _, den_all, _, product = climb(spectral, num, den, *(couplings(second, i, rows) for i in lines))
+        num, den, _ = climb(spectral, one, one, *(couplings(first, i, rows) for i in lines))
+        passed = (den - num) / den
+        _, den_all, product = climb(spectral, num, den, *(couplings(second, i, rows) for i in lines))
         ratio = product * den / den_all
         before, after = (low, high) if near_line == 0 else (high, low)
         for c in range(2):
@@ -246,52 +248,109 @@
     put_map(maps_ref, (2,), spectral, couplings(lines, 0, rows), couplings(lines, 1, rows))
 
 
-def put_level(sizes, level, d, message_ref, spectral, ref, lead):
-    rows, total = sizes[0], spectral.shape[0]
+def level_couplings(sizes, message_ref, total, downwards):
     table = message_ref[4 * total :, :]
-    lines = jnp.where((level ^ d) < level, table[0:2], table[2:4])
-    put_map(ref, lead, spectral, couplings(lines, 0, 2 * rows), couplings(lines, 1, 2 * rows))
+    lines = jnp.where(downwards, table[2:4], table[0:2])
+    return couplings(lines, 0, 2 * sizes[0]), couplings(lines, 1, 2 * sizes[0])
 
 
 def level_kernel(sizes, d, spectral_ref, message_ref, map_ref):
-    put_level(sizes, lax.axis_index("gz") // 2, d, message_ref, spectral_ref[...], map_ref, ())
-
-
-def final_kernel(sizes, pairs, late, spectral_ref, side_ref, part_ref, low_ref, high_ref, maps_ref, *rest):
-    rows, _, _, _, mode_count, height = sizes
+    level = lax.axis_index("gz") // 2
+    spectral = spectral_ref[...]
+    put_map(map_ref, (), spectral, *level_couplings(sizes, message_ref, spectral.shape[0], (level ^ d) > level))
+
+
+def quad_kernel(sizes, spectral_ref, own_ref, neighbour_ref, edge_ref):
+    spectral = spectral_ref[...]
+    total = spectral.shape[0]
+    level = lax.axis_index("gz") // 2
+    lower, outer = level < 2, (level == 0) | (level == 3)
+
+    def ports(ref, at):
+        return [ref[(at + c) * total : (at + c + 1) * total, :] for c in range(2)]
+
+    def of(ref):
+        return choose(lower, ports(ref, 2), ports(ref, 0)), choose(lower, ports(ref, 0), ports(ref, 2))
+
+    own, neighbour = of(own_ref), of(neighbour_ref)
+    leave_first = choose(outer, own[0], neighbour[0])
+    leave_then, entry_then = choose(outer, neighbour[0], own[0]), choose(outer, neighbour[1], own[1])
+    own_table, neighbour_table = own_ref[4 * total :, :], neighbour_ref[4 * total :, :]
+    own_lines = jnp.where(lower, own_table[0:2], own_table[2:4])
+    neighbour_lines = jnp.where(lower, neighbour_table[0:2], neighbour_table[2:4])
+    first, then = jnp.where(outer, own_lines, neighbour_lines), jnp.where(outer, neighbour_lines, own_lines)
+    count = 2 * sizes[0]
+    one = jnp.ones_like(spectral)
+    num, den, _ = climb(spectral, one, one, couplings(first, 0, count), couplings(first, 1, count))
+    scale = 1.0 / den
+    state = (num * scale, one, *leave_first)
+    num, den, product = climb(spectral, state[0], one, couplings(then, 0, count), couplings(then, 1, count))
+    scale = 1.0 / den
+    for i, value in enumerate([num, *leave_with(state, den, product, leave_then, entry_then)]):
+        edge_ref[i * total : (i + 1) * total, :] = value * scale
+
+
+def quads_kernel(sizes, part_ref, low_ref, high_ref, maps_ref, neighbour_map, neighbour_ref, other_ref, side_ref, *rest):
+    _, _, _, _, mode_count, height = sizes
+    total = mode_count * height
+    pair_refs, (out_hbm, out_ref, sems) = rest[: mode_count // 2 - 1], rest[mode_count // 2 - 1 :]
+    level = lax.axis_index("gz") // 2
+    odd, outer = level % 2 == 1, (level == 0) | (level == 3)
+    one, zero = jnp.ones((total, LANES), jnp.float32), jnp.zeros((total, LANES), jnp.float32)
+    wall = (one, one, zero, zero)
+    values = [other_ref[i * total : (i + 1) * total, :] for i in range(3)]
+    other = (values[0], one, *values[1:])
+    ports = [neighbour_ref[i * total : (i + 1) * total, :] for i in range(4)]
+    leave, entry = choose(odd, ports[2:], ports[:2]), choose(odd, ports[:2], ports[2:])
+    crossed = apply_map(map_of(neighbour_map, (), total), choose(outer, other, wall), leave, entry)
+    plain = choose(outer, wall, other)
+    below, above = choose(odd, crossed, plain), choose(odd, plain, crossed)
+    finish(sizes, below, above, part_ref, low_ref, high_ref, maps_ref, side_ref, pair_refs, out_hbm, out_ref, sems)
+
+
+def levels_kernel(sizes, pairs, late, spectral_ref, side_ref, part_ref, low_ref, high_ref, maps_ref, *rest):
+    _, _, _, _, mode_count, height = sizes
     chips = mode_count // 2
     total = mode_count * height
-    port = 4 * height
     pair_refs, rest = rest[: chips - 1], rest[chips - 1 :]
     messages, rest = rest[: pairs - 1], rest[pairs - 1 :]
-    level_maps, (out_hbm, out_ref, late_ref, sems) = list(rest[: pairs - 2]), rest[pairs - 2 :]
-    level_maps.insert(late - 1, late_ref)
-    me, partition = lax.axis_index("modes"), lax.axis_index("gz")
-    upside, level = partition % 2 == 1, partition // 2
-    put_level(sizes, level, late, messages[late - 1], spectral_ref[...], late_ref, ())
-    one = jnp.ones((total, LANES), jnp.float32)
-    zero = jnp.zeros((total, LANES), jnp.float32)
-    start = (one, one, zero, zero, zero)
+    level_maps, (out_hbm, out_ref, sems) = list(rest[: pairs - 2]), rest[pairs - 2 :]
+    level_maps.insert(late - 1, None)
+    spectral = spectral_ref[...]
+    level = lax.axis_index("gz") // 2
+    late_near, late_far = level_couplings(sizes, messages[late - 1], total, (level ^ late) > level)
+    one, zero = jnp.ones((total, LANES), jnp.float32), jnp.zeros((total, LANES), jnp.float32)
+    start = (one, one, zero, zero)
 
     def cross(state, d, leave, entry):
         ref = messages[d - 1]
         ports = [ref[i * total : (i + 1) * total, :] for i in (leave, leave + 1, entry, entry + 1)]
-        return apply_map(map_of(level_maps[d - 1], (), total), state, ports[:2], ports[2:])
-
-    def cross_levels(z, state, at):
-        leave, entry = (2, 0) if at < z else (0, 2)
-        return cross(state, z ^ at, leave, entry)
+        if d != late:
+            return apply_map(map_of(level_maps[d - 1], (), total), state, ports[:2], ports[2:])
+        num, den, product = climb(spectral, *state[:2], late_near, late_far)
+        return (num, den, *leave_with(state, den, product, ports[:2], ports[2:]))
+
+    def cross_all(z, ats):
+        state = start
+        for i, at in enumerate(ats):
+            if i and i % 4 == 0:
+                inverse = 1.0 / state[1]
+                state = tuple(value * inverse for value in state)
+            state = cross(state, z ^ at, *((2, 0) if at < z else (0, 2)))
+        return state
 
     def at_level(z):
-        def states():
-            below, above = start, start
-            for at in range(z):
-                below = cross_levels(z, below, at)
-            for at in range(pairs - 1, z, -1):
-                above = cross_levels(z, above, at)
-            return below, above
-
-        return states
+        return lambda: (cross_all(z, range(z)), cross_all(z, range(pairs - 1, z, -1)))
+
+    below, above = lax.switch(level, [at_level(z) for z in range(pairs)])
+    finish(sizes, below, above, part_ref, low_ref, high_ref, maps_ref, side_ref, pair_refs, out_hbm, out_ref, sems)
+
+
+def finish(sizes, below, above, part_ref, low_ref, high_ref, maps_ref, side_ref, pair_refs, out_hbm, out_ref, sems):
+    rows, _, _, _, mode_count, height = sizes
+    total = mode_count * height
+    port = 4 * height
+    me, upside = lax.axis_index("modes"), lax.axis_index("gz") % 2 == 1
 
     def pair_ports(i):
         chunks = []
@@ -300,26 +359,23 @@
             chunks.append((side_ref if d < 2 else pair_refs[d // 2 - 1])[at : at + height, :])
         return jnp.concatenate(chunks, axis=0)
 
-    below, above = lax.switch(level, [at_level(z) for z in range(pairs)])
     ports = [pair_ports(i) for i in range(4)]
-    near_state = [jnp.where(upside, b, a) for b, a in zip(below, above)]
-    leave = [jnp.where(upside, ports[2 + c], ports[c]) for c in range(2)]
-    entry = [jnp.where(upside, ports[c], ports[2 + c]) for c in range(2)]
-    crossed = apply_map(map_of(maps_ref, (2,), total), near_state, leave, entry)
-    below = [jnp.where(upside, new, old) for new, old in zip(crossed, below)]
-    above = [jnp.where(upside, old, new) for new, old in zip(crossed, above)]
+    leave, entry = choose(upside, ports[2:], ports[:2]), choose(upside, ports[:2], ports[2:])
+    crossed = apply_map(map_of(maps_ref, (2,), total), choose(upside, below, above), leave, entry)
+    below, above = choose(upside, crossed, below), choose(upside, above, crossed)
     own_first, own_last = [part_ref[0, c] for c in range(2)], [part_ref[rows - 1, c] for c in range(2)]
-    leaving_up = apply_map(map_of(maps_ref, (0,), total), below, own_last, own_first)
-    leaving_down = apply_map(map_of(maps_ref, (1,), total), above, own_first, own_last)
-    inverse_up = 1.0 / (leaving_up[0] * above[1] + leaving_up[2] * above[0])
-    inverse_down = 1.0 / (leaving_down[0] * below[1] + leaving_down[2] * below[0])
+    up = apply_map(map_of(maps_ref, (0,), total), below, own_last, own_first)
+    down = apply_map(map_of(maps_ref, (1,), total), above, own_first, own_last)
+    up_passed, down_passed = up[1] - up[0], down[1] - down[0]
+    inverse_up = 1.0 / (up[0] * above[1] + up_passed * above[0])
+    inverse_down = 1.0 / (down[0] * below[1] + down_passed * below[0])
     inverse_below, inverse_above = 1.0 / below[1], 1.0 / above[1]
     under, over = [], []
-    for c in range(3, 5):
-        last = (leaving_up[c] * above[1] + leaving_up[2] * above[c]) * inverse_up
-        over.append((above[c] + above[2] * last) * inverse_above)
-        first = (leaving_down[c] * below[1] + leaving_down[2] * below[c]) * inverse_down
-        under.append((below[c] + below[2] * first) * inverse_below)
+    for c in range(2, 4):
+        last = (up[c] * above[1] + up_passed * above[c]) * inverse_up
+        over.append((above[c] + (above[1] - above[0]) * last) * inverse_above)
+        first = (down[c] * below[1] + down_passed * below[c]) * inverse_down
+        under.append((below[c] + (below[1] - below[0]) * first) * inverse_below)
     copies = []
     for i, (first, size) in enumerate(chunks_of(rows)):
         for k in range(first, first + size):
@@ -352,12 +408,12 @@
     f32 = jnp.float32
     chunk_sems = pltpu.SemaphoreType.DMA((len(chunks_of(rows)),))
 
-    def move(array, modes_by=0, pair=0, level=0):
+    def move(array, modes_by=0, pair=0, level=0, core=lambda z: 0):
         links = []
         for m in range(mode_count):
             for g in range(partitions):
                 to = ((g // 2) ^ level) * 2 + ((g % 2) ^ pair)
-                links.append((m * partitions + g, (m ^ modes_by) * partitions + to))
+                links.append((m * partitions + g, (m ^ modes_by ^ core(g // 2)) * partitions + to))
         return lax.ppermute(array, ("modes", "gz"), links)
 
     span = eigen_span.reshape(-1, LANES)
@@ -366,7 +422,7 @@
         out_shape=(
             pltpu.VMEM((2, chips, 4 * height, LANES), f32),
             pltpu.VMEM((SUBLANES, LANES), f32),
-            pltpu.VMEM((total, LANES), f32),
+            pltpu.VMEM((2, total, LANES), f32),
             pltpu.VMEM(source_field.shape, f32),
         ),
         in_specs=[ANY] * 5,
@@ -389,22 +445,52 @@
         name="regroup",
     )(*near(source))
 
-    taken = move(ports[1], modes_by=1)
+    quads = pairs == 4
+    even = (lax.axis_index("gz") // 2) % 2 == 0
+    swapped = (lambda z: 1 - z % 2) if quads else (lambda z: 0)
+    if quads:
+        taken = move(ports, modes_by=1)
+        theirs = taken[1]
+    else:
+        theirs = move(ports[1], modes_by=1)
+    blocks_out = [jnp.concatenate([ports[0, d], theirs[d]], axis=0) for d in range(chips)]
     own_parts, pair_parts = [], []
     for d in range(1, chips):
-        block = jnp.concatenate([ports[0, d], taken[d]], axis=0)
-        pair_parts.append(move(block, modes_by=2 * d, pair=1))
-        own_parts.append(move(block, modes_by=2 * d))
-    side = move(jnp.concatenate([ports[0, 0], taken[0], table], axis=0), pair=1)
+        pair_parts.append(move(blocks_out[d], modes_by=2 * d, pair=1, core=swapped))
+        own_parts.append(move(blocks_out[d], modes_by=2 * d, core=swapped))
+    side = move(jnp.concatenate([blocks_out[0], table], axis=0), pair=1, core=swapped)
     sources = [move(blocks[d], modes_by=d) if d else blocks[0] for d in range(mode_count)]
+    both_spectral = spectral
+    own_block, merged_spectral, spectral = blocks_out[0], spectral[0], spectral[0]
+    if quads:
+        own_block = jnp.where(even, jnp.concatenate([taken[0, 0], ports[1, 0]], axis=0), own_block)
+        merged_spectral = jnp.where(even, both_spectral[1], spectral)
     message = pl.pallas_call(
         functools.partial(merge_kernel, sizes),
         out_shape=pltpu.VMEM((4 * total + SUBLANES, LANES), f32),
-        in_specs=[VMEM] * (5 + 2 * (chips - 1)),
+        in_specs=[VMEM] * (4 + 2 * (chips - 1)),
         out_specs=VMEM,
         name="merge",
-    )(*near(spectral, table, ports, taken, side, *own_parts, *pair_parts))
-    messages = [move(message, level=d) for d in range(1, pairs)]
+    )(*near(merged_spectral, table, own_block, side, *own_parts, *pair_parts))
+    if quads:
+        messages = [move(message, modes_by=1, level=1)]
+        edge = pl.pallas_call(
+            functools.partial(quad_kernel, sizes),
+            out_shape=pltpu.VMEM((3 * total, LANES), f32),
+            in_specs=[VMEM] * 3,
+            out_specs=VMEM,
+            name="quad",
+        )(*near(merged_spectral, message, messages[0]))
+        other = move(edge, level=2, core=swapped)
+        parcel = jnp.concatenate([side, *pair_parts, messages[0][: 4 * total]], axis=0)
+        parcel = jnp.where(even, move(parcel, modes_by=1), parcel)
+        lines = side.shape[0]
+        owned = [parcel[lines * 0 : lines]]
+        for d in range(1, chips):
+            owned.append(parcel[lines + (d - 1) * 8 * height : lines + d * 8 * height])
+        owned_neighbour = parcel[lines + (chips - 1) * 8 * height :]
+    else:
+        messages = [move(message, level=d) for d in range(1, pairs)]
     map_lines = MAP_PARTS * total
     *local, maps = pl.pallas_call(
         functools.partial(prepare_kernel, sizes),
@@ -418,9 +504,9 @@
         out_specs=(VMEM,) * 4,
         name="prepare",
     )(*near(spectral, table, side, *sources))
-    late = late_level(pairs)
+    late = None if quads else late_level(pairs)
     level_maps = []
-    for d in range(1, pairs):
+    for d in range(1, 2 if quads else pairs):
         if d != late:
             level_maps.append(
                 pl.pallas_call(
@@ -431,19 +517,21 @@
                     name="levels",
                 )(*near(spectral, messages[d - 1]))
             )
+    if quads:
+        kernel = functools.partial(quads_kernel, sizes)
+        operands = (*local, maps, level_maps[0], owned_neighbour, other, *owned)
+    else:
+        kernel = functools.partial(levels_kernel, sizes, pairs, late)
+        operands = (spectral, side, *local, maps, *pair_parts, *messages, *level_maps)
     out = pl.pallas_call(
-        functools.partial(final_kernel, sizes, pairs, late),
+        kernel,
         out_shape=jax.ShapeDtypeStruct((rows, 2, mode_count, height, LANES), f32),
-        in_specs=[VMEM] * (6 + (chips - 1) + (pairs - 1) + len(level_maps)),
+        in_specs=[VMEM] * len(operands),
         out_specs=ANY,
-        scratch_shapes=[
-            pltpu.VMEM((rows, 2, mode_count, height, LANES), f32),
-            pltpu.VMEM((map_lines, LANES), f32),
-            chunk_sems,
-        ],
+        scratch_shapes=[pltpu.VMEM((rows, 2, mode_count, height, LANES), f32), chunk_sems],
         name="solve",
         compiler_params=LIMIT,
-    )(*near(spectral, side, *local, maps, *pair_parts, *messages, *level_maps))
+    )(*near(*operands))
     out = out.reshape(rows, 2, mode_count * tiles, kx_count, LANES).transpose(0, 1, 3, 2, 4)
     return out.reshape(rows, 2, kx_count, -1)
 

time: 26.1 us -> 28.8 us (1.10)
  waiting for transfers between devices: 8.93 us -> 11.9 us
  Pallas kernels: 4.4 us -> 4.07 us
    ppermute x10, waiting for transfers between devices: 8.93 us -> 11.9 us  [move(): return lax.ppermute(array, ('modes', 'gz'), links)]
    pallas_call x2 -> x1, Pallas kernels: 0.66 us -> 0.32 us  [solve(): pl.pallas_call(functools.partial(level_kernel, sizes, d), out_shape=pltpu...]
    pallas_call x1 -> x2, Pallas kernels: 1.31 us -> 1.34 us  [the longest x1 0.98 us: solve(): pl.pallas_call(kernel, out_shape=jax.ShapeDtypeStruct((rows, 2, mode_coun...]
  transfers between devices with their start and end apart: 10 -> 10, of which waited for: 4 -> 7; matrix products, arithmetic and copies ran while one was open for 0% -> 0% of each run, Pallas kernels for 7% -> 5%
where the time goes in v5:
time: 28.8 us; the launch traced here: 28.7 us
  starting transfers between devices  12.5 us (43%)
  waiting for transfers between devices  11.9 us (41%)
  Pallas kernels  4.07 us (14%)
    ppermute x10, starting transfers between devices, move(): return lax.ppermute(array, ('modes', 'gz'), links)  12.5 us
    ppermute x10, waiting for transfers between devices, move(): return lax.ppermute(array, ('modes', 'gz'), links)  11.9 us
    pallas_call x1, Pallas kernels, solve(): pl.pallas_call(functools.partial(reduce_kernel, sizes), out_shape=(pltpu....  1.24 us
    pallas_call x1, Pallas kernels, solve(): pl.pallas_call(kernel, out_shape=jax.ShapeDtypeStruct((rows, 2, mode_coun...  0.98 us
    pallas_call x1, Pallas kernels, solve(): pl.pallas_call(functools.partial(prepare_kernel, sizes), out_shape=(pltpu...  0.61 us
  transfers between devices with their start and end apart: 10, of which 7 were waited for; matrix products, arithmetic and copies ran while one was open for 0% of the time, Pallas kernels for 5%

profile of v5, /device:TPU:0, one launch (start us, length us, event | category | flops | bytes accessed | tf_op | source)
XLA Modules:
  0.0 28.7 jit_solution(10947779164515143089)
XLA Ops:
  0.0 1.2 %reduce.1 = (f32[2,2,32,128]{3,2,1,0:T(8,128)S(1)}, f32[8,128]{1,0:T(8,128)S(1)}, f32[2,32,128]{2,1,0:T(8,128)S(1)}, f32[16,2,8,512]{3,2,1,0:T(8,128)S(1)}) custom-call(f32[16]{0:T(128)} %below_hbm.1, f32[16]{0:T(128)} %above_hbm.1, f32[8]{0:T(128)} %stream_hbm.1, f32[16,128]{1,0:T(8,128)} %bitcast.32, f32[16,2,8,512]{3,2,1,0:T(8,128)} %source_hbm.1), custom_call_target="tpu_custom_call" | custom-call | tf_op jit(solution)/shard_map/reduce/pallas_call | solution.py:420
  1.2 0.6 %collective-permute-start = (f32[2,2,32,128]{3,2,1,0:T(8,128)S(1)}, f32[2,2,32,128]{3,2,1,0:T(8,128)S(1)}, u32[]{:S(2)}, u32[]{:S(2)}) collective-permute-start(f32[2,2,32,128]{3,2,1,0:T(8,128)S(1)} %get-tuple-element.15), channel_id=1, source_target_pairs={{0,8},{1,9},{2,10},{3,11},{4,12},{5,13},{6,14},{7,15},{8,0},{9,1},... | collective-permute-start | bytes 196616 | tf_op jit(solution)/shard_map/ppermute | solution.py:417
  1.8 0.2 regroup.1
  2.0 0.7 %collective-permute-done = f32[2,2,32,128]{3,2,1,0:T(8,128)S(1)} collective-permute-done((f32[2,2,32,128]{3,2,1,0:T(8,128)S(1)}, f32[2,2,32,128]{3,2,1,0:T(8,128)S(1)}, u32[]{:S(2)}, u32[]{:S(2)}) %collective-permute-start) | collective-permute-done | bytes 65568 | tf_op jit(solution)/shard_map/ppermute | solution.py:417
  2.7 2.7 %collective-permute-start.5 = (f32[64,128]{1,0:T(8,128)S(1)}, f32[64,128]{1,0:T(8,128)S(1)}, u32[]{:S(2)}, u32[]{:S(2)}) collective-permute-start(f32[64,128]{1,0:T(8,128)S(1)} %pad_maximum_fusion.2), channel_id=1, source_target_pairs={{0,24},{1,25},{2,18},{3,19},{4,28},{5,29},{6,22},{7,23},{8,16},{9,... | collective-permute-start | bytes 98312 | tf_op jit(solution)/shard_map/ppermute | solution.py:417
  5.4 1.4 %collective-permute-start.6 = (f32[64,128]{1,0:T(8,128)S(1)}, f32[64,128]{1,0:T(8,128)S(1)}, u32[]{:S(2)}, u32[]{:S(2)}) collective-permute-start(f32[64,128]{1,0:T(8,128)S(1)} %pad_maximum_fusion.2), channel_id=1, source_target_pairs={{0,25},{1,24},{2,19},{3,18},{4,29},{5,28},{6,23},{7,22},{8,17},{9,... | collective-permute-start | bytes 98312 | tf_op jit(solution)/shard_map/ppermute | solution.py:417
  6.8 0.1 collective-permute-start.1
  6.9 0.1 collective-permute-done.5.rest_0_
  7.0 2.6 %collective-permute-done.6.rest_1_ = f32[64,128]{1,0:T(8,128)S(1)} collective-permute-done((f32[64,128]{1,0:T(8,128)S(1)}, f32[64,128]{1,0:T(8,128)S(1)}, u32[]{:S(2)}, u32[]{:S(2)}) %collective-permute-start.6) | collective-permute-done | bytes 32800 | tf_op jit(solution)/shard_map/ppermute | solution.py:417
  9.6 0.6 %collective-permute-done.1.side_ref = f32[72,128]{1,0:T(8,128)S(1)} collective-permute-done((f32[72,128]{1,0:T(8,128)S(1)}, f32[72,128]{1,0:T(8,128)S(1)}, u32[]{:S(2)}, u32[]{:S(2)}) %collective-permute-start.1) | collective-permute-done | bytes 36896 | tf_op jit(solution)/shard_map/ppermute | solution.py:417
  10.2 0.4 %merge.1.own_ref = f32[136,128]{1,0:T(8,128)S(1)} custom-call(f32[32,128]{1,0:T(8,128)S(1)} %bitcast_select_fusion.spectral_ref, f32[8,128]{1,0:T(8,128)S(1)} %get-tuple-element.14.table_ref, f32[64,128]{1,0:T(8,128)S(1)} %maximum_select_fusion.own_ref, f32[72,128]{1,0:T(8,128)S(1)} %collective-permute-done.1.side_ref, ...), custom_call_target="tpu_custom_call" | custom-call | tf_op jit(solution)/shard_map/merge/pallas_call | solution.py:468
  10.6 0.7 %collective-permute-start.7 = (f32[136,128]{1,0:T(8,128)S(1)}, f32[136,128]{1,0:T(8,128)S(1)}, u32[]{:S(2)}, u32[]{:S(2)}) collective-permute-start(f32[136,128]{1,0:T(8,128)S(1)} %merge.1.own_ref), channel_id=1, source_target_pairs={{0,10},{1,11},{2,8},{3,9},{4,14},{5,15},{6,12},{7,13},{8,2},{9,3},... | collective-permute-start | bytes 208904 | tf_op jit(solution)/shard_map/ppermute | solution.py:417
  11.4 1.9 %collective-permute-start.2 = (f32[16,2,8,128]{3,2,1,0:T(8,128)S(1)}, f32[16,2,8,128]{3,2,1,0:T(8,128)S(1)}, u32[]{:S(2)}, u32[]{:S(2)}) collective-permute-start(f32[16,2,8,128]{3,2,1,0:T(8,128)S(1)} %get-tuple-element.23), channel_id=1, source_target_pairs={{0,8},{1,9},{2,10},{3,11},{4,12},{5,13},{6,14},{7,15},{8,0},{9,1},... | collective-permute-start | bytes 393224 | tf_op jit(solution)/shard_map/ppermute | solution.py:417
  13.3 1.5 %collective-permute-start.3 = (f32[16,2,8,128]{3,2,1,0:T(8,128)S(1)}, f32[16,2,8,128]{3,2,1,0:T(8,128)S(1)}, u32[]{:S(2)}, u32[]{:S(2)}) collective-permute-start(f32[16,2,8,128]{3,2,1,0:T(8,128)S(1)} %get-tuple-element.22), channel_id=1, source_target_pairs={{0,16},{1,17},{2,18},{3,19},{4,20},{5,21},{6,22},{7,23},{8,24},{9,... | collective-permute-start | bytes 393224 | tf_op jit(solution)/shard_map/ppermute | solution.py:417
  14.8 0.0 collective-permute-start.4
  14.8 0.0 collective-permute-done.7.message_ref.neighbour_ref
  14.8 0.7 %collective-permute-start.8 = (f32[264,128]{1,0:T(8,128)S(1)}, f32[264,128]{1,0:T(8,128)S(1)}, u32[]{:S(2)}, u32[]{:S(2)}) collective-permute-start(f32[264,128]{1,0:T(8,128)S(1)} %pad_maximum_fusion), channel_id=1, source_target_pairs={{0,8},{1,9},{2,10},{3,11},{4,12},{5,13},{6,14},{7,15},{8,0},{9,1},... | collective-permute-start | bytes 405512 | tf_op jit(solution)/shard_map/ppermute | solution.py:417
  15.5 0.0 collective-permute-done.2.rest_1_
  15.5 4.1 %collective-permute-done.3.rest_2_ = f32[16,2,8,128]{3,2,1,0:T(8,128)S(1)} collective-permute-done((f32[16,2,8,128]{3,2,1,0:T(8,128)S(1)}, f32[16,2,8,128]{3,2,1,0:T(8,128)S(1)}, u32[]{:S(2)}, u32[]{:S(2)}) %collective-permute-start.3) | collective-permute-done | bytes 131104 | tf_op jit(solution)/shard_map/ppermute | solution.py:417
  19.6 1.0 %collective-permute-done.4.rest_3_ = f32[16,2,8,128]{3,2,1,0:T(8,128)S(1)} collective-permute-done((f32[16,2,8,128]{3,2,1,0:T(8,128)S(1)}, f32[16,2,8,128]{3,2,1,0:T(8,128)S(1)}, u32[]{:S(2)}, u32[]{:S(2)}) %collective-permute-start.4) | collective-permute-done | bytes 131104 | tf_op jit(solution)/shard_map/ppermute | solution.py:417
  20.7 0.6 %prepare.1 = (f32[16,2,32,128]{3,2,1,0:T(8,128)S(1)}, f32[16,32,128]{2,1,0:T(8,128)S(1)}, f32[16,32,128]{2,1,0:T(8,128)S(1)}, f32[3,160,128]{2,1,0:T(8,128)S(1)}) custom-call(f32[32,128]{1,0:T(8,128)S(1)} %slice_bitcast_fusion.10.spectral_ref, f32[8,128]{1,0:T(8,128)S(1)} %get-tuple-element.14.table_ref, f32[72,128]{1,0:T(8,128)S(1)} %collective-permute-done.1.side_ref, ...), custom_call_target="tpu_custom_call" | custom-call | tf_op jit(solution)/shard_map/prepare/pallas_call | solution.py:495
  21.3 0.4 %quad.1 = f32[96,128]{1,0:T(8,128)S(1)} custom-call(f32[32,128]{1,0:T(8,128)S(1)} %bitcast_select_fusion.spectral_ref, f32[136,128]{1,0:T(8,128)S(1)} %merge.1.own_ref, f32[136,128]{1,0:T(8,128)S(1)} %collective-permute-done.7.message_ref.neighbour_ref), custom_call_target="tpu_custom_call" | custom-call | tf_op jit(solution)/shard_map/quad/pallas_call | solution.py:477
  21.7 3.0 %collective-permute-start.9 = (f32[96,128]{1,0:T(8,128)S(1)}, f32[96,128]{1,0:T(8,128)S(1)}, u32[]{:S(2)}, u32[]{:S(2)}) collective-permute-start(f32[96,128]{1,0:T(8,128)S(1)} %quad.1), channel_id=1, source_target_pairs={{0,12},{1,13},{2,6},{3,7},{4,8},{5,9},{6,2},{7,3},{8,4},{9,5},{10,... | collective-permute-start | bytes 147464 | tf_op jit(solution)/shard_map/ppermute | solution.py:417
  24.6 0.3 %levels.1.neighbour_map = f32[160,128]{1,0:T(8,128)S(1)} custom-call(f32[32,128]{1,0:T(8,128)S(1)} %slice_bitcast_fusion.10.spectral_ref, f32[136,128]{1,0:T(8,128)S(1)} %collective-permute-done.7.message_ref.neighbour_ref), custom_call_target="tpu_custom_call" | custom-call | tf_op jit(solution)/shard_map/levels/pallas_call | solution.py:512
  25.0 0.0 collective-permute-done.8
  25.0 2.7 %collective-permute-done.9.other_ref = f32[96,128]{1,0:T(8,128)S(1)} collective-permute-done((f32[96,128]{1,0:T(8,128)S(1)}, f32[96,128]{1,0:T(8,128)S(1)}, u32[]{:S(2)}, u32[]{:S(2)}) %collective-permute-start.9) | collective-permute-done | bytes 49184 | tf_op jit(solution)/shard_map/ppermute | solution.py:417
  27.7 1.0 %solve.1 = f32[16,2,4,8,128]{4,3,2,1,0:T(8,128)} custom-call(f32[16,2,32,128]{3,2,1,0:T(8,128)S(1)} %get-tuple-element.17.part_ref, f32[16,32,128]{2,1,0:T(8,128)S(1)} %get-tuple-element.18.low_ref, f32[16,32,128]{2,1,0:T(8,128)S(1)} %get-tuple-element.19.high_ref, f32[3,160,128]{2,1,0:T(8,128)S(1)} %get-tuple-element.20.maps_ref, ...), custom_call_target="tpu_custom_call" | custom-call | tf_op jit(solution)/shard_map/solve/pallas_call | solution.py:526
  (14 shorter events, 0.1 us)
Async XLA Ops:
  1.2 1.5 %collective-permute-start = (f32[2,2,32,128]{3,2,1,0:T(8,128)S(1)}, f32[2,2,32,128]{3,2,1,0:T(8,128)S(1)}, u32[]{:S(2)}, u32[]{:S(2)}) collective-permute-start(f32[2,2,32,128]{3,2,1,0:T(8,128)S(1)} %get-tuple-element.15), channel_id=1, source_target_pairs={{0,8},{1,9},{2,10},{3,11},{4,12},{5,13},{6,14},{7,15},{8,0},{9,1},... | collective-permute-start | bytes 196616 | tf_op jit(solution)/shard_map/ppermute | solution.py:417
  2.7 4.3 %collective-permute-start.5 = (f32[64,128]{1,0:T(8,128)S(1)}, f32[64,128]{1,0:T(8,128)S(1)}, u32[]{:S(2)}, u32[]{:S(2)}) collective-permute-start(f32[64,128]{1,0:T(8,128)S(1)} %pad_maximum_fusion.2), channel_id=1, source_target_pairs={{0,24},{1,25},{2,18},{3,19},{4,28},{5,29},{6,22},{7,23},{8,16},{9,... | collective-permute-start | bytes 98312 | tf_op jit(solution)/shard_map/ppermute | solution.py:417
  5.4 4.2 %collective-permute-start.6 = (f32[64,128]{1,0:T(8,128)S(1)}, f32[64,128]{1,0:T(8,128)S(1)}, u32[]{:S(2)}, u32[]{:S(2)}) collective-permute-start(f32[64,128]{1,0:T(8,128)S(1)} %pad_maximum_fusion.2), channel_id=1, source_target_pairs={{0,25},{1,24},{2,19},{3,18},{4,29},{5,28},{6,23},{7,22},{8,17},{9,... | collective-permute-start | bytes 98312 | tf_op jit(solution)/shard_map/ppermute | solution.py:417
  6.8 3.4 %collective-permute-start.1 = (f32[72,128]{1,0:T(8,128)S(1)}, f32[72,128]{1,0:T(8,128)S(1)}, u32[]{:S(2)}, u32[]{:S(2)}) collective-permute-start(f32[72,128]{1,0:T(8,128)S(1)} %pad_maximum_fusion.1), channel_id=1, source_target_pairs={{0,9},{1,8},{2,3},{3,2},{4,13},{5,12},{6,7},{7,6},{8,1},{9,0},{10,... | collective-permute-start | bytes 110600 | tf_op jit(solution)/shard_map/ppermute | solution.py:417
  10.6 4.2 %collective-permute-start.7 = (f32[136,128]{1,0:T(8,128)S(1)}, f32[136,128]{1,0:T(8,128)S(1)}, u32[]{:S(2)}, u32[]{:S(2)}) collective-permute-start(f32[136,128]{1,0:T(8,128)S(1)} %merge.1.own_ref), channel_id=1, source_target_pairs={{0,10},{1,11},{2,8},{3,9},{4,14},{5,15},{6,12},{7,13},{8,2},{9,3},... | collective-permute-start | bytes 208904 | tf_op jit(solution)/shard_map/ppermute | solution.py:417
  11.4 4.1 %collective-permute-start.2 = (f32[16,2,8,128]{3,2,1,0:T(8,128)S(1)}, f32[16,2,8,128]{3,2,1,0:T(8,128)S(1)}, u32[]{:S(2)}, u32[]{:S(2)}) collective-permute-start(f32[16,2,8,128]{3,2,1,0:T(8,128)S(1)} %get-tuple-element.23), channel_id=1, source_target_pairs={{0,8},{1,9},{2,10},{3,11},{4,12},{5,13},{6,14},{7,15},{8,0},{9,1},... | collective-permute-start | bytes 393224 | tf_op jit(solution)/shard_map/ppermute | solution.py:417
  13.3 6.4 %collective-permute-start.3 = (f32[16,2,8,128]{3,2,1,0:T(8,128)S(1)}, f32[16,2,8,128]{3,2,1,0:T(8,128)S(1)}, u32[]{:S(2)}, u32[]{:S(2)}) collective-permute-start(f32[16,2,8,128]{3,2,1,0:T(8,128)S(1)} %get-tuple-element.22), channel_id=1, source_target_pairs={{0,16},{1,17},{2,18},{3,19},{4,20},{5,21},{6,22},{7,23},{8,24},{9,... | collective-permute-start | bytes 393224 | tf_op jit(solution)/shard_map/ppermute | solution.py:417
  14.8 5.9 %collective-permute-start.4 = (f32[16,2,8,128]{3,2,1,0:T(8,128)S(1)}, f32[16,2,8,128]{3,2,1,0:T(8,128)S(1)}, u32[]{:S(2)}, u32[]{:S(2)}) collective-permute-start(f32[16,2,8,128]{3,2,1,0:T(8,128)S(1)} %get-tuple-element.21), channel_id=1, source_target_pairs={{0,24},{1,25},{2,26},{3,27},{4,28},{5,29},{6,30},{7,31},{8,16},{9,... | collective-permute-start | bytes 393224 | tf_op jit(solution)/shard_map/ppermute | solution.py:417
  14.8 10.1 %collective-permute-start.8 = (f32[264,128]{1,0:T(8,128)S(1)}, f32[264,128]{1,0:T(8,128)S(1)}, u32[]{:S(2)}, u32[]{:S(2)}) collective-permute-start(f32[264,128]{1,0:T(8,128)S(1)} %pad_maximum_fusion), channel_id=1, source_target_pairs={{0,8},{1,9},{2,10},{3,11},{4,12},{5,13},{6,14},{7,15},{8,0},{9,1},... | collective-permute-start | bytes 405512 | tf_op jit(solution)/shard_map/ppermute | solution.py:417
  21.7 6.1 %collective-permute-start.9 = (f32[96,128]{1,0:T(8,128)S(1)}, f32[96,128]{1,0:T(8,128)S(1)}, u32[]{:S(2)}, u32[]{:S(2)}) collective-permute-start(f32[96,128]{1,0:T(8,128)S(1)} %quad.1), channel_id=1, source_target_pairs={{0,12},{1,13},{2,6},{3,7},{4,8},{5,9},{6,2},{7,3},{8,4},{9,5},{10,... | collective-permute-start | bytes 147464 | tf_op jit(solution)/shard_map/ppermute | solution.py:417

commit v6 on v5

--- a/solution.py
+++ b/solution.py
@@ -260,33 +260,33 @@
     put_map(map_ref, (), spectral, *level_couplings(sizes, message_ref, spectral.shape[0], (level ^ d) > level))
 
 
-def quad_kernel(sizes, spectral_ref, own_ref, neighbour_ref, edge_ref):
+def ahead_kernel(sizes, spectral_ref, own_ref, map_ref):
+    spectral = spectral_ref[...]
+    lower = lax.axis_index("gz") // 2 < 2
+    put_map(map_ref, (), spectral, *level_couplings(sizes, own_ref, spectral.shape[0], jnp.logical_not(lower)))
+
+
+def quad_kernel(sizes, spectral_ref, map_ref, own_ref, neighbour_ref, edge_ref):
     spectral = spectral_ref[...]
     total = spectral.shape[0]
     level = lax.axis_index("gz") // 2
     lower, outer = level < 2, (level == 0) | (level == 3)
 
-    def ports(ref, at):
-        return [ref[(at + c) * total : (at + c + 1) * total, :] for c in range(2)]
-
-    def of(ref):
-        return choose(lower, ports(ref, 2), ports(ref, 0)), choose(lower, ports(ref, 0), ports(ref, 2))
-
-    own, neighbour = of(own_ref), of(neighbour_ref)
-    leave_first = choose(outer, own[0], neighbour[0])
-    leave_then, entry_then = choose(outer, neighbour[0], own[0]), choose(outer, neighbour[1], own[1])
-    own_table, neighbour_table = own_ref[4 * total :, :], neighbour_ref[4 * total :, :]
-    own_lines = jnp.where(lower, own_table[0:2], own_table[2:4])
-    neighbour_lines = jnp.where(lower, neighbour_table[0:2], neighbour_table[2:4])
-    first, then = jnp.where(outer, own_lines, neighbour_lines), jnp.where(outer, neighbour_lines, own_lines)
-    count = 2 * sizes[0]
-    one = jnp.ones_like(spectral)
-    num, den, _ = climb(spectral, one, one, couplings(first, 0, count), couplings(first, 1, count))
+    def ports(ref):
+        low, high = ([ref[(at + c) * total : (at + c + 1) * total, :] for c in range(2)] for at in (0, 2))
+        return choose(lower, high, low), choose(lower, low, high)
+
+    own, neighbour = ports(own_ref), ports(neighbour_ref)
+    own_map = map_of(map_ref, (), total)
+    one, zero = jnp.ones_like(spectral), jnp.zeros_like(spectral)
+    start = choose(outer, (own_map(0) + own_map(1), one, *own[0]), (one, one, zero, zero))
+    num, den, product = climb(
+        spectral, start[0], one, *level_couplings(sizes, neighbour_ref, total, jnp.logical_not(lower))
+    )
+    passed = (num, den, *leave_with(start, den, product, *neighbour))
+    num, den, *partial = choose(outer, passed, apply_map(own_map, passed, *own))
     scale = 1.0 / den
-    state = (num * scale, one, *leave_first)
-    num, den, product = climb(spectral, state[0], one, couplings(then, 0, count), couplings(then, 1, count))
-    scale = 1.0 / den
-    for i, value in enumerate([num, *leave_with(state, den, product, leave_then, entry_then)]):
+    for i, value in enumerate([num, *partial]):
         edge_ref[i * total : (i + 1) * total, :] = value * scale
 
 
@@ -391,6 +391,8 @@
         copy.wait()
 
 
+AWAY = (1, 0, 1, 1)
+
 LIMIT = pltpu.CompilerParams(vmem_limit_bytes=16 << 20)
 VMEM = pl.BlockSpec(memory_space=pltpu.VMEM)
 ANY = pl.BlockSpec(memory_space=pl.ANY)
@@ -446,8 +448,8 @@
     )(*near(source))
 
     quads = pairs == 4
-    even = (lax.axis_index("gz") // 2) % 2 == 0
-    swapped = (lambda z: 1 - z % 2) if quads else (lambda z: 0)
+    away = functools.reduce(lambda a, z: a | (lax.axis_index("gz") // 2 == z), [z for z in range(4) if AWAY[z]], False)
+    swapped = (lambda z: AWAY[z]) if quads else (lambda z: 0)
     if quads:
         taken = move(ports, modes_by=1)
         theirs = taken[1]
@@ -463,8 +465,8 @@
     both_spectral = spectral
     own_block, merged_spectral, spectral = blocks_out[0], spectral[0], spectral[0]
     if quads:
-        own_block = jnp.where(even, jnp.concatenate([taken[0, 0], ports[1, 0]], axis=0), own_block)
-        merged_spectral = jnp.where(even, both_spectral[1], spectral)
+        own_block = jnp.where(away, jnp.concatenate([taken[0, 0], ports[1, 0]], axis=0), own_block)
+        merged_spectral = jnp.where(away, both_spectral[1], spectral)
     message = pl.pallas_call(
         functools.partial(merge_kernel, sizes),
         out_shape=pltpu.VMEM((4 * total + SUBLANES, LANES), f32),
@@ -473,17 +475,24 @@
         name="merge",
     )(*near(merged_spectral, table, own_block, side, *own_parts, *pair_parts))
     if quads:
-        messages = [move(message, modes_by=1, level=1)]
+        messages = [move(message, level=1, core=lambda z: AWAY[z] ^ AWAY[z ^ 1])]
+        ahead = pl.pallas_call(
+            functools.partial(ahead_kernel, sizes),
+            out_shape=pltpu.VMEM((MAP_PARTS * total, LANES), f32),
+            in_specs=[VMEM] * 2,
+            out_specs=VMEM,
+            name="ahead",
+        )(*near(merged_spectral, message))
         edge = pl.pallas_call(
             functools.partial(quad_kernel, sizes),
             out_shape=pltpu.VMEM((3 * total, LANES), f32),
-            in_specs=[VMEM] * 3,
+            in_specs=[VMEM] * 4,
             out_specs=VMEM,
             name="quad",
-        )(*near(merged_spectral, message, messages[0]))
+        )(*near(merged_spectral, ahead, message, messages[0]))
         other = move(edge, level=2, core=swapped)
         parcel = jnp.concatenate([side, *pair_parts, messages[0][: 4 * total]], axis=0)
-        parcel = jnp.where(even, move(parcel, modes_by=1), parcel)
+        parcel = jnp.where(away, move(parcel, modes_by=1), parcel)
         lines = side.shape[0]
         owned = [parcel[lines * 0 : lines]]
         for d in range(1, chips):

time: 28.8 us -> 28.5 us (0.990)
  starting transfers between devices: 12.5 us -> 12 us
    ppermute x10, starting transfers between devices: 12.5 us -> 12 us  [move(): return lax.ppermute(array, ('modes', 'gz'), links)]
    pallas_call x0 -> x1, Pallas kernels: none -> 0.32 us  [solve(): pl.pallas_call(functools.partial(ahead_kernel, sizes), out_shape=pltpu.VM...]
  transfers between devices with their start and end apart: 10 -> 10, of which waited for: 7 -> 7; matrix products, arithmetic and copies ran while one was open for 0% -> 0% of each run, Pallas kernels for 5% -> 6%
where the time goes in v6:
time: 28.5 us; the launch traced here: 28.4 us
  starting transfers between devices  12 us (42%)
  waiting for transfers between devices  11.8 us (41%)
  Pallas kernels  4.3 us (15%)
    ppermute x10, starting transfers between devices, move(): return lax.ppermute(array, ('modes', 'gz'), links)  12 us
    ppermute x10, waiting for transfers between devices, move(): return lax.ppermute(array, ('modes', 'gz'), links)  11.8 us
    pallas_call x1, Pallas kernels, solve(): pl.pallas_call(functools.partial(reduce_kernel, sizes), out_shape=(pltpu....  1.24 us
    pallas_call x1, Pallas kernels, solve(): pl.pallas_call(kernel, out_shape=jax.ShapeDtypeStruct((rows, 2, mode_coun...  0.98 us
    pallas_call x1, Pallas kernels, solve(): pl.pallas_call(functools.partial(prepare_kernel, sizes), out_shape=(pltpu...  0.62 us
  transfers between devices with their start and end apart: 10, of which 7 were waited for; matrix products, arithmetic and copies ran while one was open for 0% of the time, Pallas kernels for 6%

profile of v6, /device:TPU:0, one launch (start us, length us, event | category | flops | bytes accessed | tf_op | source)
XLA Modules:
  0.0 28.4 jit_solution(6455330476188175538)
XLA Ops:
  0.0 1.2 %reduce.1 = (f32[2,2,32,128]{3,2,1,0:T(8,128)S(1)}, f32[8,128]{1,0:T(8,128)S(1)}, f32[2,32,128]{2,1,0:T(8,128)S(1)}, f32[16,2,8,512]{3,2,1,0:T(8,128)S(1)}) custom-call(f32[16]{0:T(128)} %below_hbm.1, f32[16]{0:T(128)} %above_hbm.1, f32[8]{0:T(128)} %stream_hbm.1, f32[16,128]{1,0:T(8,128)} %bitcast.32, f32[16,2,8,512]{3,2,1,0:T(8,128)} %source_hbm.1), custom_call_target="tpu_custom_call" | custom-call | tf_op jit(solution)/shard_map/reduce/pallas_call | solution.py:422
  1.2 0.6 %collective-permute-start = (f32[2,2,32,128]{3,2,1,0:T(8,128)S(1)}, f32[2,2,32,128]{3,2,1,0:T(8,128)S(1)}, u32[]{:S(2)}, u32[]{:S(2)}) collective-permute-start(f32[2,2,32,128]{3,2,1,0:T(8,128)S(1)} %get-tuple-element.15), channel_id=1, source_target_pairs={{0,8},{1,9},{2,10},{3,11},{4,12},{5,13},{6,14},{7,15},{8,0},{9,1},... | collective-permute-start | bytes 196616 | tf_op jit(solution)/shard_map/ppermute | solution.py:419
  1.8 0.2 regroup.1
  2.0 0.7 %collective-permute-done = f32[2,2,32,128]{3,2,1,0:T(8,128)S(1)} collective-permute-done((f32[2,2,32,128]{3,2,1,0:T(8,128)S(1)}, f32[2,2,32,128]{3,2,1,0:T(8,128)S(1)}, u32[]{:S(2)}, u32[]{:S(2)}) %collective-permute-start) | collective-permute-done | bytes 65568 | tf_op jit(solution)/shard_map/ppermute | solution.py:419
  2.7 2.7 %collective-permute-start.5 = (f32[64,128]{1,0:T(8,128)S(1)}, f32[64,128]{1,0:T(8,128)S(1)}, u32[]{:S(2)}, u32[]{:S(2)}) collective-permute-start(f32[64,128]{1,0:T(8,128)S(1)} %pad_maximum_fusion.2), channel_id=1, source_target_pairs={{0,24},{1,25},{2,18},{3,19},{4,28},{5,29},{6,30},{7,31},{8,16},{9,... | collective-permute-start | bytes 98312 | tf_op jit(solution)/shard_map/ppermute | solution.py:419
  5.4 1.4 %collective-permute-start.6 = (f32[64,128]{1,0:T(8,128)S(1)}, f32[64,128]{1,0:T(8,128)S(1)}, u32[]{:S(2)}, u32[]{:S(2)}) collective-permute-start(f32[64,128]{1,0:T(8,128)S(1)} %pad_maximum_fusion.2), channel_id=1, source_target_pairs={{0,25},{1,24},{2,19},{3,18},{4,29},{5,28},{6,31},{7,30},{8,17},{9,... | collective-permute-start | bytes 98312 | tf_op jit(solution)/shard_map/ppermute | solution.py:419
  6.8 0.1 collective-permute-start.1
  6.9 0.1 collective-permute-done.5.rest_0_
  7.0 2.6 %collective-permute-done.6.rest_1_ = f32[64,128]{1,0:T(8,128)S(1)} collective-permute-done((f32[64,128]{1,0:T(8,128)S(1)}, f32[64,128]{1,0:T(8,128)S(1)}, u32[]{:S(2)}, u32[]{:S(2)}) %collective-permute-start.6) | collective-permute-done | bytes 32800 | tf_op jit(solution)/shard_map/ppermute | solution.py:419
  9.6 0.6 %collective-permute-done.1.side_ref = f32[72,128]{1,0:T(8,128)S(1)} collective-permute-done((f32[72,128]{1,0:T(8,128)S(1)}, f32[72,128]{1,0:T(8,128)S(1)}, u32[]{:S(2)}, u32[]{:S(2)}) %collective-permute-start.1) | collective-permute-done | bytes 36896 | tf_op jit(solution)/shard_map/ppermute | solution.py:419
  10.2 0.4 %merge.1.own_ref = f32[136,128]{1,0:T(8,128)S(1)} custom-call(f32[32,128]{1,0:T(8,128)S(1)} %bitcast_select_fusion.spectral_ref, f32[8,128]{1,0:T(8,128)S(1)} %get-tuple-element.14.table_ref, f32[64,128]{1,0:T(8,128)S(1)} %maximum_select_fusion.own_ref, f32[72,128]{1,0:T(8,128)S(1)} %collective-permute-done.1.side_ref, ...), custom_call_target="tpu_custom_call" | custom-call | tf_op jit(solution)/shard_map/merge/pallas_call | solution.py:470
  10.6 0.7 %collective-permute-start.7 = (f32[136,128]{1,0:T(8,128)S(1)}, f32[136,128]{1,0:T(8,128)S(1)}, u32[]{:S(2)}, u32[]{:S(2)}) collective-permute-start(f32[136,128]{1,0:T(8,128)S(1)} %merge.1.own_ref), channel_id=1, source_target_pairs={{0,10},{1,11},{2,8},{3,9},{4,6},{5,7},{6,4},{7,5},{8,2},{9,3},{10,... | collective-permute-start | bytes 208904 | tf_op jit(solution)/shard_map/ppermute | solution.py:419
  11.4 1.9 %collective-permute-start.2 = (f32[16,2,8,128]{3,2,1,0:T(8,128)S(1)}, f32[16,2,8,128]{3,2,1,0:T(8,128)S(1)}, u32[]{:S(2)}, u32[]{:S(2)}) collective-permute-start(f32[16,2,8,128]{3,2,1,0:T(8,128)S(1)} %get-tuple-element.23), channel_id=1, source_target_pairs={{0,8},{1,9},{2,10},{3,11},{4,12},{5,13},{6,14},{7,15},{8,0},{9,1},... | collective-permute-start | bytes 393224 | tf_op jit(solution)/shard_map/ppermute | solution.py:419
  13.3 1.5 %collective-permute-start.3 = (f32[16,2,8,128]{3,2,1,0:T(8,128)S(1)}, f32[16,2,8,128]{3,2,1,0:T(8,128)S(1)}, u32[]{:S(2)}, u32[]{:S(2)}) collective-permute-start(f32[16,2,8,128]{3,2,1,0:T(8,128)S(1)} %get-tuple-element.22), channel_id=1, source_target_pairs={{0,16},{1,17},{2,18},{3,19},{4,20},{5,21},{6,22},{7,23},{8,24},{9,... | collective-permute-start | bytes 393224 | tf_op jit(solution)/shard_map/ppermute | solution.py:419
  14.8 0.0 collective-permute-start.4
  14.8 0.0 collective-permute-done.7.message_ref.neighbour_ref
  14.8 0.7 %collective-permute-start.8 = (f32[264,128]{1,0:T(8,128)S(1)}, f32[264,128]{1,0:T(8,128)S(1)}, u32[]{:S(2)}, u32[]{:S(2)}) collective-permute-start(f32[264,128]{1,0:T(8,128)S(1)} %pad_maximum_fusion), channel_id=1, source_target_pairs={{0,8},{1,9},{2,10},{3,11},{4,12},{5,13},{6,14},{7,15},{8,0},{9,1},... | collective-permute-start | bytes 405512 | tf_op jit(solution)/shard_map/ppermute | solution.py:419
  15.5 0.3 %ahead.1.map_ref = f32[160,128]{1,0:T(8,128)S(1)} custom-call(f32[32,128]{1,0:T(8,128)S(1)} %bitcast_select_fusion.spectral_ref, f32[136,128]{1,0:T(8,128)S(1)} %merge.1.own_ref), custom_call_target="tpu_custom_call" | custom-call | tf_op jit(solution)/shard_map/ahead/pallas_call | solution.py:479
  15.8 0.0 collective-permute-done.2.rest_1_
  15.9 3.8 %collective-permute-done.3.rest_2_ = f32[16,2,8,128]{3,2,1,0:T(8,128)S(1)} collective-permute-done((f32[16,2,8,128]{3,2,1,0:T(8,128)S(1)}, f32[16,2,8,128]{3,2,1,0:T(8,128)S(1)}, u32[]{:S(2)}, u32[]{:S(2)}) %collective-permute-start.3) | collective-permute-done | bytes 131104 | tf_op jit(solution)/shard_map/ppermute | solution.py:419
  19.6 1.0 %collective-permute-done.4.rest_3_ = f32[16,2,8,128]{3,2,1,0:T(8,128)S(1)} collective-permute-done((f32[16,2,8,128]{3,2,1,0:T(8,128)S(1)}, f32[16,2,8,128]{3,2,1,0:T(8,128)S(1)}, u32[]{:S(2)}, u32[]{:S(2)}) %collective-permute-start.4) | collective-permute-done | bytes 131104 | tf_op jit(solution)/shard_map/ppermute | solution.py:419
  20.7 0.6 %prepare.1 = (f32[16,2,32,128]{3,2,1,0:T(8,128)S(1)}, f32[16,32,128]{2,1,0:T(8,128)S(1)}, f32[16,32,128]{2,1,0:T(8,128)S(1)}, f32[3,160,128]{2,1,0:T(8,128)S(1)}) custom-call(f32[32,128]{1,0:T(8,128)S(1)} %slice_bitcast_fusion.10.spectral_ref, f32[8,128]{1,0:T(8,128)S(1)} %get-tuple-element.14.table_ref, f32[72,128]{1,0:T(8,128)S(1)} %collective-permute-done.1.side_ref, ...), custom_call_target="tpu_custom_call" | custom-call | tf_op jit(solution)/shard_map/prepare/pallas_call | solution.py:504
  21.3 0.3 quad.1
  21.6 2.5 %collective-permute-start.9 = (f32[96,128]{1,0:T(8,128)S(1)}, f32[96,128]{1,0:T(8,128)S(1)}, u32[]{:S(2)}, u32[]{:S(2)}) collective-permute-start(f32[96,128]{1,0:T(8,128)S(1)} %quad.1), channel_id=1, source_target_pairs={{0,12},{1,13},{2,6},{3,7},{4,8},{5,9},{6,10},{7,11},{8,4},{9,5},{1... | collective-permute-start | bytes 147464 | tf_op jit(solution)/shard_map/ppermute | solution.py:419
  24.1 0.3 %levels.1.neighbour_map = f32[160,128]{1,0:T(8,128)S(1)} custom-call(f32[32,128]{1,0:T(8,128)S(1)} %slice_bitcast_fusion.10.spectral_ref, f32[136,128]{1,0:T(8,128)S(1)} %collective-permute-done.7.message_ref.neighbour_ref), custom_call_target="tpu_custom_call" | custom-call | tf_op jit(solution)/shard_map/levels/pallas_call | solution.py:521
  24.4 0.0 collective-permute-done.8
  24.5 2.9 %collective-permute-done.9.other_ref = f32[96,128]{1,0:T(8,128)S(1)} collective-permute-done((f32[96,128]{1,0:T(8,128)S(1)}, f32[96,128]{1,0:T(8,128)S(1)}, u32[]{:S(2)}, u32[]{:S(2)}) %collective-permute-start.9) | collective-permute-done | bytes 49184 | tf_op jit(solution)/shard_map/ppermute | solution.py:419
  27.4 1.0 %solve.1 = f32[16,2,4,8,128]{4,3,2,1,0:T(8,128)} custom-call(f32[16,2,32,128]{3,2,1,0:T(8,128)S(1)} %get-tuple-element.17.part_ref, f32[16,32,128]{2,1,0:T(8,128)S(1)} %get-tuple-element.18.low_ref, f32[16,32,128]{2,1,0:T(8,128)S(1)} %get-tuple-element.19.high_ref, f32[3,160,128]{2,1,0:T(8,128)S(1)} %get-tuple-element.20.maps_ref, ...), custom_call_target="tpu_custom_call" | custom-call | tf_op jit(solution)/shard_map/solve/pallas_call | solution.py:535
  (14 shorter events, 0.1 us)
Async XLA Ops:
  1.2 1.5 %collective-permute-start = (f32[2,2,32,128]{3,2,1,0:T(8,128)S(1)}, f32[2,2,32,128]{3,2,1,0:T(8,128)S(1)}, u32[]{:S(2)}, u32[]{:S(2)}) collective-permute-start(f32[2,2,32,128]{3,2,1,0:T(8,128)S(1)} %get-tuple-element.15), channel_id=1, source_target_pairs={{0,8},{1,9},{2,10},{3,11},{4,12},{5,13},{6,14},{7,15},{8,0},{9,1},... | collective-permute-start | bytes 196616 | tf_op jit(solution)/shard_map/ppermute | solution.py:419
  2.7 4.3 %collective-permute-start.5 = (f32[64,128]{1,0:T(8,128)S(1)}, f32[64,128]{1,0:T(8,128)S(1)}, u32[]{:S(2)}, u32[]{:S(2)}) collective-permute-start(f32[64,128]{1,0:T(8,128)S(1)} %pad_maximum_fusion.2), channel_id=1, source_target_pairs={{0,24},{1,25},{2,18},{3,19},{4,28},{5,29},{6,30},{7,31},{8,16},{9,... | collective-permute-start | bytes 98312 | tf_op jit(solution)/shard_map/ppermute | solution.py:419
  5.4 4.2 %collective-permute-start.6 = (f32[64,128]{1,0:T(8,128)S(1)}, f32[64,128]{1,0:T(8,128)S(1)}, u32[]{:S(2)}, u32[]{:S(2)}) collective-permute-start(f32[64,128]{1,0:T(8,128)S(1)} %pad_maximum_fusion.2), channel_id=1, source_target_pairs={{0,25},{1,24},{2,19},{3,18},{4,29},{5,28},{6,31},{7,30},{8,17},{9,... | collective-permute-start | bytes 98312 | tf_op jit(solution)/shard_map/ppermute | solution.py:419
  6.8 3.4 %collective-permute-start.1 = (f32[72,128]{1,0:T(8,128)S(1)}, f32[72,128]{1,0:T(8,128)S(1)}, u32[]{:S(2)}, u32[]{:S(2)}) collective-permute-start(f32[72,128]{1,0:T(8,128)S(1)} %pad_maximum_fusion.1), channel_id=1, source_target_pairs={{0,9},{1,8},{2,3},{3,2},{4,13},{5,12},{6,15},{7,14},{8,1},{9,0},{1... | collective-permute-start | bytes 110600 | tf_op jit(solution)/shard_map/ppermute | solution.py:419
  10.6 4.2 %collective-permute-start.7 = (f32[136,128]{1,0:T(8,128)S(1)}, f32[136,128]{1,0:T(8,128)S(1)}, u32[]{:S(2)}, u32[]{:S(2)}) collective-permute-start(f32[136,128]{1,0:T(8,128)S(1)} %merge.1.own_ref), channel_id=1, source_target_pairs={{0,10},{1,11},{2,8},{3,9},{4,6},{5,7},{6,4},{7,5},{8,2},{9,3},{10,... | collective-permute-start | bytes 208904 | tf_op jit(solution)/shard_map/ppermute | solution.py:419
  11.4 4.5 %collective-permute-start.2 = (f32[16,2,8,128]{3,2,1,0:T(8,128)S(1)}, f32[16,2,8,128]{3,2,1,0:T(8,128)S(1)}, u32[]{:S(2)}, u32[]{:S(2)}) collective-permute-start(f32[16,2,8,128]{3,2,1,0:T(8,128)S(1)} %get-tuple-element.23), channel_id=1, source_target_pairs={{0,8},{1,9},{2,10},{3,11},{4,12},{5,13},{6,14},{7,15},{8,0},{9,1},... | collective-permute-start | bytes 393224 | tf_op jit(solution)/shard_map/ppermute | solution.py:419
  13.3 6.4 %collective-permute-start.3 = (f32[16,2,8,128]{3,2,1,0:T(8,128)S(1)}, f32[16,2,8,128]{3,2,1,0:T(8,128)S(1)}, u32[]{:S(2)}, u32[]{:S(2)}) collective-permute-start(f32[16,2,8,128]{3,2,1,0:T(8,128)S(1)} %get-tuple-element.22), channel_id=1, source_target_pairs={{0,16},{1,17},{2,18},{3,19},{4,20},{5,21},{6,22},{7,23},{8,24},{9,... | collective-permute-start | bytes 393224 | tf_op jit(solution)/shard_map/ppermute | solution.py:419
  14.8 5.9 %collective-permute-start.4 = (f32[16,2,8,128]{3,2,1,0:T(8,128)S(1)}, f32[16,2,8,128]{3,2,1,0:T(8,128)S(1)}, u32[]{:S(2)}, u32[]{:S(2)}) collective-permute-start(f32[16,2,8,128]{3,2,1,0:T(8,128)S(1)} %get-tuple-element.21), channel_id=1, source_target_pairs={{0,24},{1,25},{2,26},{3,27},{4,28},{5,29},{6,30},{7,31},{8,16},{9,... | collective-permute-start | bytes 393224 | tf_op jit(solution)/shard_map/ppermute | solution.py:419
  14.8 9.5 %collective-permute-start.8 = (f32[264,128]{1,0:T(8,128)S(1)}, f32[264,128]{1,0:T(8,128)S(1)}, u32[]{:S(2)}, u32[]{:S(2)}) collective-permute-start(f32[264,128]{1,0:T(8,128)S(1)} %pad_maximum_fusion), channel_id=1, source_target_pairs={{0,8},{1,9},{2,10},{3,11},{4,12},{5,13},{6,14},{7,15},{8,0},{9,1},... | collective-permute-start | bytes 405512 | tf_op jit(solution)/shard_map/ppermute | solution.py:419
  21.6 5.8 %collective-permute-start.9 = (f32[96,128]{1,0:T(8,128)S(1)}, f32[96,128]{1,0:T(8,128)S(1)}, u32[]{:S(2)}, u32[]{:S(2)}) collective-permute-start(f32[96,128]{1,0:T(8,128)S(1)} %quad.1), channel_id=1, source_target_pairs={{0,12},{1,13},{2,6},{3,7},{4,8},{5,9},{6,10},{7,11},{8,4},{9,5},{1... | collective-permute-start | bytes 147464 | tf_op jit(solution)/shard_map/ppermute | solution.py:419

commit v7 on v6

--- a/solution.py
+++ b/solution.py
@@ -161,7 +161,13 @@
     return lambda i: ref[(*lead, slice(i * total, (i + 1) * total), slice(None))]
 
 
-def merge_kernel(sizes, spectral_ref, table_ref, own_ref, side_ref, *rest):
+def locals_kernel(sizes, spectral_ref, table_ref, maps_ref):
+    spectral, table = spectral_ref[...], table_ref[...]
+    for i in range(2):
+        put_map(maps_ref, (i,), spectral, *(couplings(table, 2 * i + j, sizes[0]) for j in range(2)))
+
+
+def merge_kernel(sizes, spectral_ref, table_ref, maps_ref, own_ref, side_ref, *rest):
     rows, _, _, _, mode_count, height = sizes
     chips = mode_count // 2
     own_refs, pair_refs, message_ref = rest[: chips - 1], rest[chips - 1 : 2 * (chips - 1)], rest[-1]
@@ -169,17 +175,12 @@
     port = 4 * height
     upside = lax.axis_index("gz") % 2 == 1
 
-    def gather(i, chunk):
-        return jnp.concatenate([chunk(d, i * height) for d in range(mode_count)], axis=0)
-
-    def own_chunk(d, at):
-        start = (d % 2) * port + at
-        return (own_ref if d < 2 else own_refs[d // 2 - 1])[start : start + height, :]
-
-    def pair_chunk(d, at):
-        start = (d % 2) * port + at
-        ref = side_ref if d < 2 else pair_refs[d // 2 - 1]
-        return ref[start : start + height, :]
+    def gather(first_ref, refs, i):
+        chunks = []
+        for d in range(mode_count):
+            start = i * height + (d % 2) * port
+            chunks.append((first_ref if d < 2 else refs[d // 2 - 1])[start : start + height, :])
+        return jnp.concatenate(chunks, axis=0)
 
     own_table, pair_table = table_ref[...], side_ref[2 * port :, :]
     low_table = jnp.where(upside, pair_table, own_table)
@@ -191,23 +192,24 @@
     message_ref[4 * total :, :] = jnp.where(lane < rows, ahead, pltpu.roll(behind, rows, 1))
     spectral = spectral_ref[...]
     one = jnp.ones((total, LANES), jnp.float32)
-    own = [gather(i, own_chunk) for i in range(4)]
-    pair = [gather(i, pair_chunk) for i in range(4)]
-    low = [jnp.where(upside, b, a) for a, b in zip(own, pair)]
-    high = [jnp.where(upside, a, b) for a, b in zip(own, pair)]
-
-    def store(i, value):
+    own = [gather(own_ref, own_refs, i) for i in range(4)]
+    pair = [gather(side_ref, pair_refs, i) for i in range(4)]
+    far_own, near_own = choose(upside, own[:2], own[2:]), choose(upside, own[2:], own[:2])
+    far_pair, near_pair = choose(upside, pair[:2], pair[2:]), choose(upside, pair[2:], pair[:2])
+    away_lines = jnp.where(upside, pair_table[2:4], pair_table[0:2])
+    back_lines = jnp.where(upside, pair_table[0:2], pair_table[2:4])
+    turn = lax.axis_index("gz") % 2
+    away_map, back_map = map_of(maps_ref, (turn,), total), map_of(maps_ref, (1 - turn,), total)
+    state = (away_map(0) + away_map(1), one, *far_own)
+    num, den, product = climb(spectral, state[0], one, *(couplings(away_lines, i, rows) for i in range(2)))
+    scale = 1.0 / den
+    away = [value * scale for value in leave_with(state, den, product, far_pair, near_pair)]
+    num, den, _ = climb(spectral, one, one, *(couplings(back_lines, i, rows) for i in range(2)))
+    state = apply_map(back_map, (num, den, *(value * den for value in near_pair)), near_own, far_own)
+    scale = 1.0 / state[1]
+    back = [value * scale for value in state[2:]]
+    for i, value in enumerate([*choose(upside, away, back), *choose(upside, back, away)]):
         message_ref[i * total : (i + 1) * total, :] = value
-
-    for near_line, first, second, near_side, far_side in ((0, low_table, high_table, 0, 2), (2, high_table, low_table, 2, 0)):
-        lines = (near_line, near_line + 1)
-        num, den, _ = climb(spectral, one, one, *(couplings(first, i, rows) for i in lines))
-        passed = (den - num) / den
-        _, den_all, product = climb(spectral, num, den, *(couplings(second, i, rows) for i in lines))
-        ratio = product * den / den_all
-        before, after = (low, high) if near_line == 0 else (high, low)
-        for c in range(2):
-            store(far_side + c, after[far_side + c] + ratio * (before[far_side + c] + passed * after[near_side + c]))
 
 
 def prepare_kernel(sizes, spectral_ref, table_ref, side_ref, *rest):
@@ -467,13 +469,20 @@
     if quads:
         own_block = jnp.where(away, jnp.concatenate([taken[0, 0], ports[1, 0]], axis=0), own_block)
         merged_spectral = jnp.where(away, both_spectral[1], spectral)
+    local_maps = pl.pallas_call(
+        functools.partial(locals_kernel, sizes),
+        out_shape=pltpu.VMEM((2, MAP_PARTS * total, LANES), f32),
+        in_specs=[VMEM] * 2,
+        out_specs=VMEM,
+        name="locals",
+    )(*near(merged_spectral, table))
     message = pl.pallas_call(
         functools.partial(merge_kernel, sizes),
         out_shape=pltpu.VMEM((4 * total + SUBLANES, LANES), f32),
-        in_specs=[VMEM] * (4 + 2 * (chips - 1)),
+        in_specs=[VMEM] * (5 + 2 * (chips - 1)),
         out_specs=VMEM,
         name="merge",
-    )(*near(merged_spectral, table, own_block, side, *own_parts, *pair_parts))
+    )(*near(merged_spectral, table, local_maps, own_block, side, *own_parts, *pair_parts))
     if quads:
         messages = [move(message, level=1, core=lambda z: AWAY[z] ^ AWAY[z ^ 1])]
         ahead = pl.pallas_call(

time: 28.5 us -> 28.4 us (level)
  waiting for transfers between devices: 11.8 us -> 11.5 us
    ppermute x10, waiting for transfers between devices: 11.8 us -> 11.5 us  [move(): return lax.ppermute(array, ('modes', 'gz'), links)]
    pallas_call x0 -> x1, Pallas kernels: none -> 0.32 us  [solve(): pl.pallas_call(functools.partial(locals_kernel, sizes), out_shape=pltpu.V...]
  transfers between devices with their start and end apart: 10 -> 10, of which waited for: 7 -> 7; matrix products, arithmetic and copies ran while one was open for 0% -> 0% of each run, Pallas kernels for 6% -> 7%
where the time goes in v7:
time: 28.4 us; the launch traced here: 28.3 us
  starting transfers between devices  12 us (42%)
  waiting for transfers between devices  11.5 us (40%)
  Pallas kernels  4.5 us (16%)
    ppermute x10, starting transfers between devices, move(): return lax.ppermute(array, ('modes', 'gz'), links)  12 us
    ppermute x10, waiting for transfers between devices, move(): return lax.ppermute(array, ('modes', 'gz'), links)  11.5 us
    pallas_call x1, Pallas kernels, solve(): pl.pallas_call(functools.partial(reduce_kernel, sizes), out_shape=(pltpu....  1.24 us
    pallas_call x1, Pallas kernels, solve(): pl.pallas_call(kernel, out_shape=jax.ShapeDtypeStruct((rows, 2, mode_coun...  0.98 us
    pallas_call x1, Pallas kernels, solve(): pl.pallas_call(functools.partial(prepare_kernel, sizes), out_shape=(pltpu...  0.61 us
  transfers between devices with their start and end apart: 10, of which 7 were waited for; matrix products, arithmetic and copies ran while one was open for 0% of the time, Pallas kernels for 7%

profile of v7, /device:TPU:0, one launch (start us, length us, event | category | flops | bytes accessed | tf_op | source)
XLA Modules:
  0.0 28.3 jit_solution(14677442933318784526)
XLA Ops:
  0.0 1.2 %reduce.1 = (f32[2,2,32,128]{3,2,1,0:T(8,128)S(1)}, f32[8,128]{1,0:T(8,128)S(1)}, f32[2,32,128]{2,1,0:T(8,128)S(1)}, f32[16,2,8,512]{3,2,1,0:T(8,128)S(1)}) custom-call(f32[16]{0:T(128)} %below_hbm.1, f32[16]{0:T(128)} %above_hbm.1, f32[8]{0:T(128)} %stream_hbm.1, f32[16,128]{1,0:T(8,128)} %bitcast.32, f32[16,2,8,512]{3,2,1,0:T(8,128)} %source_hbm.1), custom_call_target="tpu_custom_call" | custom-call | tf_op jit(solution)/shard_map/reduce/pallas_call | solution.py:424
  1.2 0.6 %collective-permute-start = (f32[2,2,32,128]{3,2,1,0:T(8,128)S(1)}, f32[2,2,32,128]{3,2,1,0:T(8,128)S(1)}, u32[]{:S(2)}, u32[]{:S(2)}) collective-permute-start(f32[2,2,32,128]{3,2,1,0:T(8,128)S(1)} %get-tuple-element.15), channel_id=1, source_target_pairs={{0,8},{1,9},{2,10},{3,11},{4,12},{5,13},{6,14},{7,15},{8,0},{9,1},... | collective-permute-start | bytes 196616 | tf_op jit(solution)/shard_map/ppermute | solution.py:421
  1.8 0.2 regroup.1
  2.0 0.3 %locals.1.maps_ref = f32[2,160,128]{2,1,0:T(8,128)S(1)} custom-call(f32[32,128]{1,0:T(8,128)S(1)} %bitcast_select_fusion.spectral_ref, f32[8,128]{1,0:T(8,128)S(1)} %get-tuple-element.14.table_ref), custom_call_target="tpu_custom_call" | custom-call | tf_op jit(solution)/shard_map/locals/pallas_call | solution.py:472
  2.3 0.4 %collective-permute-done = f32[2,2,32,128]{3,2,1,0:T(8,128)S(1)} collective-permute-done((f32[2,2,32,128]{3,2,1,0:T(8,128)S(1)}, f32[2,2,32,128]{3,2,1,0:T(8,128)S(1)}, u32[]{:S(2)}, u32[]{:S(2)}) %collective-permute-start) | collective-permute-done | bytes 65568 | tf_op jit(solution)/shard_map/ppermute | solution.py:421
  2.7 2.7 %collective-permute-start.5 = (f32[64,128]{1,0:T(8,128)S(1)}, f32[64,128]{1,0:T(8,128)S(1)}, u32[]{:S(2)}, u32[]{:S(2)}) collective-permute-start(f32[64,128]{1,0:T(8,128)S(1)} %pad_maximum_fusion.2), channel_id=1, source_target_pairs={{0,24},{1,25},{2,18},{3,19},{4,28},{5,29},{6,30},{7,31},{8,16},{9,... | collective-permute-start | bytes 98312 | tf_op jit(solution)/shard_map/ppermute | solution.py:421
  5.4 1.4 %collective-permute-start.6 = (f32[64,128]{1,0:T(8,128)S(1)}, f32[64,128]{1,0:T(8,128)S(1)}, u32[]{:S(2)}, u32[]{:S(2)}) collective-permute-start(f32[64,128]{1,0:T(8,128)S(1)} %pad_maximum_fusion.2), channel_id=1, source_target_pairs={{0,25},{1,24},{2,19},{3,18},{4,29},{5,28},{6,31},{7,30},{8,17},{9,... | collective-permute-start | bytes 98312 | tf_op jit(solution)/shard_map/ppermute | solution.py:421
  6.8 0.1 collective-permute-start.1
  6.9 0.1 collective-permute-done.5.rest_0_
  7.0 2.6 %collective-permute-done.6.rest_1_ = f32[64,128]{1,0:T(8,128)S(1)} collective-permute-done((f32[64,128]{1,0:T(8,128)S(1)}, f32[64,128]{1,0:T(8,128)S(1)}, u32[]{:S(2)}, u32[]{:S(2)}) %collective-permute-start.6) | collective-permute-done | bytes 32800 | tf_op jit(solution)/shard_map/ppermute | solution.py:421
  9.6 0.6 %collective-permute-done.1.side_ref = f32[72,128]{1,0:T(8,128)S(1)} collective-permute-done((f32[72,128]{1,0:T(8,128)S(1)}, f32[72,128]{1,0:T(8,128)S(1)}, u32[]{:S(2)}, u32[]{:S(2)}) %collective-permute-start.1) | collective-permute-done | bytes 36896 | tf_op jit(solution)/shard_map/ppermute | solution.py:421
  10.2 0.3 merge.1.own_ref
  10.5 0.7 %collective-permute-start.7 = (f32[136,128]{1,0:T(8,128)S(1)}, f32[136,128]{1,0:T(8,128)S(1)}, u32[]{:S(2)}, u32[]{:S(2)}) collective-permute-start(f32[136,128]{1,0:T(8,128)S(1)} %merge.1.own_ref), channel_id=1, source_target_pairs={{0,10},{1,11},{2,8},{3,9},{4,6},{5,7},{6,4},{7,5},{8,2},{9,3},{10,... | collective-permute-start | bytes 208904 | tf_op jit(solution)/shard_map/ppermute | solution.py:421
  11.3 1.9 %collective-permute-start.2 = (f32[16,2,8,128]{3,2,1,0:T(8,128)S(1)}, f32[16,2,8,128]{3,2,1,0:T(8,128)S(1)}, u32[]{:S(2)}, u32[]{:S(2)}) collective-permute-start(f32[16,2,8,128]{3,2,1,0:T(8,128)S(1)} %get-tuple-element.23), channel_id=1, source_target_pairs={{0,8},{1,9},{2,10},{3,11},{4,12},{5,13},{6,14},{7,15},{8,0},{9,1},... | collective-permute-start | bytes 393224 | tf_op jit(solution)/shard_map/ppermute | solution.py:421
  13.2 1.5 %collective-permute-start.3 = (f32[16,2,8,128]{3,2,1,0:T(8,128)S(1)}, f32[16,2,8,128]{3,2,1,0:T(8,128)S(1)}, u32[]{:S(2)}, u32[]{:S(2)}) collective-permute-start(f32[16,2,8,128]{3,2,1,0:T(8,128)S(1)} %get-tuple-element.22), channel_id=1, source_target_pairs={{0,16},{1,17},{2,18},{3,19},{4,20},{5,21},{6,22},{7,23},{8,24},{9,... | collective-permute-start | bytes 393224 | tf_op jit(solution)/shard_map/ppermute | solution.py:421
  14.7 0.0 collective-permute-start.4
  14.7 0.0 collective-permute-done.7.message_ref.neighbour_ref
  14.7 0.7 %collective-permute-start.8 = (f32[264,128]{1,0:T(8,128)S(1)}, f32[264,128]{1,0:T(8,128)S(1)}, u32[]{:S(2)}, u32[]{:S(2)}) collective-permute-start(f32[264,128]{1,0:T(8,128)S(1)} %pad_maximum_fusion), channel_id=1, source_target_pairs={{0,8},{1,9},{2,10},{3,11},{4,12},{5,13},{6,14},{7,15},{8,0},{9,1},... | collective-permute-start | bytes 405512 | tf_op jit(solution)/shard_map/ppermute | solution.py:421
  15.4 0.3 %ahead.1.map_ref = f32[160,128]{1,0:T(8,128)S(1)} custom-call(f32[32,128]{1,0:T(8,128)S(1)} %bitcast_select_fusion.spectral_ref, f32[136,128]{1,0:T(8,128)S(1)} %merge.1.own_ref), custom_call_target="tpu_custom_call" | custom-call | tf_op jit(solution)/shard_map/ahead/pallas_call | solution.py:488
  15.7 0.0 collective-permute-done.2.rest_1_
  15.7 3.8 %collective-permute-done.3.rest_2_ = f32[16,2,8,128]{3,2,1,0:T(8,128)S(1)} collective-permute-done((f32[16,2,8,128]{3,2,1,0:T(8,128)S(1)}, f32[16,2,8,128]{3,2,1,0:T(8,128)S(1)}, u32[]{:S(2)}, u32[]{:S(2)}) %collective-permute-start.3) | collective-permute-done | bytes 131104 | tf_op jit(solution)/shard_map/ppermute | solution.py:421
  19.5 1.0 %collective-permute-done.4.rest_3_ = f32[16,2,8,128]{3,2,1,0:T(8,128)S(1)} collective-permute-done((f32[16,2,8,128]{3,2,1,0:T(8,128)S(1)}, f32[16,2,8,128]{3,2,1,0:T(8,128)S(1)}, u32[]{:S(2)}, u32[]{:S(2)}) %collective-permute-start.4) | collective-permute-done | bytes 131104 | tf_op jit(solution)/shard_map/ppermute | solution.py:421
  20.6 0.6 %prepare.1 = (f32[16,2,32,128]{3,2,1,0:T(8,128)S(1)}, f32[16,32,128]{2,1,0:T(8,128)S(1)}, f32[16,32,128]{2,1,0:T(8,128)S(1)}, f32[3,160,128]{2,1,0:T(8,128)S(1)}) custom-call(f32[32,128]{1,0:T(8,128)S(1)} %slice_bitcast_fusion.10.spectral_ref, f32[8,128]{1,0:T(8,128)S(1)} %get-tuple-element.14.table_ref, f32[72,128]{1,0:T(8,128)S(1)} %collective-permute-done.1.side_ref, ...), custom_call_target="tpu_custom_call" | custom-call | tf_op jit(solution)/shard_map/prepare/pallas_call | solution.py:513
  21.2 0.3 quad.1
  21.5 2.5 %collective-permute-start.9 = (f32[96,128]{1,0:T(8,128)S(1)}, f32[96,128]{1,0:T(8,128)S(1)}, u32[]{:S(2)}, u32[]{:S(2)}) collective-permute-start(f32[96,128]{1,0:T(8,128)S(1)} %quad.1), channel_id=1, source_target_pairs={{0,12},{1,13},{2,6},{3,7},{4,8},{5,9},{6,10},{7,11},{8,4},{9,5},{1... | collective-permute-start | bytes 147464 | tf_op jit(solution)/shard_map/ppermute | solution.py:421
  23.9 0.3 %levels.1.neighbour_map = f32[160,128]{1,0:T(8,128)S(1)} custom-call(f32[32,128]{1,0:T(8,128)S(1)} %slice_bitcast_fusion.10.spectral_ref, f32[136,128]{1,0:T(8,128)S(1)} %collective-permute-done.7.message_ref.neighbour_ref), custom_call_target="tpu_custom_call" | custom-call | tf_op jit(solution)/shard_map/levels/pallas_call | solution.py:530
  24.3 0.0 collective-permute-done.8
  24.3 2.9 %collective-permute-done.9.other_ref = f32[96,128]{1,0:T(8,128)S(1)} collective-permute-done((f32[96,128]{1,0:T(8,128)S(1)}, f32[96,128]{1,0:T(8,128)S(1)}, u32[]{:S(2)}, u32[]{:S(2)}) %collective-permute-start.9) | collective-permute-done | bytes 49184 | tf_op jit(solution)/shard_map/ppermute | solution.py:421
  27.3 1.0 %solve.1 = f32[16,2,4,8,128]{4,3,2,1,0:T(8,128)} custom-call(f32[16,2,32,128]{3,2,1,0:T(8,128)S(1)} %get-tuple-element.17.part_ref, f32[16,32,128]{2,1,0:T(8,128)S(1)} %get-tuple-element.18.low_ref, f32[16,32,128]{2,1,0:T(8,128)S(1)} %get-tuple-element.19.high_ref, f32[3,160,128]{2,1,0:T(8,128)S(1)} %get-tuple-element.20.maps_ref, ...), custom_call_target="tpu_custom_call" | custom-call | tf_op jit(solution)/shard_map/solve/pallas_call | solution.py:544
  (14 shorter events, 0.1 us)
Async XLA Ops:
  1.2 1.5 %collective-permute-start = (f32[2,2,32,128]{3,2,1,0:T(8,128)S(1)}, f32[2,2,32,128]{3,2,1,0:T(8,128)S(1)}, u32[]{:S(2)}, u32[]{:S(2)}) collective-permute-start(f32[2,2,32,128]{3,2,1,0:T(8,128)S(1)} %get-tuple-element.15), channel_id=1, source_target_pairs={{0,8},{1,9},{2,10},{3,11},{4,12},{5,13},{6,14},{7,15},{8,0},{9,1},... | collective-permute-start | bytes 196616 | tf_op jit(solution)/shard_map/ppermute | solution.py:421
  2.7 4.3 %collective-permute-start.5 = (f32[64,128]{1,0:T(8,128)S(1)}, f32[64,128]{1,0:T(8,128)S(1)}, u32[]{:S(2)}, u32[]{:S(2)}) collective-permute-start(f32[64,128]{1,0:T(8,128)S(1)} %pad_maximum_fusion.2), channel_id=1, source_target_pairs={{0,24},{1,25},{2,18},{3,19},{4,28},{5,29},{6,30},{7,31},{8,16},{9,... | collective-permute-start | bytes 98312 | tf_op jit(solution)/shard_map/ppermute | solution.py:421
  5.4 4.2 %collective-permute-start.6 = (f32[64,128]{1,0:T(8,128)S(1)}, f32[64,128]{1,0:T(8,128)S(1)}, u32[]{:S(2)}, u32[]{:S(2)}) collective-permute-start(f32[64,128]{1,0:T(8,128)S(1)} %pad_maximum_fusion.2), channel_id=1, source_target_pairs={{0,25},{1,24},{2,19},{3,18},{4,29},{5,28},{6,31},{7,30},{8,17},{9,... | collective-permute-start | bytes 98312 | tf_op jit(solution)/shard_map/ppermute | solution.py:421
  6.8 3.4 %collective-permute-start.1 = (f32[72,128]{1,0:T(8,128)S(1)}, f32[72,128]{1,0:T(8,128)S(1)}, u32[]{:S(2)}, u32[]{:S(2)}) collective-permute-start(f32[72,128]{1,0:T(8,128)S(1)} %pad_maximum_fusion.1), channel_id=1, source_target_pairs={{0,9},{1,8},{2,3},{3,2},{4,13},{5,12},{6,15},{7,14},{8,1},{9,0},{1... | collective-permute-start | bytes 110600 | tf_op jit(solution)/shard_map/ppermute | solution.py:421
  10.5 4.2 %collective-permute-start.7 = (f32[136,128]{1,0:T(8,128)S(1)}, f32[136,128]{1,0:T(8,128)S(1)}, u32[]{:S(2)}, u32[]{:S(2)}) collective-permute-start(f32[136,128]{1,0:T(8,128)S(1)} %merge.1.own_ref), channel_id=1, source_target_pairs={{0,10},{1,11},{2,8},{3,9},{4,6},{5,7},{6,4},{7,5},{8,2},{9,3},{10,... | collective-permute-start | bytes 208904 | tf_op jit(solution)/shard_map/ppermute | solution.py:421
  11.3 4.5 %collective-permute-start.2 = (f32[16,2,8,128]{3,2,1,0:T(8,128)S(1)}, f32[16,2,8,128]{3,2,1,0:T(8,128)S(1)}, u32[]{:S(2)}, u32[]{:S(2)}) collective-permute-start(f32[16,2,8,128]{3,2,1,0:T(8,128)S(1)} %get-tuple-element.23), channel_id=1, source_target_pairs={{0,8},{1,9},{2,10},{3,11},{4,12},{5,13},{6,14},{7,15},{8,0},{9,1},... | collective-permute-start | bytes 393224 | tf_op jit(solution)/shard_map/ppermute | solution.py:421
  13.2 6.4 %collective-permute-start.3 = (f32[16,2,8,128]{3,2,1,0:T(8,128)S(1)}, f32[16,2,8,128]{3,2,1,0:T(8,128)S(1)}, u32[]{:S(2)}, u32[]{:S(2)}) collective-permute-start(f32[16,2,8,128]{3,2,1,0:T(8,128)S(1)} %get-tuple-element.22), channel_id=1, source_target_pairs={{0,16},{1,17},{2,18},{3,19},{4,20},{5,21},{6,22},{7,23},{8,24},{9,... | collective-permute-start | bytes 393224 | tf_op jit(solution)/shard_map/ppermute | solution.py:421
  14.7 5.9 %collective-permute-start.4 = (f32[16,2,8,128]{3,2,1,0:T(8,128)S(1)}, f32[16,2,8,128]{3,2,1,0:T(8,128)S(1)}, u32[]{:S(2)}, u32[]{:S(2)}) collective-permute-start(f32[16,2,8,128]{3,2,1,0:T(8,128)S(1)} %get-tuple-element.21), channel_id=1, source_target_pairs={{0,24},{1,25},{2,26},{3,27},{4,28},{5,29},{6,30},{7,31},{8,16},{9,... | collective-permute-start | bytes 393224 | tf_op jit(solution)/shard_map/ppermute | solution.py:421
  14.7 9.5 %collective-permute-start.8 = (f32[264,128]{1,0:T(8,128)S(1)}, f32[264,128]{1,0:T(8,128)S(1)}, u32[]{:S(2)}, u32[]{:S(2)}) collective-permute-start(f32[264,128]{1,0:T(8,128)S(1)} %pad_maximum_fusion), channel_id=1, source_target_pairs={{0,8},{1,9},{2,10},{3,11},{4,12},{5,13},{6,14},{7,15},{8,0},{9,1},... | collective-permute-start | bytes 405512 | tf_op jit(solution)/shard_map/ppermute | solution.py:421
  21.5 5.8 %collective-permute-start.9 = (f32[96,128]{1,0:T(8,128)S(1)}, f32[96,128]{1,0:T(8,128)S(1)}, u32[]{:S(2)}, u32[]{:S(2)}) collective-permute-start(f32[96,128]{1,0:T(8,128)S(1)} %quad.1), channel_id=1, source_target_pairs={{0,12},{1,13},{2,6},{3,7},{4,8},{5,9},{6,10},{7,11},{8,4},{9,5},{1... | collective-permute-start | bytes 147464 | tf_op jit(solution)/shard_map/ppermute | solution.py:421
